TPU v7x, 32 devices: a whole 2x2x4 slice. The times are simulated.
32 devices in a mesh: blk: 8 (over z, x), grp: 4 (over y, core).
Axes of the slice: x: 2, y: 2, z: 4, core: 2. Of those that a mesh axis runs over, the one named last changes fastest.
Arguments:
- snapshots: bfloat16 [65536, 1024], P(('grp', 'blk')), may hold values from -1200 to 1200
- start: float32 [1024, 256], replicated, may hold values from -6 to 6
- pivot_dev: int32 [32], replicated, may hold values from 0 to 31, as said below
- pivot_row: int32 [32], replicated, may hold values from 0 to 2047, as said below
Outputs:
- modes: bfloat16 [65536, 256], P(('grp', 'blk'))
- scores: float32 [65536], P(('grp', 'blk'))
- panel_basis: float32 [256, 32], replicated
Inputs may be any that keep to these rules, and one draw needn't show every extreme that they name: Together with pivot_row, names 32 distinct global rows pivot_dev * 2048 + pivot_row; the first and the last global row are always among them. `pivot_row`: see pivot_dev.
All inputs are finite; a program needn't handle non-finite values.
Results may differ from a plain program's by a relative error of at most 0.0051.
Values sent between devices are 32-bit elements; how exact they have to be, the bound alone decides.
No kernel may reach another device: no remote copies, remote signals or barrier semaphores. Data moves between devices by JAX's collectives and lax.ppermute only.
A program may use at most 64 MiB of HBM per device.

v0:
```python
import jax
import jax.numpy as jnp
from jax import lax
from jax.sharding import PartitionSpec as P

ITERS = 4


def right_solve(factor, matrix):
    return lax.linalg.triangular_solve(
        factor, matrix, left_side=False, lower=True, transpose_a=True
    )


def local(snapshots, start, pivot_dev, pivot_row):
    local_gram = lax.dot_general(
        snapshots, snapshots, (((0,), (0,)), ((), ())), preferred_element_type=jnp.float32
    )
    rows_total = snapshots.shape[0] * lax.axis_size(("grp", "blk"))
    gram_full = lax.psum(local_gram, ("grp", "blk"))

    def apply_gram(iterate):
        return jnp.dot(gram_full, iterate, precision=lax.Precision.HIGHEST)

    iterate = start
    for repeat in range(ITERS):
        image = apply_gram(iterate)
        square = jnp.dot(image.T, image, precision=lax.Precision.HIGHEST)
        iterate = right_solve(jnp.linalg.cholesky(square), image)
    image = apply_gram(iterate)
    small_gram = jnp.dot(iterate.T, image, precision=lax.Precision.HIGHEST) / rows_total
    coef = right_solve(jnp.linalg.cholesky(small_gram), iterate).astype(jnp.bfloat16)
    basis = jnp.dot(snapshots, coef, preferred_element_type=jnp.float32)
    myself = lax.axis_index(("grp", "blk"))
    picked = basis[pivot_row]
    owned = (pivot_dev == myself)[:, None]
    panel = lax.psum(jnp.where(owned, picked, 0.0), ("grp", "blk"))
    panel_gram = jnp.dot(panel, panel.T, precision=lax.Precision.HIGHEST)
    panel_basis = right_solve(jnp.linalg.cholesky(panel_gram), panel.T)
    coeffs = jnp.dot(basis, panel_basis, precision=lax.Precision.HIGHEST)
    remaining = basis - jnp.dot(coeffs, panel_basis.T, precision=lax.Precision.HIGHEST)
    scores = jnp.sum(remaining * remaining, axis=1) / basis.shape[1]
    return (basis.astype(jnp.bfloat16), scores, panel_basis)


def solution(mesh):
    placed = (P(("grp", "blk"), None), P(), P(), P())
    return jax.shard_map(
        local,
        mesh=mesh,
        in_specs=placed,
        out_specs=(P(("grp", "blk"), None), P(("grp", "blk")), P()),
        check_vma=False,
    )
```

profile of v0, /device:TPU:0, one launch (start us, length us, event | category | flops | bytes accessed | tf_op | source)
XLA Modules:
  0.0 595.9 jit_solution(3653849216793346499)
XLA Ops:
  7.2 10.1 %fusion.87 = f32[1024,1024]{1,0:T(8,128)} fusion(bf16[2048,1024]{1,0:T(8,128)(2,1)} %param.7), kind=kOutput, calls=%fused_computation.175 | convolution fusion | flops 4294967296 | bytes 8388608 | tf_op jit(solution)/shard_map/dot_general | solution.py:16
  18.0 144.5 %all-reduce.3.cloned.1.call-done = f32[1024,1024]{1,0:T(8,128)} async-done(((f32[1024,1024]{1,0:T(8,128)}), f32[1024,1024]{1,0:T(8,128)}) %all-reduce.3.cloned.1.call-update) | async-done | bytes 4194320 | tf_op jit(solution)/shard_map/psum | solution.py:20
  162.5 5.5 fusion.88
  167.9 1.8 fusion.89
  170.0 11.7 %cholesky.291 = f32[128,128]{1,0:T(8,128)S(1)} custom-call(f32[128,128]{1,0:T(8,128)S(1)} %cholesky.457), custom_call_target="Cholesky" | custom-call | tf_op jit(solution)/shard_map/jit(cholesky)/cholesky | solution.py:29
  181.7 9.8 %custom-call.26 = f32[1,128,128]{1,2,0:T(8,128)S(1)} custom-call(f32[1,128,128]{2,1,0:T(8,128)S(1)} %get-tuple-element.114), custom_call_target="InvertDiagBlocksLowerTriangular" | custom-call | tf_op jit(solution)/shard_map/jit(cholesky)/cholesky | solution.py:29
  192.1 11.7 %cholesky.308 = f32[128,128]{1,0:T(8,128)S(1)} custom-call(f32[128,128]{1,0:T(8,128)S(1)} %convolution_subtract_fusion.10), custom_call_target="Cholesky" | custom-call | tf_op jit(solution)/shard_map/jit(cholesky)/cholesky | solution.py:29
  218.7 3.9 while.10
  222.6 19.7 %custom-call.27 = f32[2,128,128]{1,2,0:T(8,128)S(1)} custom-call(f32[2,128,128]{2,1,0:T(8,128)S(1)} %get-tuple-element.37), custom_call_target="InvertDiagBlocksLowerTriangular" | custom-call | tf_op jit(solution)/shard_map/triangular_solve/custom-call.4 | solution.py:10
  244.6 5.3 fusion.2
  249.9 1.8 fusion.90
  252.0 11.7 %cholesky.325 = f32[128,128]{1,0:T(8,128)S(1)} custom-call(f32[128,128]{1,0:T(8,128)S(1)} %cholesky.460), custom_call_target="Cholesky" | custom-call | tf_op jit(solution)/shard_map/jit(cholesky)/cholesky | solution.py:29
  263.7 9.8 %custom-call.28 = f32[1,128,128]{1,2,0:T(8,128)S(1)} custom-call(f32[1,128,128]{2,1,0:T(8,128)S(1)} %get-tuple-element.110), custom_call_target="InvertDiagBlocksLowerTriangular" | custom-call | tf_op jit(solution)/shard_map/jit(cholesky)/cholesky | solution.py:29
  274.0 11.7 %cholesky.342 = f32[128,128]{1,0:T(8,128)S(1)} custom-call(f32[128,128]{1,0:T(8,128)S(1)} %convolution_subtract_fusion.9), custom_call_target="Cholesky" | custom-call | tf_op jit(solution)/shard_map/jit(cholesky)/cholesky | solution.py:29
  288.8 4.0 while.11
  289.4 1.4 bitcast_dynamic-update-slice_fusion.11
  291.4 1.4 bitcast_dynamic-update-slice_fusion.11
  292.8 19.7 %custom-call.29 = f32[2,128,128]{1,2,0:T(8,128)S(1)} custom-call(f32[2,128,128]{2,1,0:T(8,128)S(1)} %get-tuple-element.38), custom_call_target="InvertDiagBlocksLowerTriangular" | custom-call | tf_op jit(solution)/shard_map/triangular_solve/custom-call.4 | solution.py:10
  314.8 5.5 fusion.6
  320.3 1.8 fusion.91
  322.3 11.7 %cholesky.359 = f32[128,128]{1,0:T(8,128)S(1)} custom-call(f32[128,128]{1,0:T(8,128)S(1)} %cholesky.463), custom_call_target="Cholesky" | custom-call | tf_op jit(solution)/shard_map/jit(cholesky)/cholesky | solution.py:29
  334.1 9.8 %custom-call.30 = f32[1,128,128]{1,2,0:T(8,128)S(1)} custom-call(f32[1,128,128]{2,1,0:T(8,128)S(1)} %get-tuple-element.106), custom_call_target="InvertDiagBlocksLowerTriangular" | custom-call | tf_op jit(solution)/shard_map/jit(cholesky)/cholesky | solution.py:29
  344.4 11.7 %cholesky.376 = f32[128,128]{1,0:T(8,128)S(1)} custom-call(f32[128,128]{1,0:T(8,128)S(1)} %convolution_subtract_fusion.8), custom_call_target="Cholesky" | custom-call | tf_op jit(solution)/shard_map/jit(cholesky)/cholesky | solution.py:29
  359.0 4.0 while.12
  363.0 19.7 %custom-call.31 = f32[2,128,128]{1,2,0:T(8,128)S(1)} custom-call(f32[2,128,128]{2,1,0:T(8,128)S(1)} %get-tuple-element.39), custom_call_target="InvertDiagBlocksLowerTriangular" | custom-call | tf_op jit(solution)/shard_map/triangular_solve/custom-call.4 | solution.py:10
  385.0 5.8 fusion.10
  390.8 1.8 fusion.92
  392.8 11.7 %cholesky.393 = f32[128,128]{1,0:T(8,128)S(1)} custom-call(f32[128,128]{1,0:T(8,128)S(1)} %cholesky.466), custom_call_target="Cholesky" | custom-call | tf_op jit(solution)/shard_map/jit(cholesky)/cholesky | solution.py:29
  404.6 9.8 %custom-call.32 = f32[1,128,128]{1,2,0:T(8,128)S(1)} custom-call(f32[1,128,128]{2,1,0:T(8,128)S(1)} %get-tuple-element.102), custom_call_target="InvertDiagBlocksLowerTriangular" | custom-call | tf_op jit(solution)/shard_map/jit(cholesky)/cholesky | solution.py:29
  414.9 11.7 %cholesky.410 = f32[128,128]{1,0:T(8,128)S(1)} custom-call(f32[128,128]{1,0:T(8,128)S(1)} %convolution_subtract_fusion.7), custom_call_target="Cholesky" | custom-call | tf_op jit(solution)/shard_map/jit(cholesky)/cholesky | solution.py:29
  429.4 4.0 while.13
  433.5 19.7 %custom-call.33 = f32[2,128,128]{1,2,0:T(8,128)S(1)} custom-call(f32[2,128,128]{2,1,0:T(8,128)S(1)} %get-tuple-element.40), custom_call_target="InvertDiagBlocksLowerTriangular" | custom-call | tf_op jit(solution)/shard_map/triangular_solve/custom-call.4 | solution.py:10
  455.4 5.3 fusion.14
  460.7 1.9 convolution_multiply_fusion
  462.8 11.7 %cholesky.427 = f32[128,128]{1,0:T(8,128)S(1)} custom-call(f32[128,128]{1,0:T(8,128)S(1)} %cholesky.469), custom_call_target="Cholesky" | custom-call | tf_op jit(solution)/shard_map/jit(cholesky)/cholesky | solution.py:32
  474.6 9.8 %custom-call.34 = f32[1,128,128]{1,2,0:T(8,128)S(1)} custom-call(f32[1,128,128]{2,1,0:T(8,128)S(1)} %get-tuple-element.98), custom_call_target="InvertDiagBlocksLowerTriangular" | custom-call | tf_op jit(solution)/shard_map/jit(cholesky)/cholesky | solution.py:32
  484.8 11.7 %cholesky.444 = f32[128,128]{1,0:T(8,128)S(1)} custom-call(f32[128,128]{1,0:T(8,128)S(1)} %convolution_subtract_fusion.6), custom_call_target="Cholesky" | custom-call | tf_op jit(solution)/shard_map/jit(cholesky)/cholesky | solution.py:32
  499.4 4.0 while.14
  503.4 19.7 %custom-call.35 = f32[2,128,128]{1,2,0:T(8,128)S(1)} custom-call(f32[2,128,128]{2,1,0:T(8,128)S(1)} %get-tuple-element.41), custom_call_target="InvertDiagBlocksLowerTriangular" | custom-call | tf_op jit(solution)/shard_map/triangular_solve/custom-call.4 | solution.py:10
  525.0 4.5 bitcast_convert_fusion
  529.5 1.9 copy.13
  531.3 2.2 gather_fusion
  533.6 39.5 %psum.15 = f32[32,256]{1,0:T(8,128)S(1)} all-reduce(f32[32,256]{1,0:T(8,128)S(1)} %broadcast_select_fusion), channel_id=1, replica_groups=mesh['blk'=8,'grp'=4] {'grp','blk'}, use_global_device_ids=true, to_apply=%region_5.8 | all-reduce | flops 8192 | bytes 65536 | tf_op jit(solution)/shard_map/psum | solution.py:37
  573.4 2.9 cholesky.96
  577.6 2.4 custom-call.17
  580.3 3.5 fusion.94
  583.9 1.9 fusion.1
  586.4 2.3 copy.15
  (126 shorter events, 41.7 us)
Async XLA Ops:
  7.2 155.3 %copy-start = (f32[1024,256]{1,0:T(8,128)S(1)}, f32[1024,256]{1,0:T(8,128)}, u32[]{:S(2)}) copy-start(f32[1024,256]{1,0:T(8,128)} %param.8) | copy-start | bytes 3145732
  7.2 155.3 %all-reduce.3.cloned.1.call-start = ((), (), s32[]{:S(2)}) async-start(), calls=%async_computation | async-start | bytes 8388608 | tf_op jit(solution)/shard_map/psum | solution.py:20
  17.3 0.7 copy-start.2
  17.3 0.7 copy-start.3
  580.3 8.3 %copy-start.1 = (f32[256,32]{0,1:T(8,128)}, f32[256,32]{0,1:T(8,128)S(1)}, u32[]{:S(2)}) copy-start(f32[256,32]{0,1:T(8,128)S(1)} %fusion.72) | copy-start | bytes 98308
Sparse Core Ops, SparseCore 0:
  17.4 144.9 all-reduce.2
where the time goes:
time: 601 us; the launch traced here: 596 us
  other arithmetic  279 us (46%)
  waiting for transfers between devices  144 us (24%)
  matrix products  70.2 us (12%)
  blocking collectives  39.5 us (7%)
  between operations  34.4 us (6%)
  local copies, waits for them, and re-layouts  27.6 us (5%)
    psum x1, waiting for transfers between devices, local(): gram_full = lax.psum(local_gram, ('grp', 'blk'))  144 us
    another operation x27, other arithmetic, local(): iterate = right_solve(jnp.linalg.cholesky(square), image)  138 us
    another operation x13, other arithmetic, right_solve(): lax.linalg.triangular_solve(factor, matrix, left_side=False, lower=True,...  103 us
    psum x1, blocking collectives, local(): panel = lax.psum(jnp.where(owned, picked, 0.0), ('grp', 'blk'))  39.5 us
    another operation x7, other arithmetic, local(): jnp.linalg.cholesky(small_gram)  34.6 us
    dot_general x5, matrix products, apply_gram(): return jnp.dot(gram_full, iterate, precision=lax.Precision.HIGHEST)  27.4 us
    another operation x36, local copies, waits for them, and re-layouts, right_solve(): lax.linalg.triangular_solve(factor, matrix, left_side=False, lower=True,...  19.8 us
  transfers between devices with their start and end apart: 1, of which 1 were waited for; matrix products, arithmetic and copies ran while one was open for 0% of the time, Pallas kernels for 0%

commit v1 on v0

v1 whole, which is shorter than its diff:
```python
import functools
import jax
import jax.numpy as jnp
from jax import lax
from jax.experimental import pallas as pl
from jax.experimental.pallas import tpu as pltpu
from jax.sharding import PartitionSpec as P

ITERS = 4
TILE = 128
BAND = 2
BLOCK = 64
F32, BF16 = jnp.float32, jnp.bfloat16
HIGHEST = lax.Precision.HIGHEST
VMEM = pl.BlockSpec(memory_space=pltpu.VMEM)
SMEM = pl.BlockSpec(memory_space=pltpu.SMEM)


def dot(a, b, ca, cb, precision=None):
    return lax.dot_general(
        a, b, (((ca,), (cb,)), ((), ())), precision=precision, preferred_element_type=F32
    )


def split(value):
    high = value.astype(BF16)
    return high, (value - high.astype(F32)).astype(BF16)


def iota(shape, dim):
    return lax.broadcasted_iota(jnp.int32, shape, dim)


def bands_of(tiles):
    count = tiles // BAND
    outer = [0, count - 1] if count > 1 else [0]
    return outer, [band for band in range(count) if band not in outer]


def places(tiles):
    result = []
    for bands in bands_of(tiles):
        row, entries = 0, []
        for band in bands:
            for i in range(band * BAND, band * BAND + BAND):
                for j in range(i, tiles):
                    entries.append((i, j, row))
                    row += TILE
        result.append((entries, row))
    return result


def exchange_plan(mesh_shape, rows):
    grp = [("grp", 1 << b) for b in range(mesh_shape["grp"].bit_length() - 1)]
    blk = [("blk", 1 << b) for b in range(mesh_shape["blk"].bit_length() - 1)]
    rest = blk[1:] + grp[2:]
    orders = (grp[:1] + blk[:1] + grp[1:2] + rest, grp[:1] + grp[1:2] + blk[:1] + rest)
    halvings = 0
    while halvings < len(orders[0]) and all(r % (8 << (halvings + 1)) == 0 for r in rows):
        halvings += 1
    return orders, halvings


def key_of(order, halvings):
    key = jnp.int32(0)
    for axis, mask in order[:halvings]:
        key = key * 2 + jnp.where((lax.axis_index(axis) & mask) != 0, 1, 0)
    return key


def send(value, axis, mask):
    size = lax.axis_size(axis)
    return lax.ppermute(value, axis, [(i, i ^ mask) for i in range(size)])


def exchange(values, steps):
    if all(step == steps[0] for step in steps):
        got = send(jnp.concatenate(values, axis=0), *steps[0])
        first = values[0].shape[0]
        return [got[:first], got[first:]]
    return [send(value, *step) for value, step in zip(values, steps)]


def reduce_parts(kept, sent, orders, halvings):
    for number, steps in enumerate(zip(*orders)):
        if number < halvings:
            if number:
                halves = [v.shape[0] // 2 for v in kept]
                sent = [v[h:] for v, h in zip(kept, halves)]
                kept = [v[:h] for v, h in zip(kept, halves)]
            if number == 0:
                got = [send(v, *s) for v, s in zip(sent, steps)]
            else:
                got = exchange(sent, steps)
        else:
            got = exchange(kept, steps)
        kept = [v + g for v, g in zip(kept, got)]
    for number in range(halvings - 1, 0, -1):
        got = exchange(kept, [order[number] for order in orders])
        kept = [jnp.concatenate([v, g], axis=0) for v, g in zip(kept, got)]
    got = [send(v, *order[0]) for v, order in zip(kept, orders)]
    return kept, got


def gram_kernel(chunks, dev_ref, row_ref, keys_ref, s_ref, *refs):
    outs, work = refs[:4], refs[4:]
    tiles = s_ref.shape[1] // TILE
    spots = places(tiles)
    parts = bands_of(tiles)
    pivots = dev_ref.shape[0]
    for part in range(2):
        where = {(i, j): row for i, j, row in spots[part][0]}
        for band in parts[part]:
            first = band * BAND * TILE
            strip = dot(s_ref[:, first:first + BAND * TILE], s_ref[:, first:], 0, 0)
            for a in range(BAND):
                i = band * BAND + a
                for j in range(i, tiles):
                    col = (j - band * BAND) * TILE
                    row = where[(i, j)]
                    work[part][row:row + TILE, :] = strip[
                        a * TILE:(a + 1) * TILE, col:col + TILE]
    base = spots[0][1]
    sub = iota((16, s_ref.shape[1]), 0)

    def pick(p, carry):
        at = row_ref[p]
        group = pl.multiple_of((at // 16) * 16, 16)
        rows = s_ref[pl.ds(group, 16), :].astype(F32)
        wanted = jnp.where(dev_ref[p] == keys_ref[2], at - group, -1)
        row = jnp.sum(jnp.where(sub == wanted, rows, 0.0), axis=0, keepdims=True)
        for t in range(tiles):
            work[0][pl.ds(base + t * pivots + p, 1), :] = row[:, t * TILE:(t + 1) * TILE]
        return carry

    lax.fori_loop(0, pivots, pick, 0)
    for part in range(2):
        size = work[part].shape[0] // chunks
        for q in range(chunks):
            out = outs[2 * part + q // (chunks // 2)]
            to = (q % (chunks // 2)) * size
            at = pl.multiple_of((keys_ref[part] ^ q) * size, 8)
            out[to:to + size, :] = work[part][pl.ds(at, size), :]


def local_gram(snapshots, pivot_dev, pivot_row, keys, rows, chunks):
    shapes = [jax.ShapeDtypeStruct((r // 2, TILE), F32) for r in rows for _ in range(2)]
    return pl.pallas_call(
        functools.partial(gram_kernel, chunks),
        out_shape=shapes,
        in_specs=[SMEM, SMEM, SMEM, VMEM],
        out_specs=[VMEM] * 4,
        scratch_shapes=[pltpu.VMEM((r, TILE), F32) for r in rows],
        name="local_gram",
    )(pivot_dev, pivot_row, keys, snapshots)


def eliminate(rows, at):
    shape = rows[0].shape
    sub = iota(shape, 0)

    def lane(value, j):
        return jnp.broadcast_to(value[:, j:j + 1], shape)

    def subl(value, i):
        return jnp.broadcast_to(value[i:i + 1, :], shape)

    rows = list(rows)
    count = len(rows)
    for g in range(count):
        here = rows[g]
        cols = [lane(here, at + 8 * g + j) for j in range(8)]
        p = [[subl(cols[j], i) if j >= i else None for j in range(8)] for i in range(8)]
        e = [subl(here, i) for i in range(8)]
        below = range(g + 1, count)
        c = {h: [lane(rows[h], at + 8 * g + j) for j in range(8)] for h in below}
        scale = [None] * 8
        for j in range(0, 8, 2):
            k = j + 1
            a, b, d = p[j][j], p[j][k], p[k][k]
            idet = 1.0 / (a * d - b * b)
            ia = 1.0 / a
            scale[j], scale[k] = ia, a * idet
            e[k] = e[k] - (b * ia) * e[j]
            for i in range(j + 2, 8):
                y0 = d * p[j][i] - b * p[k][i]
                y1 = a * p[k][i] - b * p[j][i]
                for m in range(i, 8):
                    p[i][m] = p[i][m] - (y0 * p[j][m] + y1 * p[k][m]) * idet
                e[i] = e[i] - (p[j][i] * ia) * e[j] - (y1 * idet) * e[k]
            for h in below:
                x0 = (d * c[h][j] - b * c[h][k]) * idet
                x1 = (a * c[h][k] - b * c[h][j]) * idet
                for m in range(j + 2, 8):
                    c[h][m] = c[h][m] - x0 * p[j][m] - x1 * p[k][m]
                rows[h] = rows[h] - (c[h][j] * ia) * e[j] - x1 * e[k]
        out, factor = e[0], scale[0]
        for i in range(1, 8):
            out = jnp.where(sub == i, e[i], out)
            factor = jnp.where(sub == i, scale[i], factor)
        rows[g] = out * jnp.sqrt(factor)
    return rows


def lower(value):
    return jnp.where(iota(value.shape, 1) <= iota(value.shape, 0), value, 0.0)


def invert_factor(m_ref):
    n, b = m_ref.shape[0], BLOCK
    lanes, subs = iota((b, n), 1), iota((b, n), 0)
    near, down = iota((b, TILE), 1), iota((b, TILE), 0)
    for k in range(n // b):
        first = k * b
        tile = first // TILE * TILE
        at = first - tile
        other = b - at
        inside = (near >= at) & (near < at + b)
        eye = jnp.where(near - other == down, 1.0, 0.0)
        block = jnp.where(inside, m_ref[first:first + b, tile:tile + TILE], eye)
        done = eliminate([block[8 * g:8 * g + 8] for g in range(b // 8)], at)
        inverse = lower(jnp.concatenate(done, axis=0)[:, other:other + b])
        mine = (lanes >= first) & (lanes < first + b)
        unit = jnp.where(lanes - first == subs, 1.0, 0.0)
        row = dot(inverse, jnp.where(mine, unit, m_ref[first:first + b, :]), 1, 0, HIGHEST)
        m_ref[first:first + b, :] = row
        if first + b < n:
            update = dot(row, row, 0, 0, HIGHEST)
            for q in range(first + b, n, b):
                m_ref[q:q + b, :] = (
                    jnp.where(mine, 0.0, m_ref[q:q + b, :]) - update[q:q + b, :]
                )


def inverse_factor(matrix, m_ref):
    n = matrix.shape[0]
    diagonal = jnp.where(iota((n, n), 0) == iota((n, n), 1), matrix, 0.0)
    down = lax.rsqrt(jnp.sum(diagonal, axis=1, keepdims=True))
    across = lax.rsqrt(jnp.sum(diagonal, axis=0, keepdims=True))
    m_ref[...] = matrix * down * across
    invert_factor(m_ref)
    return lower(m_ref[...]) * across


def solve_kernel(
    chunks, rows_total, keys_ref, start_ref, s_ref, a0_ref, a1_ref, b0_ref, b1_ref,
    modes_ref, scores_ref, basis_ref, pa_ref, pb_ref, gh_ref, gl_ref, xh_ref, xl_ref,
    y_ref, m_ref,
):
    packed = (pa_ref, pb_ref)
    halves = ((a0_ref, a1_ref), (b0_ref, b1_ref))
    snap, rank = start_ref.shape
    tiles = snap // TILE
    for part in range(2):
        size = packed[part].shape[0] // chunks
        for q in range(chunks):
            half = halves[part][q // (chunks // 2)]
            at = (q % (chunks // 2)) * size
            to = pl.multiple_of((keys_ref[part] ^ q) * size, 8)
            packed[part][pl.ds(to, size), :] = half[at:at + size, :]
    spots = places(tiles)
    for part in range(2):
        for i, j, row in spots[part][0]:
            value = packed[part][row:row + TILE, :]
            high, low = split(value)
            gh_ref[i * TILE:(i + 1) * TILE, j * TILE:(j + 1) * TILE] = high
            gl_ref[i * TILE:(i + 1) * TILE, j * TILE:(j + 1) * TILE] = low
            if i != j:
                high, low = split(jnp.transpose(value))
                gh_ref[j * TILE:(j + 1) * TILE, i * TILE:(i + 1) * TILE] = high
                gl_ref[j * TILE:(j + 1) * TILE, i * TILE:(i + 1) * TILE] = low
    xh_ref[...], xl_ref[...] = split(start_ref[...])
    step = 256

    def apply_gram():
        xh, xl = xh_ref[...], xl_ref[...]

        def strip(r, carry):
            at = pl.ds(pl.multiple_of(r * step, step), step)
            gh = gh_ref[at, :]
            y_ref[at, :] = dot(gh, xh, 1, 0) + (dot(gh, xl, 1, 0) + dot(gl_ref[at, :], xh, 1, 0))
            return carry

        lax.fori_loop(0, snap // step, strip, 0)

    def iteration(_, carry):
        apply_gram()
        yh, yl = split(y_ref[...])
        factor = inverse_factor(dot(yh, yh, 0, 0), m_ref).astype(BF16)
        xh_ref[...], xl_ref[...] = split(dot(yh, factor, 1, 1) + dot(yl, factor, 1, 1))
        return carry

    lax.fori_loop(0, ITERS, iteration, 0)
    apply_gram()
    yh, yl = split(y_ref[...])
    xh, xl = xh_ref[...], xl_ref[...]
    small = dot(xh, yh, 0, 0) + (dot(xh, yl, 0, 0) + dot(xl, yh, 0, 0))
    small = (small + jnp.transpose(small)) * (0.5 / rows_total)
    fh, fl = split(inverse_factor(small, m_ref))
    coef = (dot(xh, fh, 1, 1) + (dot(xh, fl, 1, 1) + dot(xl, fh, 1, 1))).astype(BF16)
    xh_ref[...] = coef

    base = spots[0][1]
    pivots = basis_ref.shape[1]
    picked = jnp.concatenate(
        [pa_ref[base + t * pivots:base + (t + 1) * pivots, :] for t in range(tiles)], axis=1
    )
    panel = dot(picked.astype(BF16), coef, 1, 0)
    gram = dot(panel, panel, 1, 1, HIGHEST)
    same = iota((pivots, pivots), 0) == iota((pivots, pivots), 1)
    diagonal = jnp.where(same, gram, 0.0)
    down = lax.rsqrt(jnp.sum(diagonal, axis=1, keepdims=True))
    across = lax.rsqrt(jnp.sum(diagonal, axis=0, keepdims=True))
    wide = jnp.concatenate(
        [gram * down * across, jnp.where(same, 1.0, 0.0)]
        + [jnp.zeros((pivots, TILE - 2 * pivots), F32)], axis=1
    )
    done = eliminate([wide[8 * g:8 * g + 8] for g in range(pivots // 8)], 0)
    factor = lower(jnp.concatenate(done, axis=0)[:, pivots:2 * pivots]) * across
    turned = dot(factor, panel, 1, 0, HIGHEST)
    basis_ref[...] = dot(panel, factor, 0, 1, HIGHEST)
    th, tl = split(turned)
    ones = jnp.ones((8, rank), BF16)
    chunk = 512

    def project(r, carry):
        at = pl.ds(pl.multiple_of(r * chunk, chunk), chunk)
        basis = dot(s_ref[at, :], xh_ref[...], 1, 0)
        bh, bl = split(basis)
        modes_ref[at, :] = bh
        coeffs = dot(bh, th, 1, 1) + (dot(bh, tl, 1, 1) + dot(bl, th, 1, 1))
        ch, cl = split(coeffs)
        left = basis - (dot(ch, th, 1, 0) + (dot(ch, tl, 1, 0) + dot(cl, th, 1, 0)))
        qh, ql = split(left * left)
        total = (dot(ones, qh, 1, 1) + dot(ones, ql, 1, 1)) * (1.0 / rank)
        scores_ref[:, at] = total[0:1, :]
        return carry

    lax.fori_loop(0, s_ref.shape[0] // chunk, project, 0)


def solve(snapshots, start, keys, pieces, pivots, rows, chunks, rows_total):
    snap, rank = start.shape
    here = snapshots.shape[0]
    return pl.pallas_call(
        functools.partial(solve_kernel, chunks, rows_total),
        out_shape=[
            jax.ShapeDtypeStruct((here, rank), BF16),
            jax.ShapeDtypeStruct((1, here), F32),
            jax.ShapeDtypeStruct((rank, pivots), F32),
        ],
        in_specs=[SMEM] + [VMEM] * 6,
        out_specs=[VMEM] * 3,
        scratch_shapes=[pltpu.VMEM((r, TILE), F32) for r in rows] + [
            pltpu.VMEM((snap, snap), BF16),
            pltpu.VMEM((snap, snap), BF16),
            pltpu.VMEM((snap, rank), BF16),
            pltpu.VMEM((snap, rank), BF16),
            pltpu.VMEM((snap, rank), F32),
            pltpu.VMEM((rank, rank), F32),
        ],
        name="solve",
    )(keys, start, snapshots, *pieces)


def local(mesh_shape, snapshots, start, pivot_dev, pivot_row):
    here, snap = snapshots.shape
    pivots = pivot_dev.shape[0]
    spots = places(snap // TILE)
    rows = [spots[0][1] + pivots * (snap // TILE), spots[1][1]]
    orders, halvings = exchange_plan(mesh_shape, rows)
    chunks = 1 << halvings
    myself = lax.axis_index(("grp", "blk"))
    keys = jnp.stack([key_of(orders[0], halvings), key_of(orders[1], halvings), myself])
    a0, a1, b0, b1 = local_gram(snapshots, pivot_dev, pivot_row, keys, rows, chunks)
    own, other = reduce_parts([a0, b0], [a1, b1], orders, halvings)
    pieces = (own[0], other[0], own[1], other[1])
    rows_total = here * mesh_shape["grp"] * mesh_shape["blk"]
    modes, scores, basis = solve(
        snapshots, start, keys, pieces, pivots, rows, chunks, rows_total
    )
    return modes, scores.reshape(here), basis


def solution(mesh):
    placed = (P(("grp", "blk"), None), P(), P(), P())
    return jax.shard_map(
        functools.partial(local, dict(mesh.shape)),
        mesh=mesh,
        in_specs=placed,
        out_specs=(P(("grp", "blk"), None), P(("grp", "blk")), P()),
        check_vma=False,
    )
```

time: 601 us -> 155 us (0.26)
  other arithmetic: 279 us -> 3.14 us
  waiting for transfers between devices: 144 us -> 43.1 us
  Pallas kernels: 0 us -> 86 us
  matrix products: 70.2 us -> 0 us
  blocking collectives: 39.5 us -> 0 us
  between operations: 34.4 us -> 0.91 us
  local copies, waits for them, and re-layouts: 27.6 us -> 3.47 us
  starting transfers between devices: 0.04 us -> 17.8 us
    another operation x50 -> x1, other arithmetic: 278 us -> 0.59 us  [local(): jnp.stack([key_of(orders[0], halvings), key_of(orders[1], halvings), myse...]
    psum x1 -> x0, waiting for transfers between devices: 144 us -> none  [local(): gram_full = lax.psum(local_gram, ('grp', 'blk'))]
    pallas_call x0 -> x2, Pallas kernels: none -> 86 us  [the longest x1 78.2 us: solve(): pl.pallas_call(functools.partial(solve_kernel, chunks, rows_total), out_s...]
    dot_general x15 -> x0, matrix products: 56.7 us -> none  [the longest x5 27.4 us: apply_gram(): return jnp.dot(gram_full, iterate, precision=lax.Precision.HIGHEST)]
    ppermute x0 -> x16, waiting for transfers between devices: none -> 43.1 us  [send(): return lax.ppermute(value, axis, [(i, i ^ mask) for i in range(size)])]
    psum x1 -> x0, blocking collectives: 39.5 us -> none  [local(): panel = lax.psum(jnp.where(owned, picked, 0.0), ('grp', 'blk'))]
    another operation x46 -> x0, local copies, waits for them, and re-layouts: 19.9 us -> none  [the longest x36 19.8 us: right_solve(): lax.linalg.triangular_solve(factor, matrix, left_side=False, lower=True,...]
    ppermute x0 -> x16, starting transfers between devices: none -> 17.8 us  [send(): return lax.ppermute(value, axis, [(i, i ^ mask) for i in range(size)])]
  transfers between devices with their start and end apart: 1 -> 16, of which waited for: 1 -> 13; matrix products, arithmetic and copies ran while one was open for 0% -> 2% of each run, Pallas kernels for 0% -> 0%
where the time goes in v1:
time: 155 us; the launch traced here: 154 us
  Pallas kernels  86 us (55%)
  waiting for transfers between devices  43.1 us (28%)
  starting transfers between devices  17.8 us (11%)
  local copies, waits for them, and re-layouts  3.47 us (2%)
  other arithmetic  3.14 us (2%)
    pallas_call x1, Pallas kernels, solve(): pl.pallas_call(functools.partial(solve_kernel, chunks, rows_total), out_s...  78.2 us
    ppermute x16, waiting for transfers between devices, send(): return lax.ppermute(value, axis, [(i, i ^ mask) for i in range(size)])  43.1 us
    ppermute x16, starting transfers between devices, send(): return lax.ppermute(value, axis, [(i, i ^ mask) for i in range(size)])  17.8 us
    pallas_call x1, Pallas kernels, local_gram(): pl.pallas_call(functools.partial(gram_kernel, chunks), out_shape=shapes,...  7.82 us
    unnamed x12, local copies, waits for them, and re-layouts  3.31 us
  transfers between devices with their start and end apart: 16, of which 13 were waited for; matrix products, arithmetic and copies ran while one was open for 2% of the time, Pallas kernels for 0%

profile of v1, /device:TPU:0, one launch (start us, length us, event | category | flops | bytes accessed | tf_op | source)
XLA Modules:
  0.0 154.4 jit_solution(2449661413931615491)
XLA Ops:
  0.7 0.6 pad_add_fusion.keys_ref
  1.3 7.8 %local_gram.1 = (f32[1280,128]{1,0:T(8,128)}, f32[1280,128]{1,0:T(8,128)}, f32[1152,128]{1,0:T(8,128)}, f32[1152,128]{1,0:T(8,128)}) custom-call(s32[32]{0:T(128)} %dev_ref.1, s32[32]{0:T(128)} %row_ref.1, s32[3]{0:T(128)} %pad_add_fusion.keys_ref, bf16[2048,1024]{1,0:T(8,128)(2,1)} %s_ref.3), custom_call_target="tpu_custom_call" | custom-call | tf_op jit(solution)/shard_map/local_gram/pallas_call | solution.py:148
  9.1 0.5 collective-permute-start.3
  9.6 0.0 collective-permute-start
  9.6 1.8 %collective-permute-done.3 = f32[1152,128]{1,0:T(8,128)S(1)} collective-permute-done((f32[1152,128]{1,0:T(8,128)}, f32[1152,128]{1,0:T(8,128)S(1)}, u32[]{:S(2)}, u32[]{:S(2)}) %collective-permute-start.3) | collective-permute-done | bytes 589856 | tf_op jit(solution)/shard_map/ppermute | solution.py:73
  11.4 1.1 add.69
  12.6 2.9 %collective-permute-start.4 = (f32[576,128]{1,0:T(8,128)S(1)}, f32[576,128]{1,0:T(8,128)S(1)}, u32[]{:S(2)}, u32[]{:S(2)}) collective-permute-start(f32[576,128]{1,0:T(8,128)S(1)} %slice.103), channel_id=1, source_target_pairs={{0,2},{1,3},{2,0},{3,1},{4,6},{5,7},{6,4},{7,5},{8,10},{9,11},{10,... | collective-permute-start | bytes 884744 | tf_op jit(solution)/shard_map/ppermute | solution.py:73
  15.5 0.0 collective-permute-done
  15.5 1.2 add.66
  16.7 1.6 %collective-permute-start.1 = (f32[640,128]{1,0:T(8,128)S(1)}, f32[640,128]{1,0:T(8,128)S(1)}, u32[]{:S(2)}, u32[]{:S(2)}) collective-permute-start(f32[640,128]{1,0:T(8,128)S(1)} %slice.97), channel_id=1, source_target_pairs={{0,4},{4,0},{8,12},{12,8},{16,20},{20,16},{24,28},{28,24},{1,5},{5... | collective-permute-start | bytes 983048 | tf_op jit(solution)/shard_map/ppermute | solution.py:73
  18.3 4.6 %collective-permute-done.4 = f32[576,128]{1,0:T(8,128)S(1)} collective-permute-done((f32[576,128]{1,0:T(8,128)S(1)}, f32[576,128]{1,0:T(8,128)S(1)}, u32[]{:S(2)}, u32[]{:S(2)}) %collective-permute-start.4) | collective-permute-done | bytes 294944 | tf_op jit(solution)/shard_map/ppermute | solution.py:73
  22.9 1.8 %collective-permute-start.5 = (f32[288,128]{1,0:T(8,128)S(1)}, f32[288,128]{1,0:T(8,128)S(1)}, u32[]{:S(2)}, u32[]{:S(2)}) collective-permute-start(f32[288,128]{1,0:T(8,128)S(1)} %slice.105), channel_id=1, source_target_pairs={{0,4},{4,0},{8,12},{12,8},{16,20},{20,16},{24,28},{28,24},{1,5},{5... | collective-permute-start | bytes 442376 | tf_op jit(solution)/shard_map/ppermute | solution.py:73
  24.6 2.7 %collective-permute-done.1 = f32[640,128]{1,0:T(8,128)S(1)} collective-permute-done((f32[640,128]{1,0:T(8,128)S(1)}, f32[640,128]{1,0:T(8,128)S(1)}, u32[]{:S(2)}, u32[]{:S(2)}) %collective-permute-start.1) | collective-permute-done | bytes 327712 | tf_op jit(solution)/shard_map/ppermute | solution.py:73
  27.4 0.1 collective-permute-start.2
  27.5 1.9 %collective-permute-done.5 = f32[288,128]{1,0:T(8,128)S(1)} collective-permute-done((f32[288,128]{1,0:T(8,128)S(1)}, f32[288,128]{1,0:T(8,128)S(1)}, u32[]{:S(2)}, u32[]{:S(2)}) %collective-permute-start.5) | collective-permute-done | bytes 147488 | tf_op jit(solution)/shard_map/ppermute | solution.py:73
  29.4 3.4 %collective-permute-done.2 = f32[320,128]{1,0:T(8,128)S(1)} collective-permute-done((f32[320,128]{1,0:T(8,128)S(1)}, f32[320,128]{1,0:T(8,128)S(1)}, u32[]{:S(2)}, u32[]{:S(2)}) %collective-permute-start.2) | collective-permute-done | bytes 163872 | tf_op jit(solution)/shard_map/ppermute | solution.py:73
  32.9 1.6 %collective-permute-start.6 = (f32[304,128]{1,0:T(8,128)S(1)}, f32[304,128]{1,0:T(8,128)S(1)}, u32[]{:S(2)}, u32[]{:S(2)}) collective-permute-start(f32[304,128]{1,0:T(8,128)S(1)} %pad_maximum_fusion.3), channel_id=1, source_target_pairs={{0,8},{4,12},{8,0},{12,4},{16,24},{20,28},{24,16},{28,20},{1,9},{5... | collective-permute-start | bytes 466952 | tf_op jit(solution)/shard_map/ppermute | solution.py:73
  34.5 4.5 %collective-permute-done.6 = f32[304,128]{1,0:T(8,128)S(1)} collective-permute-done((f32[304,128]{1,0:T(8,128)S(1)}, f32[304,128]{1,0:T(8,128)S(1)}, u32[]{:S(2)}, u32[]{:S(2)}) %collective-permute-start.6) | collective-permute-done | bytes 155680 | tf_op jit(solution)/shard_map/ppermute | solution.py:73
  39.1 2.5 %collective-permute-start.7 = (f32[152,128]{1,0:T(8,128)S(1)}, f32[152,128]{1,0:T(8,128)S(1)}, u32[]{:S(2)}, u32[]{:S(2)}) collective-permute-start(f32[152,128]{1,0:T(8,128)S(1)} %pad_maximum_fusion.6), channel_id=1, source_target_pairs={{0,16},{4,20},{8,24},{12,28},{16,0},{20,4},{24,8},{28,12},{1,17},{... | collective-permute-start | bytes 233480 | tf_op jit(solution)/shard_map/ppermute | solution.py:73
  41.6 4.3 %collective-permute-done.7 = f32[152,128]{1,0:T(8,128)S(1)} collective-permute-done((f32[152,128]{1,0:T(8,128)S(1)}, f32[152,128]{1,0:T(8,128)S(1)}, u32[]{:S(2)}, u32[]{:S(2)}) %collective-permute-start.7) | collective-permute-done | bytes 77856 | tf_op jit(solution)/shard_map/ppermute | solution.py:73
  45.9 1.1 collective-permute-start.8
  47.0 4.7 %collective-permute-done.8 = f32[152,128]{1,0:T(8,128)S(1)} collective-permute-done((f32[152,128]{1,0:T(8,128)S(1)}, f32[152,128]{1,0:T(8,128)S(1)}, u32[]{:S(2)}, u32[]{:S(2)}) %collective-permute-start.8) | collective-permute-done | bytes 77856 | tf_op jit(solution)/shard_map/ppermute | solution.py:73
  51.7 1.5 collective-permute-start.9
  53.2 3.8 %collective-permute-done.9 = f32[304,128]{1,0:T(8,128)S(1)} collective-permute-done((f32[304,128]{1,0:T(8,128)S(1)}, f32[304,128]{1,0:T(8,128)S(1)}, u32[]{:S(2)}, u32[]{:S(2)}) %collective-permute-start.9) | collective-permute-done | bytes 155680 | tf_op jit(solution)/shard_map/ppermute | solution.py:73
  57.1 0.5 collective-permute-start.10
  57.6 1.6 %collective-permute-start.13 = (f32[288,128]{1,0:T(8,128)S(1)}, f32[288,128]{1,0:T(8,128)S(1)}, u32[]{:S(2)}, u32[]{:S(2)}) collective-permute-start(f32[288,128]{1,0:T(8,128)S(1)} %pad_maximum_fusion.5), channel_id=1, source_target_pairs={{0,4},{4,0},{8,12},{12,8},{16,20},{20,16},{24,28},{28,24},{1,5},{5... | collective-permute-start | bytes 442376 | tf_op jit(solution)/shard_map/ppermute | solution.py:73
  59.2 3.3 %collective-permute-done.10 = f32[320,128]{1,0:T(8,128)S(1)} collective-permute-done((f32[320,128]{1,0:T(8,128)S(1)}, f32[320,128]{1,0:T(8,128)S(1)}, u32[]{:S(2)}, u32[]{:S(2)}) %collective-permute-start.10) | collective-permute-done | bytes 163872 | tf_op jit(solution)/shard_map/ppermute | solution.py:73
  62.5 1.5 %collective-permute-start.11 = (f32[640,128]{1,0:T(8,128)S(1)}, f32[640,128]{1,0:T(8,128)S(1)}, u32[]{:S(2)}, u32[]{:S(2)}) collective-permute-start(f32[640,128]{1,0:T(8,128)S(1)} %pad_maximum_fusion), channel_id=1, source_target_pairs={{0,4},{4,0},{8,12},{12,8},{16,20},{20,16},{24,28},{28,24},{1,5},{5... | collective-permute-start | bytes 983048 | tf_op jit(solution)/shard_map/ppermute | solution.py:73
  64.0 0.0 collective-permute-done.13
  64.0 0.5 collective-permute-start.14
  64.6 5.0 %collective-permute-done.11 = f32[640,128]{1,0:T(8,128)S(1)} collective-permute-done((f32[640,128]{1,0:T(8,128)S(1)}, f32[640,128]{1,0:T(8,128)S(1)}, u32[]{:S(2)}, u32[]{:S(2)}) %collective-permute-start.11) | collective-permute-done | bytes 327712 | tf_op jit(solution)/shard_map/ppermute | solution.py:73
  69.6 0.0 copy-start
  69.6 0.1 collective-permute-start.12
  69.7 1.1 collective-permute-done.14
  70.9 0.0 copy-start.1
  70.9 0.1 collective-permute-start.15
  70.9 2.0 %collective-permute-done.15.b1_ref = f32[1152,128]{1,0:T(8,128)S(1)} collective-permute-done((f32[1152,128]{1,0:T(8,128)S(1)}, f32[1152,128]{1,0:T(8,128)S(1)}, u32[]{:S(2)}, u32[]{:S(2)}) %collective-permute-start.15) | collective-permute-done | bytes 589856 | tf_op jit(solution)/shard_map/ppermute | solution.py:73
  72.9 0.0 copy-start.3
  72.9 0.0 collective-permute-done.12.a1_ref
  72.9 0.0 copy-done
  72.9 0.0 copy-done.1
  73.0 0.8 copy-done.3
  73.8 0.0 copy-start.2
  73.8 0.9 copy-done.2
  74.6 78.2 %solve.1 = (bf16[2048,256]{1,0:T(8,128)(2,1)}, f32[1,2048]{1,0:T(1,128)}, f32[256,32]{1,0:T(8,128)}) custom-call(s32[3]{0:T(128)} %pad_add_fusion.keys_ref, f32[1024,256]{1,0:T(8,128)} %start_ref.1, bf16[2048,1024]{1,0:T(8,128)(2,1)} %s_ref.3, f32[1280,128]{1,0:T(8,128)} %copy-done, f32[1280,128]{1,0:T(8,128)} %copy-done.2, f32[1152,128]{1,0:T(8,128)} %copy-done.1, ...), custom_call_target="tpu_custom_call" | custom-call | tf_op jit(solution)/shard_map/solve/pallas_call | solution.py:345
  152.8 1.6 %copy.7 = f32[256,32]{0,1:T(8,128)} copy(f32[256,32]{1,0:T(8,128)} %get-tuple-element.19) | data formatting | bytes 65536
  (32 shorter events, 0.5 us)
Async XLA Ops:
  9.1 2.3 %collective-permute-start.3 = (f32[1152,128]{1,0:T(8,128)}, f32[1152,128]{1,0:T(8,128)S(1)}, u32[]{:S(2)}, u32[]{:S(2)}) collective-permute-start(f32[1152,128]{1,0:T(8,128)} %get-tuple-element.13), channel_id=1, source_target_pairs={{0,1},{1,0},{2,3},{3,2},{4,5},{5,4},{6,7},{7,6},{8,9},{9,8},{10,11... | collective-permute-start | bytes 1769480 | tf_op jit(solution)/shard_map/ppermute | solution.py:73
  9.6 5.9 %collective-permute-start = (f32[1280,128]{1,0:T(8,128)}, f32[1280,128]{1,0:T(8,128)S(1)}, u32[]{:S(2)}, u32[]{:S(2)}) collective-permute-start(f32[1280,128]{1,0:T(8,128)} %get-tuple-element.11), channel_id=1, source_target_pairs={{0,1},{1,0},{2,3},{3,2},{4,5},{5,4},{6,7},{7,6},{8,9},{9,8},{10,11... | collective-permute-start | bytes 1966088 | tf_op jit(solution)/shard_map/ppermute | solution.py:73
  12.6 10.2 %collective-permute-start.4 = (f32[576,128]{1,0:T(8,128)S(1)}, f32[576,128]{1,0:T(8,128)S(1)}, u32[]{:S(2)}, u32[]{:S(2)}) collective-permute-start(f32[576,128]{1,0:T(8,128)S(1)} %slice.103), channel_id=1, source_target_pairs={{0,2},{1,3},{2,0},{3,1},{4,6},{5,7},{6,4},{7,5},{8,10},{9,11},{10,... | collective-permute-start | bytes 884744 | tf_op jit(solution)/shard_map/ppermute | solution.py:73
  16.7 10.7 %collective-permute-start.1 = (f32[640,128]{1,0:T(8,128)S(1)}, f32[640,128]{1,0:T(8,128)S(1)}, u32[]{:S(2)}, u32[]{:S(2)}) collective-permute-start(f32[640,128]{1,0:T(8,128)S(1)} %slice.97), channel_id=1, source_target_pairs={{0,4},{4,0},{8,12},{12,8},{16,20},{20,16},{24,28},{28,24},{1,5},{5... | collective-permute-start | bytes 983048 | tf_op jit(solution)/shard_map/ppermute | solution.py:73
  22.9 6.5 %collective-permute-start.5 = (f32[288,128]{1,0:T(8,128)S(1)}, f32[288,128]{1,0:T(8,128)S(1)}, u32[]{:S(2)}, u32[]{:S(2)}) collective-permute-start(f32[288,128]{1,0:T(8,128)S(1)} %slice.105), channel_id=1, source_target_pairs={{0,4},{4,0},{8,12},{12,8},{16,20},{20,16},{24,28},{28,24},{1,5},{5... | collective-permute-start | bytes 442376 | tf_op jit(solution)/shard_map/ppermute | solution.py:73
  27.4 5.4 %collective-permute-start.2 = (f32[320,128]{1,0:T(8,128)S(1)}, f32[320,128]{1,0:T(8,128)S(1)}, u32[]{:S(2)}, u32[]{:S(2)}) collective-permute-start(f32[320,128]{1,0:T(8,128)S(1)} %slice.99), channel_id=1, source_target_pairs={{0,2},{1,3},{2,0},{3,1},{4,6},{5,7},{6,4},{7,5},{8,10},{9,11},{10,... | collective-permute-start | bytes 491528 | tf_op jit(solution)/shard_map/ppermute | solution.py:73
  32.9 6.1 %collective-permute-start.6 = (f32[304,128]{1,0:T(8,128)S(1)}, f32[304,128]{1,0:T(8,128)S(1)}, u32[]{:S(2)}, u32[]{:S(2)}) collective-permute-start(f32[304,128]{1,0:T(8,128)S(1)} %pad_maximum_fusion.3), channel_id=1, source_target_pairs={{0,8},{4,12},{8,0},{12,4},{16,24},{20,28},{24,16},{28,20},{1,9},{5... | collective-permute-start | bytes 466952 | tf_op jit(solution)/shard_map/ppermute | solution.py:73
  39.1 6.8 %collective-permute-start.7 = (f32[152,128]{1,0:T(8,128)S(1)}, f32[152,128]{1,0:T(8,128)S(1)}, u32[]{:S(2)}, u32[]{:S(2)}) collective-permute-start(f32[152,128]{1,0:T(8,128)S(1)} %pad_maximum_fusion.6), channel_id=1, source_target_pairs={{0,16},{4,20},{8,24},{12,28},{16,0},{20,4},{24,8},{28,12},{1,17},{... | collective-permute-start | bytes 233480 | tf_op jit(solution)/shard_map/ppermute | solution.py:73
  45.9 5.8 %collective-permute-start.8 = (f32[152,128]{1,0:T(8,128)S(1)}, f32[152,128]{1,0:T(8,128)S(1)}, u32[]{:S(2)}, u32[]{:S(2)}) collective-permute-start(f32[152,128]{1,0:T(8,128)S(1)} %pad_maximum_fusion.7), channel_id=1, source_target_pairs={{0,16},{4,20},{8,24},{12,28},{16,0},{20,4},{24,8},{28,12},{1,17},{... | collective-permute-start | bytes 233480 | tf_op jit(solution)/shard_map/ppermute | solution.py:73
  51.7 5.3 %collective-permute-start.9 = (f32[304,128]{1,0:T(8,128)S(1)}, f32[304,128]{1,0:T(8,128)S(1)}, u32[]{:S(2)}, u32[]{:S(2)}) collective-permute-start(f32[304,128]{1,0:T(8,128)S(1)} %pad_maximum_fusion.4), channel_id=1, source_target_pairs={{0,8},{4,12},{8,0},{12,4},{16,24},{20,28},{24,16},{28,20},{1,9},{5... | collective-permute-start | bytes 466952 | tf_op jit(solution)/shard_map/ppermute | solution.py:73
  57.1 5.4 %collective-permute-start.10 = (f32[320,128]{1,0:T(8,128)S(1)}, f32[320,128]{1,0:T(8,128)S(1)}, u32[]{:S(2)}, u32[]{:S(2)}) collective-permute-start(f32[320,128]{1,0:T(8,128)S(1)} %pad_maximum_fusion.2), channel_id=1, source_target_pairs={{0,2},{1,3},{2,0},{3,1},{4,6},{5,7},{6,4},{7,5},{8,10},{9,11},{10,... | collective-permute-start | bytes 491528 | tf_op jit(solution)/shard_map/ppermute | solution.py:73
  57.6 6.4 %collective-permute-start.13 = (f32[288,128]{1,0:T(8,128)S(1)}, f32[288,128]{1,0:T(8,128)S(1)}, u32[]{:S(2)}, u32[]{:S(2)}) collective-permute-start(f32[288,128]{1,0:T(8,128)S(1)} %pad_maximum_fusion.5), channel_id=1, source_target_pairs={{0,4},{4,0},{8,12},{12,8},{16,20},{20,16},{24,28},{28,24},{1,5},{5... | collective-permute-start | bytes 442376 | tf_op jit(solution)/shard_map/ppermute | solution.py:73
  62.5 7.1 %collective-permute-start.11 = (f32[640,128]{1,0:T(8,128)S(1)}, f32[640,128]{1,0:T(8,128)S(1)}, u32[]{:S(2)}, u32[]{:S(2)}) collective-permute-start(f32[640,128]{1,0:T(8,128)S(1)} %pad_maximum_fusion), channel_id=1, source_target_pairs={{0,4},{4,0},{8,12},{12,8},{16,20},{20,16},{24,28},{28,24},{1,5},{5... | collective-permute-start | bytes 983048 | tf_op jit(solution)/shard_map/ppermute | solution.py:73
  64.0 6.8 %collective-permute-start.14 = (f32[576,128]{1,0:T(8,128)S(1)}, f32[576,128]{1,0:T(8,128)S(1)}, u32[]{:S(2)}, u32[]{:S(2)}) collective-permute-start(f32[576,128]{1,0:T(8,128)S(1)} %pad_maximum_fusion.1), channel_id=1, source_target_pairs={{0,2},{1,3},{2,0},{3,1},{4,6},{5,7},{6,4},{7,5},{8,10},{9,11},{10,... | collective-permute-start | bytes 884744 | tf_op jit(solution)/shard_map/ppermute | solution.py:73
  69.6 3.3 %copy-start = (f32[1280,128]{1,0:T(8,128)}, f32[1280,128]{1,0:T(8,128)S(1)}, u32[]{:S(2)}) copy-start(f32[1280,128]{1,0:T(8,128)S(1)} %constant_dynamic-update-slice_fusion.a0_ref) | copy-start | bytes 1966084
  69.6 3.3 %collective-permute-start.12 = (f32[1280,128]{1,0:T(8,128)S(1)}, f32[1280,128]{1,0:T(8,128)S(1)}, u32[]{:S(2)}, u32[]{:S(2)}) collective-permute-start(f32[1280,128]{1,0:T(8,128)S(1)} %constant_dynamic-update-slice_fusion.a0_ref), channel_id=1, source_target_pairs={{0,1},{1,0},{2,3},{3,2},{4,5},{5,4},{6,7},{7,6},{8,9},{9,8},{10,11... | collective-permute-start | bytes 1966088 | tf_op jit(solution)/shard_map/ppermute | solution.py:73
  70.9 2.1 %copy-start.1 = (f32[1152,128]{1,0:T(8,128)}, f32[1152,128]{1,0:T(8,128)S(1)}, u32[]{:S(2)}) copy-start(f32[1152,128]{1,0:T(8,128)S(1)} %constant_dynamic-update-slice_fusion.5.b0_ref) | copy-start | bytes 1769476
  70.9 2.1 %collective-permute-start.15 = (f32[1152,128]{1,0:T(8,128)S(1)}, f32[1152,128]{1,0:T(8,128)S(1)}, u32[]{:S(2)}, u32[]{:S(2)}) collective-permute-start(f32[1152,128]{1,0:T(8,128)S(1)} %constant_dynamic-update-slice_fusion.5.b0_ref), channel_id=1, source_target_pairs={{0,1},{1,0},{2,3},{3,2},{4,5},{5,4},{6,7},{7,6},{8,9},{9,8},{10,11... | collective-permute-start | bytes 1769480 | tf_op jit(solution)/shard_map/ppermute | solution.py:73
  72.9 0.8 copy-start.3
  73.8 0.9 copy-start.2

commit v2 on v1

v2 whole, which is shorter than its diff:
```python
import functools
import jax
import jax.numpy as jnp
from jax import lax
from jax.experimental import pallas as pl
from jax.experimental.pallas import tpu as pltpu
from jax.sharding import PartitionSpec as P


ITERS = 4
TILE = 128
BAND = 2
BLOCK = 64
LOADS = 4
F32, BF16 = jnp.float32, jnp.bfloat16
HIGHEST = lax.Precision.HIGHEST
VMEM = pl.BlockSpec(memory_space=pltpu.VMEM)
SMEM = pl.BlockSpec(memory_space=pltpu.SMEM)
ANY = pl.BlockSpec(memory_space=pl.ANY)


def dot(a, b, ca, cb, precision=None):
    return lax.dot_general(
        a, b, (((ca,), (cb,)), ((), ())), precision=precision, preferred_element_type=F32
    )


def split(value):
    high = value.astype(BF16)
    return high, (value - high.astype(F32)).astype(BF16)


def iota(shape, dim):
    return lax.broadcasted_iota(jnp.int32, shape, dim)


def bands_of(tiles):
    count = tiles // BAND
    outer = [0, count - 1] if count > 1 else [0]
    return outer, [band for band in range(count) if band not in outer]


def places(tiles):
    result = []
    for bands in bands_of(tiles):
        row, entries = 0, []
        for band in bands:
            for i in range(band * BAND, band * BAND + BAND):
                for j in range(i, tiles):
                    entries.append((i, j, row))
                    row += TILE
        result.append((entries, row))
    return result


def exchange_plan(mesh_shape, rows):
    grp = [("grp", 1 << b) for b in range(mesh_shape["grp"].bit_length() - 1)]
    blk = [("blk", 1 << b) for b in range(mesh_shape["blk"].bit_length() - 1)]
    rest = blk[1:] + grp[2:]
    orders = (grp[:1] + blk[:1] + grp[1:2] + rest, grp[:1] + grp[1:2] + blk[:1] + rest)
    halvings = 0
    while halvings < len(orders[0]) and all(r % (8 << (halvings + 1)) == 0 for r in rows):
        halvings += 1
    return orders, halvings


def key_of(order, halvings):
    key = jnp.int32(0)
    for axis, mask in order[:halvings]:
        key = key * 2 + jnp.where((lax.axis_index(axis) & mask) != 0, 1, 0)
    return key


def send(value, axis, mask):
    size = lax.axis_size(axis)
    return lax.ppermute(value, axis, [(i, i ^ mask) for i in range(size)])


def exchange(values, steps):
    if all(step == steps[0] for step in steps):
        got = send(jnp.concatenate(values, axis=0), *steps[0])
        first = values[0].shape[0]
        return [got[:first], got[first:]]
    result = []
    for value, step in zip(values, steps):
        result.append(send(value, *step))
    return result


def halve(values, got):
    halves = [v.shape[0] // 2 for v in values]
    sent = [v[h:] + g[h:] for v, g, h in zip(values, got, halves)]
    kept = [v[:h] + g[:h] for v, g, h in zip(values, got, halves)]
    return sent, kept


def reduce_parts(kept, sent, got, orders, halvings):
    steps = list(zip(*orders))
    for number in range(1, len(steps)):
        if number < halvings:
            sent, kept = halve(kept, got)
            got = exchange(sent, steps[number])
        else:
            kept = [v + g for v, g in zip(kept, got)]
            got = exchange(kept, steps[number])
    kept = [v + g for v, g in zip(kept, got)]
    for number in range(halvings - 1, 0, -1):
        got = exchange(kept, steps[number])
        kept = [jnp.concatenate([v, g], axis=0) for v, g in zip(kept, got)]
    return kept, [send(v, *order[0]) for v, order in zip(kept, orders)]


def gram_kernel(part, chunks, dev_ref, row_ref, keys_ref, s_hbm, low_ref, high_ref, s_ref, work, sems):
    tiles = s_ref.shape[1] // TILE
    spots = places(tiles)
    here = s_ref.shape[0]
    piece = here // LOADS
    copies = []
    for q in range(LOADS):
        at = pl.ds(q * piece, piece)
        copies.append(pltpu.make_async_copy(s_hbm.at[at, :], s_ref.at[at, :], sems.at[q]))
        copies[-1].start()
    where = {(i, j): row for i, j, row in spots[part][0]}
    for q in range(LOADS):
        copies[q].wait()
        rows = slice(q * piece, (q + 1) * piece)
        for band in bands_of(tiles)[part]:
            first = band * BAND * TILE
            strip = dot(s_ref[rows, first:first + BAND * TILE], s_ref[rows, first:], 0, 0)
            for a in range(BAND):
                i = band * BAND + a
                for j in range(i, tiles):
                    col = (j - band * BAND) * TILE
                    row = where[(i, j)]
                    term = strip[a * TILE:(a + 1) * TILE, col:col + TILE]
                    if q:
                        term = work[row:row + TILE, :] + term
                    work[row:row + TILE, :] = term
    if part == 0:
        base = spots[0][1]
        pivots = dev_ref.shape[0]
        sub = iota((16, s_ref.shape[1]), 0)

        def pick(p, carry):
            at = row_ref[p]
            group = pl.multiple_of((at // 16) * 16, 16)
            rows = s_ref[pl.ds(group, 16), :].astype(F32)
            wanted = jnp.where(dev_ref[p] == keys_ref[2], at - group, -1)
            row = jnp.sum(jnp.where(sub == wanted, rows, 0.0), axis=0, keepdims=True)
            for t in range(tiles):
                work[pl.ds(base + t * pivots + p, 1), :] = row[:, t * TILE:(t + 1) * TILE]
            return carry

        lax.fori_loop(0, pivots, pick, 0)
    size = work.shape[0] // chunks
    for q in range(chunks):
        out = low_ref if q < chunks // 2 else high_ref
        to = (q % (chunks // 2)) * size
        at = pl.multiple_of((keys_ref[part] ^ q) * size, 8)
        out[to:to + size, :] = work[pl.ds(at, size), :]


def local_gram(part, snapshots, pivot_dev, pivot_row, keys, rows, chunks):
    here, snap = snapshots.shape
    return pl.pallas_call(
        functools.partial(gram_kernel, part, chunks),
        out_shape=[jax.ShapeDtypeStruct((rows // 2, TILE), F32)] * 2,
        in_specs=[SMEM, SMEM, SMEM, ANY],
        out_specs=[VMEM] * 2,
        scratch_shapes=[
            pltpu.VMEM((here, snap), BF16),
            pltpu.VMEM((rows, TILE), F32),
            pltpu.SemaphoreType.DMA((LOADS,)),
        ],
    )(pivot_dev, pivot_row, keys, snapshots)


def eliminate(rows, at):
    shape = rows[0].shape
    sub = iota(shape, 0)
    one = jnp.where(sub >= 0, 1.0, 0.0)

    def lane(value, j):
        return jnp.broadcast_to(value[:, j:j + 1], shape)

    def subl(value, i):
        return jnp.broadcast_to(value[i:i + 1, :], shape)

    rows = list(rows)
    count = len(rows)
    for g in range(count):
        here = rows[g]
        cols = [lane(here, at + 8 * g + j) * one for j in range(8)]
        p = [[subl(cols[j], i) if j >= i else None for j in range(8)] for i in range(8)]
        e = [subl(here, i) for i in range(8)]
        c = {h: [lane(rows[h], at + 8 * g + j) for j in range(8)] for h in range(g + 1, count)}
        scale = []
        u = [[None] * 8 for _ in range(8)]
        for j in range(8):
            inverse = 1.0 / p[j][j]
            scale.append(inverse)
            for i in range(j + 1, 8):
                u[j][i] = p[j][i] * inverse
            for i in range(j + 1, 8):
                for m in range(i, 8):
                    if i == j + 1 and m <= j + 2:
                        p[i][m] = p[i][m] - (p[j][i] * p[j][m]) * inverse
                    else:
                        p[i][m] = p[i][m] - u[j][i] * p[j][m]
                e[i] = e[i] - u[j][i] * e[j]
            if g + 1 < count:
                near = c[g + 1]
                x = near[j] * inverse
                rows[g + 1] = rows[g + 1] - x * e[j]
                for m in range(j + 1, 8):
                    near[m] = near[m] - x * p[j][m]
        if g + 2 < count:
            t = [e[i] * scale[i] for i in range(8)]
            for i in range(7, 0, -1):
                for m in range(i):
                    t[m] = t[m] - u[m][i] * t[i]
            for h in range(g + 2, count):
                terms = [c[h][j] * t[j] for j in range(8)]
                while len(terms) > 1:
                    terms = [terms[q] + terms[q + 1] for q in range(0, len(terms), 2)]
                rows[h] = rows[h] - terms[0]
        out, factor = e[0], scale[0]
        for i in range(1, 8):
            out = jnp.where(sub == i, e[i], out)
            factor = jnp.where(sub == i, scale[i], factor)
        rows[g] = out * jnp.sqrt(factor)
    return rows


def lower(value):
    return jnp.where(iota(value.shape, 1) <= iota(value.shape, 0), value, 0.0)


def invert_factor(m_ref, beside=None):
    n, b = m_ref.shape[0], BLOCK
    lanes, subs = iota((b, n), 1), iota((b, n), 0)
    near, down = iota((b, TILE), 1), iota((b, TILE), 0)
    block = m_ref[:b, :TILE]
    for k in range(n // b):
        first = k * b
        at = first % TILE
        other = b - at
        inside = (near >= at) & (near < at + b)
        eye = jnp.where(near - other == down, 1.0, 0.0)
        block = jnp.where(inside, block, eye)
        if beside is not None:
            beside(k)
        done = eliminate([block[8 * g:8 * g + 8] for g in range(b // 8)], at)
        inverse = lower(jnp.concatenate(done, axis=0)[:, other:other + b])
        mine = (lanes >= first) & (lanes < first + b)
        unit = jnp.where(lanes - first == subs, 1.0, 0.0)
        wh, wl = split(inverse)
        rh, rl = split(jnp.where(mine, unit, m_ref[first:first + b, :]))
        row = dot(wh, rh, 1, 0) + (dot(wh, rl, 1, 0) + dot(wl, rh, 1, 0))
        m_ref[first:first + b, :] = row
        q = first + b
        if q < n:
            uh, ul = split(row)
            left = jnp.concatenate([uh, uh, ul], axis=0)
            right = jnp.concatenate([uh, ul, uh], axis=0)
            tile = q // TILE * TILE
            block = m_ref[q:q + b, tile:tile + TILE] - dot(
                left[:, q:q + b], right[:, tile:tile + TILE], 0, 0)
            update = dot(left, right, 0, 0)
            for q in range(first + b, n, b):
                m_ref[q:q + b, :] = (
                    jnp.where(mine, 0.0, m_ref[q:q + b, :]) - update[q:q + b, :]
                )


def inverse_factor(matrix, m_ref, beside=None):
    n = matrix.shape[0]
    diagonal = jnp.where(iota((n, n), 0) == iota((n, n), 1), matrix, 0.0)
    down = lax.rsqrt(jnp.sum(diagonal, axis=1, keepdims=True))
    across = lax.rsqrt(jnp.sum(diagonal, axis=0, keepdims=True))
    m_ref[...] = matrix * down * across
    invert_factor(m_ref, beside)
    return lower(m_ref[...]) * across


def solve_kernel(
    chunks, rows_total, keys_ref, start_ref, s_hbm, a0_ref, a1_ref, b0_ref, b1_ref,
    modes_ref, scores_ref, basis_ref, pa_ref, pb_ref, gh_ref, gl_ref, xh_ref, xl_ref,
    yh_ref, yl_ref, z_ref, m_ref, s_ref, sem,
):
    load = pltpu.make_async_copy(s_hbm, s_ref, sem)
    load.start()
    packed = (pa_ref, pb_ref)
    halves = ((a0_ref, a1_ref), (b0_ref, b1_ref))
    snap, rank = start_ref.shape
    tiles = snap // TILE
    for part in range(2):
        size = packed[part].shape[0] // chunks
        for q in range(chunks):
            half = halves[part][q // (chunks // 2)]
            at = (q % (chunks // 2)) * size
            to = pl.multiple_of((keys_ref[part] ^ q) * size, 8)
            packed[part][pl.ds(to, size), :] = half[at:at + size, :]
    spots = places(tiles)
    for part in range(2):
        for i, j, row in spots[part][0]:
            value = packed[part][row:row + TILE, :]
            high, low = split(value)
            gh_ref[i * TILE:(i + 1) * TILE, j * TILE:(j + 1) * TILE] = high
            gl_ref[i * TILE:(i + 1) * TILE, j * TILE:(j + 1) * TILE] = low
            if i != j:
                high, low = split(jnp.transpose(value))
                gh_ref[j * TILE:(j + 1) * TILE, i * TILE:(i + 1) * TILE] = high
                gl_ref[j * TILE:(j + 1) * TILE, i * TILE:(i + 1) * TILE] = low
    strips = rank // BLOCK
    step = snap // strips

    def product(at, xh, xl):
        gh = gh_ref[at, :]
        return dot(gh, xh, 1, 0) + (dot(gh, xl, 1, 0) + dot(gl_ref[at, :], xh, 1, 0))

    yh_ref[...], yl_ref[...] = split(start_ref[...])
    for r in range(strips):
        at = pl.ds(r * step, step)
        z_ref[at, :] = product(at, yh_ref[...], yl_ref[...])
    yh_ref[...], yl_ref[...] = split(z_ref[...])

    def iteration(number, carry):
        def beside(k):
            at = pl.ds(k * step, step)
            z_ref[at, :] = product(at, yh_ref[...], yl_ref[...])

        yh = yh_ref[...]
        factor = inverse_factor(dot(yh, yh, 0, 0), m_ref, beside).astype(BF16)

        @pl.when(number == ITERS - 1)
        def _():
            iterate = dot(yh_ref[...], factor, 1, 1) + dot(yl_ref[...], factor, 1, 1)
            xh_ref[...], xl_ref[...] = split(iterate)

        zh, zl = split(z_ref[...])
        yh_ref[...], yl_ref[...] = split(dot(zh, factor, 1, 1) + dot(zl, factor, 1, 1))
        return carry

    lax.fori_loop(0, ITERS, iteration, 0)
    yh, yl = yh_ref[...], yl_ref[...]
    xh, xl = xh_ref[...], xl_ref[...]
    small = dot(xh, yh, 0, 0) + (dot(xh, yl, 0, 0) + dot(xl, yh, 0, 0))
    small = (small + jnp.transpose(small)) * (0.5 / rows_total)
    fh, fl = split(inverse_factor(small, m_ref))
    coef = (dot(xh, fh, 1, 1) + (dot(xh, fl, 1, 1) + dot(xl, fh, 1, 1))).astype(BF16)
    xh_ref[...] = coef

    base = spots[0][1]
    pivots = basis_ref.shape[1]
    picked = jnp.concatenate(
        [pa_ref[base + t * pivots:base + (t + 1) * pivots, :] for t in range(tiles)], axis=1
    )
    panel = dot(picked.astype(BF16), coef, 1, 0)
    gram = dot(panel, panel, 1, 1, HIGHEST)
    same = iota((pivots, pivots), 0) == iota((pivots, pivots), 1)
    diagonal = jnp.where(same, gram, 0.0)
    down = lax.rsqrt(jnp.sum(diagonal, axis=1, keepdims=True))
    across = lax.rsqrt(jnp.sum(diagonal, axis=0, keepdims=True))
    wide = jnp.concatenate(
        [gram * down * across, jnp.where(same, 1.0, 0.0)]
        + [jnp.zeros((pivots, TILE - 2 * pivots), F32)], axis=1
    )
    done = eliminate([wide[8 * g:8 * g + 8] for g in range(pivots // 8)], 0)
    factor = lower(jnp.concatenate(done, axis=0)[:, pivots:2 * pivots]) * across
    turned = dot(factor, panel, 1, 0, HIGHEST)
    basis_ref[...] = dot(panel, factor, 0, 1, HIGHEST)
    th, tl = split(turned)
    ones = jnp.ones((8, rank), BF16)
    chunk = 512
    load.wait()

    def project(r, carry):
        at = pl.ds(pl.multiple_of(r * chunk, chunk), chunk)
        basis = dot(s_ref[at, :], xh_ref[...], 1, 0)
        bh, bl = split(basis)
        modes_ref[at, :] = bh
        coeffs = dot(bh, th, 1, 1) + (dot(bh, tl, 1, 1) + dot(bl, th, 1, 1))
        ch, cl = split(coeffs)
        left = basis - (dot(ch, th, 1, 0) + (dot(ch, tl, 1, 0) + dot(cl, th, 1, 0)))
        qh, ql = split(left * left)
        total = (dot(ones, qh, 1, 1) + dot(ones, ql, 1, 1)) * (1.0 / rank)
        scores_ref[:, at] = total[0:1, :]
        return carry

    lax.fori_loop(0, s_ref.shape[0] // chunk, project, 0)


def solve(snapshots, start, keys, pieces, pivots, rows, chunks, rows_total):
    snap, rank = start.shape
    here = snapshots.shape[0]
    return pl.pallas_call(
        functools.partial(solve_kernel, chunks, rows_total),
        out_shape=[
            jax.ShapeDtypeStruct((here, rank), BF16),
            jax.ShapeDtypeStruct((1, here), F32),
            jax.ShapeDtypeStruct((rank, pivots), F32),
        ],
        in_specs=[SMEM, VMEM, ANY] + [VMEM] * 4,
        out_specs=[VMEM] * 3,
        scratch_shapes=[pltpu.VMEM((r, TILE), F32) for r in rows] + [
            pltpu.VMEM((snap, snap), BF16),
            pltpu.VMEM((snap, snap), BF16),
            pltpu.VMEM((snap, rank), BF16),
            pltpu.VMEM((snap, rank), BF16),
            pltpu.VMEM((snap, rank), BF16),
            pltpu.VMEM((snap, rank), BF16),
            pltpu.VMEM((snap, rank), F32),
            pltpu.VMEM((rank, rank), F32),
            pltpu.VMEM((here, snap), BF16),
            pltpu.SemaphoreType.DMA,
        ],
        name="solve",
    )(keys, start, snapshots, *pieces)


def local(mesh_shape, snapshots, start, pivot_dev, pivot_row):
    here, snap = snapshots.shape
    pivots = pivot_dev.shape[0]
    spots = places(snap // TILE)
    rows = [spots[0][1] + pivots * (snap // TILE), spots[1][1]]
    orders, halvings = exchange_plan(mesh_shape, rows)
    chunks = 1 << halvings
    myself = lax.axis_index(("grp", "blk"))
    keys = jnp.stack([key_of(orders[0], halvings), key_of(orders[1], halvings), myself])
    first = [order[0] for order in orders]
    a0, a1 = local_gram(0, snapshots, pivot_dev, pivot_row, keys, rows[0], chunks)
    got_a = send(a1, *first[0])
    b0, b1 = local_gram(1, snapshots, pivot_dev, pivot_row, keys, rows[1], chunks)
    got = [got_a, send(b1, *first[1])]
    own, other = reduce_parts([a0, b0], [a1, b1], got, orders, halvings)
    pieces = (own[0], other[0], own[1], other[1])
    rows_total = here * mesh_shape["grp"] * mesh_shape["blk"]
    modes, scores, basis = solve(
        snapshots, start, keys, pieces, pivots, rows, chunks, rows_total
    )
    return modes, scores.reshape(here), basis


def solution(mesh):
    placed = (P(("grp", "blk"), None), P(), P(), P())

    def body(*args):
        return local(dict(mesh.shape), *args)

    return jax.shard_map(
        body,
        mesh=mesh,
        in_specs=placed,
        out_specs=(P(("grp", "blk"), None), P(("grp", "blk")), P()),
        check_vma=False,
    )
```

time: 155 us -> 136 us (0.88)
  Pallas kernels: 86 us -> 70.1 us
  waiting for transfers between devices: 43.1 us -> 35.6 us
  starting transfers between devices: 17.8 us -> 24 us
    pallas_call x1, Pallas kernels: 78.2 us -> 58.5 us  [solve(): pl.pallas_call(functools.partial(solve_kernel, chunks, rows_total), out_s...]
    ppermute x16, waiting for transfers between devices: 43.1 us -> 35.6 us  [send(): return lax.ppermute(value, axis, [(i, i ^ mask) for i in range(size)])]
    ppermute x16, starting transfers between devices: 17.8 us -> 24 us  [send(): return lax.ppermute(value, axis, [(i, i ^ mask) for i in range(size)])]
    pallas_call x1 -> x2, Pallas kernels: 7.82 us -> 11.6 us  [local_gram(): pl.pallas_call(functools.partial(gram_kernel, part, chunks), out_shape=[j...]
    unnamed x12 -> x14, local copies, waits for them, and re-layouts: 3.31 us -> 3.3 us
  transfers between devices with their start and end apart: 16 -> 16, of which waited for: 13 -> 12; matrix products, arithmetic and copies ran while one was open for 2% -> 1% of each run, Pallas kernels for 0% -> 5%
where the time goes in v2:
time: 136 us
  Pallas kernels  70.1 us (52%)
  waiting for transfers between devices  35.6 us (26%)
  starting transfers between devices  24 us (18%)
  local copies, waits for them, and re-layouts  3.37 us (2%)
  other arithmetic  2.03 us (1%)
    pallas_call x1, Pallas kernels, solve(): pl.pallas_call(functools.partial(solve_kernel, chunks, rows_total), out_s...  58.5 us
    ppermute x16, waiting for transfers between devices, send(): return lax.ppermute(value, axis, [(i, i ^ mask) for i in range(size)])  35.6 us
    ppermute x16, starting transfers between devices, send(): return lax.ppermute(value, axis, [(i, i ^ mask) for i in range(size)])  24 us
    pallas_call x2, Pallas kernels, local_gram(): pl.pallas_call(functools.partial(gram_kernel, part, chunks), out_shape=[j...  11.6 us
    unnamed x14, local copies, waits for them, and re-layouts  3.3 us
  transfers between devices with their start and end apart: 16, of which 12 were waited for; matrix products, arithmetic and copies ran while one was open for 1% of the time, Pallas kernels for 5%

profile of v2, /device:TPU:0, one launch (start us, length us, event | category | flops | bytes accessed | tf_op | source)
XLA Modules:
  0.0 136.0 jit_solution(148500990377187098)
XLA Ops:
  0.7 0.6 pad_add_fusion.keys_ref
  1.2 5.2 %shard_map.68 = (f32[1152,128]{1,0:T(8,128)}, f32[1152,128]{1,0:T(8,128)}) custom-call(s32[32]{0:T(128)} %dev_ref.3, s32[32]{0:T(128)} %row_ref.3, s32[3]{0:T(128)} %pad_add_fusion.keys_ref, bf16[2048,1024]{1,0:T(8,128)(2,1)} %s_hbm.5), custom_call_target="tpu_custom_call" | custom-call | tf_op jit(solution)/shard_map/pallas_call | solution.py:165
  6.4 0.0 copy-start.3
  6.4 0.6 collective-permute-start.3
  7.0 6.4 %shard_map.67 = (f32[1280,128]{1,0:T(8,128)}, f32[1280,128]{1,0:T(8,128)}) custom-call(s32[32]{0:T(128)} %dev_ref.3, s32[32]{0:T(128)} %row_ref.3, s32[3]{0:T(128)} %pad_add_fusion.keys_ref, bf16[2048,1024]{1,0:T(8,128)(2,1)} %s_hbm.5), custom_call_target="tpu_custom_call" | custom-call | tf_op jit(solution)/shard_map/pallas_call | solution.py:165
  13.4 0.2 collective-permute-start
  13.6 0.0 collective-permute-done.3
  13.6 0.0 copy-done.3
  13.6 0.1 slice_add_fusion.3
  13.7 2.9 %collective-permute-start.4 = (f32[576,128]{1,0:T(8,128)S(1)}, f32[576,128]{1,0:T(8,128)S(1)}, u32[]{:S(2)}, u32[]{:S(2)}) collective-permute-start(f32[576,128]{1,0:T(8,128)S(1)} %get-tuple-element.27), channel_id=1, source_target_pairs={{0,2},{1,3},{2,0},{3,1},{4,6},{5,7},{6,4},{7,5},{8,10},{9,11},{10,... | collective-permute-start | bytes 884744 | tf_op jit(solution)/shard_map/ppermute | solution.py:76
  16.6 0.0 collective-permute-done
  16.6 1.1 slice_add_fusion.1
  17.7 1.8 %collective-permute-start.1 = (f32[640,128]{1,0:T(8,128)S(1)}, f32[640,128]{1,0:T(8,128)S(1)}, u32[]{:S(2)}, u32[]{:S(2)}) collective-permute-start(f32[640,128]{1,0:T(8,128)S(1)} %get-tuple-element.25), channel_id=1, source_target_pairs={{0,4},{4,0},{8,12},{12,8},{16,20},{20,16},{24,28},{28,24},{1,5},{5... | collective-permute-start | bytes 983048 | tf_op jit(solution)/shard_map/ppermute | solution.py:76
  19.6 4.3 %collective-permute-done.4 = f32[576,128]{1,0:T(8,128)S(1)} collective-permute-done((f32[576,128]{1,0:T(8,128)S(1)}, f32[576,128]{1,0:T(8,128)S(1)}, u32[]{:S(2)}, u32[]{:S(2)}) %collective-permute-start.4) | collective-permute-done | bytes 294944 | tf_op jit(solution)/shard_map/ppermute | solution.py:76
  23.9 1.8 %collective-permute-start.5 = (f32[288,128]{1,0:T(8,128)S(1)}, f32[288,128]{1,0:T(8,128)S(1)}, u32[]{:S(2)}, u32[]{:S(2)}) collective-permute-start(f32[288,128]{1,0:T(8,128)S(1)} %get-tuple-element.31), channel_id=1, source_target_pairs={{0,4},{4,0},{8,12},{12,8},{16,20},{20,16},{24,28},{28,24},{1,5},{5... | collective-permute-start | bytes 442376 | tf_op jit(solution)/shard_map/ppermute | solution.py:76
  25.7 2.7 %collective-permute-done.1 = f32[640,128]{1,0:T(8,128)S(1)} collective-permute-done((f32[640,128]{1,0:T(8,128)S(1)}, f32[640,128]{1,0:T(8,128)S(1)}, u32[]{:S(2)}, u32[]{:S(2)}) %collective-permute-start.1) | collective-permute-done | bytes 327712 | tf_op jit(solution)/shard_map/ppermute | solution.py:76
  28.4 0.1 slice_add_fusion.5
  28.4 1.9 %collective-permute-start.2 = (f32[320,128]{1,0:T(8,128)S(1)}, f32[320,128]{1,0:T(8,128)S(1)}, u32[]{:S(2)}, u32[]{:S(2)}) collective-permute-start(f32[320,128]{1,0:T(8,128)S(1)} %get-tuple-element.29), channel_id=1, source_target_pairs={{0,2},{1,3},{2,0},{3,1},{4,6},{5,7},{6,4},{7,5},{8,10},{9,11},{10,... | collective-permute-start | bytes 491528 | tf_op jit(solution)/shard_map/ppermute | solution.py:76
  30.3 0.7 collective-permute-done.5
  31.0 2.8 %collective-permute-done.2 = f32[320,128]{1,0:T(8,128)S(1)} collective-permute-done((f32[320,128]{1,0:T(8,128)S(1)}, f32[320,128]{1,0:T(8,128)S(1)}, u32[]{:S(2)}, u32[]{:S(2)}) %collective-permute-start.2) | collective-permute-done | bytes 163872 | tf_op jit(solution)/shard_map/ppermute | solution.py:76
  33.9 1.9 %collective-permute-start.6 = (f32[304,128]{1,0:T(8,128)S(1)}, f32[304,128]{1,0:T(8,128)S(1)}, u32[]{:S(2)}, u32[]{:S(2)}) collective-permute-start(f32[304,128]{1,0:T(8,128)S(1)} %pad_maximum_fusion.3), channel_id=1, source_target_pairs={{0,8},{4,12},{8,0},{12,4},{16,24},{20,28},{24,16},{28,20},{1,9},{5... | collective-permute-start | bytes 466952 | tf_op jit(solution)/shard_map/ppermute | solution.py:76
  35.8 3.4 %collective-permute-done.6 = f32[304,128]{1,0:T(8,128)S(1)} collective-permute-done((f32[304,128]{1,0:T(8,128)S(1)}, f32[304,128]{1,0:T(8,128)S(1)}, u32[]{:S(2)}, u32[]{:S(2)}) %collective-permute-start.6) | collective-permute-done | bytes 155680 | tf_op jit(solution)/shard_map/ppermute | solution.py:76
  39.2 3.8 %collective-permute-start.7 = (f32[152,128]{1,0:T(8,128)S(1)}, f32[152,128]{1,0:T(8,128)S(1)}, u32[]{:S(2)}, u32[]{:S(2)}) collective-permute-start(f32[152,128]{1,0:T(8,128)S(1)} %pad_maximum_fusion.6), channel_id=1, source_target_pairs={{0,16},{4,20},{8,24},{12,28},{16,0},{20,4},{24,8},{28,12},{1,17},{... | collective-permute-start | bytes 233480 | tf_op jit(solution)/shard_map/ppermute | solution.py:76
  42.9 4.3 %collective-permute-done.7 = f32[152,128]{1,0:T(8,128)S(1)} collective-permute-done((f32[152,128]{1,0:T(8,128)S(1)}, f32[152,128]{1,0:T(8,128)S(1)}, u32[]{:S(2)}, u32[]{:S(2)}) %collective-permute-start.7) | collective-permute-done | bytes 77856 | tf_op jit(solution)/shard_map/ppermute | solution.py:76
  47.3 1.1 collective-permute-start.8
  48.5 4.5 %collective-permute-done.8 = f32[152,128]{1,0:T(8,128)S(1)} collective-permute-done((f32[152,128]{1,0:T(8,128)S(1)}, f32[152,128]{1,0:T(8,128)S(1)}, u32[]{:S(2)}, u32[]{:S(2)}) %collective-permute-start.8) | collective-permute-done | bytes 77856 | tf_op jit(solution)/shard_map/ppermute | solution.py:76
  53.0 1.7 %collective-permute-start.9 = (f32[304,128]{1,0:T(8,128)S(1)}, f32[304,128]{1,0:T(8,128)S(1)}, u32[]{:S(2)}, u32[]{:S(2)}) collective-permute-start(f32[304,128]{1,0:T(8,128)S(1)} %pad_maximum_fusion.4), channel_id=1, source_target_pairs={{0,8},{4,12},{8,0},{12,4},{16,24},{20,28},{24,16},{28,20},{1,9},{5... | collective-permute-start | bytes 466952 | tf_op jit(solution)/shard_map/ppermute | solution.py:76
  54.7 3.5 %collective-permute-done.9 = f32[304,128]{1,0:T(8,128)S(1)} collective-permute-done((f32[304,128]{1,0:T(8,128)S(1)}, f32[304,128]{1,0:T(8,128)S(1)}, u32[]{:S(2)}, u32[]{:S(2)}) %collective-permute-start.9) | collective-permute-done | bytes 155680 | tf_op jit(solution)/shard_map/ppermute | solution.py:76
  58.3 1.6 %collective-permute-start.10 = (f32[320,128]{1,0:T(8,128)S(1)}, f32[320,128]{1,0:T(8,128)S(1)}, u32[]{:S(2)}, u32[]{:S(2)}) collective-permute-start(f32[320,128]{1,0:T(8,128)S(1)} %pad_maximum_fusion.2), channel_id=1, source_target_pairs={{0,2},{1,3},{2,0},{3,1},{4,6},{5,7},{6,4},{7,5},{8,10},{9,11},{10,... | collective-permute-start | bytes 491528 | tf_op jit(solution)/shard_map/ppermute | solution.py:76
  59.9 1.5 %collective-permute-start.13 = (f32[288,128]{1,0:T(8,128)S(1)}, f32[288,128]{1,0:T(8,128)S(1)}, u32[]{:S(2)}, u32[]{:S(2)}) collective-permute-start(f32[288,128]{1,0:T(8,128)S(1)} %pad_maximum_fusion.5), channel_id=1, source_target_pairs={{0,4},{4,0},{8,12},{12,8},{16,20},{20,16},{24,28},{28,24},{1,5},{5... | collective-permute-start | bytes 442376 | tf_op jit(solution)/shard_map/ppermute | solution.py:76
  61.5 2.3 %collective-permute-done.10 = f32[320,128]{1,0:T(8,128)S(1)} collective-permute-done((f32[320,128]{1,0:T(8,128)S(1)}, f32[320,128]{1,0:T(8,128)S(1)}, u32[]{:S(2)}, u32[]{:S(2)}) %collective-permute-start.10) | collective-permute-done | bytes 163872 | tf_op jit(solution)/shard_map/ppermute | solution.py:76
  63.8 1.4 %collective-permute-start.11 = (f32[640,128]{1,0:T(8,128)S(1)}, f32[640,128]{1,0:T(8,128)S(1)}, u32[]{:S(2)}, u32[]{:S(2)}) collective-permute-start(f32[640,128]{1,0:T(8,128)S(1)} %pad_maximum_fusion), channel_id=1, source_target_pairs={{0,4},{4,0},{8,12},{12,8},{16,20},{20,16},{24,28},{28,24},{1,5},{5... | collective-permute-start | bytes 983048 | tf_op jit(solution)/shard_map/ppermute | solution.py:76
  65.3 0.0 collective-permute-done.13
  65.3 1.6 %collective-permute-start.14 = (f32[576,128]{1,0:T(8,128)S(1)}, f32[576,128]{1,0:T(8,128)S(1)}, u32[]{:S(2)}, u32[]{:S(2)}) collective-permute-start(f32[576,128]{1,0:T(8,128)S(1)} %pad_maximum_fusion.1), channel_id=1, source_target_pairs={{0,2},{1,3},{2,0},{3,1},{4,6},{5,7},{6,4},{7,5},{8,10},{9,11},{10,... | collective-permute-start | bytes 884744 | tf_op jit(solution)/shard_map/ppermute | solution.py:76
  66.9 4.1 %collective-permute-done.11 = f32[640,128]{1,0:T(8,128)S(1)} collective-permute-done((f32[640,128]{1,0:T(8,128)S(1)}, f32[640,128]{1,0:T(8,128)S(1)}, u32[]{:S(2)}, u32[]{:S(2)}) %collective-permute-start.11) | collective-permute-done | bytes 327712 | tf_op jit(solution)/shard_map/ppermute | solution.py:76
  71.0 0.0 copy-start
  71.0 0.1 collective-permute-start.12
  71.1 1.0 collective-permute-done.14
  72.1 0.0 copy-start.1
  72.1 0.1 collective-permute-start.15
  72.2 2.0 %collective-permute-done.15.b1_ref = f32[1152,128]{1,0:T(8,128)S(1)} collective-permute-done((f32[1152,128]{1,0:T(8,128)S(1)}, f32[1152,128]{1,0:T(8,128)S(1)}, u32[]{:S(2)}, u32[]{:S(2)}) %collective-permute-start.15) | collective-permute-done | bytes 589856 | tf_op jit(solution)/shard_map/ppermute | solution.py:76
  74.2 0.0 collective-permute-done.12.a1_ref
  74.2 0.0 copy-done
  74.2 0.0 copy-done.1
  74.2 0.8 copy-done.4
  75.0 0.9 copy-done.2
  75.9 58.5 %solve.1 = (bf16[2048,256]{1,0:T(8,128)(2,1)}, f32[1,2048]{1,0:T(1,128)}, f32[256,32]{1,0:T(8,128)}) custom-call(s32[3]{0:T(128)} %pad_add_fusion.keys_ref, f32[1024,256]{1,0:T(8,128)} %start_ref.1, bf16[2048,1024]{1,0:T(8,128)(2,1)} %s_hbm.5, f32[1280,128]{1,0:T(8,128)} %copy-done, f32[1280,128]{1,0:T(8,128)} %copy-done.2, f32[1152,128]{1,0:T(8,128)} %copy-done.1, ...), custom_call_target="tpu_custom_call" | custom-call | tf_op jit(solution)/shard_map/solve/pallas_call | solution.py:397
  134.4 1.6 %copy.7 = f32[256,32]{0,1:T(8,128)} copy(f32[256,32]{1,0:T(8,128)} %get-tuple-element.19) | data formatting | bytes 65536
  (25 shorter events, 0.3 us)
Async XLA Ops:
  6.4 7.2 %copy-start.3 = (f32[1152,128]{1,0:T(8,128)S(1)}, f32[1152,128]{1,0:T(8,128)}, u32[]{:S(2)}) copy-start(f32[1152,128]{1,0:T(8,128)} %get-tuple-element.12) | copy-start | bytes 1769476
  6.4 7.2 %collective-permute-start.3 = (f32[1152,128]{1,0:T(8,128)}, f32[1152,128]{1,0:T(8,128)S(1)}, u32[]{:S(2)}, u32[]{:S(2)}) collective-permute-start(f32[1152,128]{1,0:T(8,128)} %get-tuple-element.13), channel_id=1, source_target_pairs={{0,1},{1,0},{2,3},{3,2},{4,5},{5,4},{6,7},{7,6},{8,9},{9,8},{10,11... | collective-permute-start | bytes 1769480 | tf_op jit(solution)/shard_map/ppermute | solution.py:76
  13.4 3.2 %collective-permute-start = (f32[1280,128]{1,0:T(8,128)}, f32[1280,128]{1,0:T(8,128)S(1)}, u32[]{:S(2)}, u32[]{:S(2)}) collective-permute-start(f32[1280,128]{1,0:T(8,128)} %get-tuple-element.11), channel_id=1, source_target_pairs={{0,1},{1,0},{2,3},{3,2},{4,5},{5,4},{6,7},{7,6},{8,9},{9,8},{10,11... | collective-permute-start | bytes 1966088 | tf_op jit(solution)/shard_map/ppermute | solution.py:76
  13.7 10.2 %collective-permute-start.4 = (f32[576,128]{1,0:T(8,128)S(1)}, f32[576,128]{1,0:T(8,128)S(1)}, u32[]{:S(2)}, u32[]{:S(2)}) collective-permute-start(f32[576,128]{1,0:T(8,128)S(1)} %get-tuple-element.27), channel_id=1, source_target_pairs={{0,2},{1,3},{2,0},{3,1},{4,6},{5,7},{6,4},{7,5},{8,10},{9,11},{10,... | collective-permute-start | bytes 884744 | tf_op jit(solution)/shard_map/ppermute | solution.py:76
  17.7 10.6 %collective-permute-start.1 = (f32[640,128]{1,0:T(8,128)S(1)}, f32[640,128]{1,0:T(8,128)S(1)}, u32[]{:S(2)}, u32[]{:S(2)}) collective-permute-start(f32[640,128]{1,0:T(8,128)S(1)} %get-tuple-element.25), channel_id=1, source_target_pairs={{0,4},{4,0},{8,12},{12,8},{16,20},{20,16},{24,28},{28,24},{1,5},{5... | collective-permute-start | bytes 983048 | tf_op jit(solution)/shard_map/ppermute | solution.py:76
  23.9 7.0 %collective-permute-start.5 = (f32[288,128]{1,0:T(8,128)S(1)}, f32[288,128]{1,0:T(8,128)S(1)}, u32[]{:S(2)}, u32[]{:S(2)}) collective-permute-start(f32[288,128]{1,0:T(8,128)S(1)} %get-tuple-element.31), channel_id=1, source_target_pairs={{0,4},{4,0},{8,12},{12,8},{16,20},{20,16},{24,28},{28,24},{1,5},{5... | collective-permute-start | bytes 442376 | tf_op jit(solution)/shard_map/ppermute | solution.py:76
  28.4 5.4 %collective-permute-start.2 = (f32[320,128]{1,0:T(8,128)S(1)}, f32[320,128]{1,0:T(8,128)S(1)}, u32[]{:S(2)}, u32[]{:S(2)}) collective-permute-start(f32[320,128]{1,0:T(8,128)S(1)} %get-tuple-element.29), channel_id=1, source_target_pairs={{0,2},{1,3},{2,0},{3,1},{4,6},{5,7},{6,4},{7,5},{8,10},{9,11},{10,... | collective-permute-start | bytes 491528 | tf_op jit(solution)/shard_map/ppermute | solution.py:76
  33.9 5.3 %collective-permute-start.6 = (f32[304,128]{1,0:T(8,128)S(1)}, f32[304,128]{1,0:T(8,128)S(1)}, u32[]{:S(2)}, u32[]{:S(2)}) collective-permute-start(f32[304,128]{1,0:T(8,128)S(1)} %pad_maximum_fusion.3), channel_id=1, source_target_pairs={{0,8},{4,12},{8,0},{12,4},{16,24},{20,28},{24,16},{28,20},{1,9},{5... | collective-permute-start | bytes 466952 | tf_op jit(solution)/shard_map/ppermute | solution.py:76
  39.2 8.1 %collective-permute-start.7 = (f32[152,128]{1,0:T(8,128)S(1)}, f32[152,128]{1,0:T(8,128)S(1)}, u32[]{:S(2)}, u32[]{:S(2)}) collective-permute-start(f32[152,128]{1,0:T(8,128)S(1)} %pad_maximum_fusion.6), channel_id=1, source_target_pairs={{0,16},{4,20},{8,24},{12,28},{16,0},{20,4},{24,8},{28,12},{1,17},{... | collective-permute-start | bytes 233480 | tf_op jit(solution)/shard_map/ppermute | solution.py:76
  47.3 5.6 %collective-permute-start.8 = (f32[152,128]{1,0:T(8,128)S(1)}, f32[152,128]{1,0:T(8,128)S(1)}, u32[]{:S(2)}, u32[]{:S(2)}) collective-permute-start(f32[152,128]{1,0:T(8,128)S(1)} %pad_maximum_fusion.7), channel_id=1, source_target_pairs={{0,16},{4,20},{8,24},{12,28},{16,0},{20,4},{24,8},{28,12},{1,17},{... | collective-permute-start | bytes 233480 | tf_op jit(solution)/shard_map/ppermute | solution.py:76
  53.0 5.3 %collective-permute-start.9 = (f32[304,128]{1,0:T(8,128)S(1)}, f32[304,128]{1,0:T(8,128)S(1)}, u32[]{:S(2)}, u32[]{:S(2)}) collective-permute-start(f32[304,128]{1,0:T(8,128)S(1)} %pad_maximum_fusion.4), channel_id=1, source_target_pairs={{0,8},{4,12},{8,0},{12,4},{16,24},{20,28},{24,16},{28,20},{1,9},{5... | collective-permute-start | bytes 466952 | tf_op jit(solution)/shard_map/ppermute | solution.py:76
  58.3 5.5 %collective-permute-start.10 = (f32[320,128]{1,0:T(8,128)S(1)}, f32[320,128]{1,0:T(8,128)S(1)}, u32[]{:S(2)}, u32[]{:S(2)}) collective-permute-start(f32[320,128]{1,0:T(8,128)S(1)} %pad_maximum_fusion.2), channel_id=1, source_target_pairs={{0,2},{1,3},{2,0},{3,1},{4,6},{5,7},{6,4},{7,5},{8,10},{9,11},{10,... | collective-permute-start | bytes 491528 | tf_op jit(solution)/shard_map/ppermute | solution.py:76
  59.9 5.3 %collective-permute-start.13 = (f32[288,128]{1,0:T(8,128)S(1)}, f32[288,128]{1,0:T(8,128)S(1)}, u32[]{:S(2)}, u32[]{:S(2)}) collective-permute-start(f32[288,128]{1,0:T(8,128)S(1)} %pad_maximum_fusion.5), channel_id=1, source_target_pairs={{0,4},{4,0},{8,12},{12,8},{16,20},{20,16},{24,28},{28,24},{1,5},{5... | collective-permute-start | bytes 442376 | tf_op jit(solution)/shard_map/ppermute | solution.py:76
  63.8 7.1 %collective-permute-start.11 = (f32[640,128]{1,0:T(8,128)S(1)}, f32[640,128]{1,0:T(8,128)S(1)}, u32[]{:S(2)}, u32[]{:S(2)}) collective-permute-start(f32[640,128]{1,0:T(8,128)S(1)} %pad_maximum_fusion), channel_id=1, source_target_pairs={{0,4},{4,0},{8,12},{12,8},{16,20},{20,16},{24,28},{28,24},{1,5},{5... | collective-permute-start | bytes 983048 | tf_op jit(solution)/shard_map/ppermute | solution.py:76
  65.3 6.8 %collective-permute-start.14 = (f32[576,128]{1,0:T(8,128)S(1)}, f32[576,128]{1,0:T(8,128)S(1)}, u32[]{:S(2)}, u32[]{:S(2)}) collective-permute-start(f32[576,128]{1,0:T(8,128)S(1)} %pad_maximum_fusion.1), channel_id=1, source_target_pairs={{0,2},{1,3},{2,0},{3,1},{4,6},{5,7},{6,4},{7,5},{8,10},{9,11},{10,... | collective-permute-start | bytes 884744 | tf_op jit(solution)/shard_map/ppermute | solution.py:76
  71.0 3.2 %copy-start = (f32[1280,128]{1,0:T(8,128)}, f32[1280,128]{1,0:T(8,128)S(1)}, u32[]{:S(2)}) copy-start(f32[1280,128]{1,0:T(8,128)S(1)} %constant_dynamic-update-slice_fusion.a0_ref) | copy-start | bytes 1966084
  71.0 3.2 %collective-permute-start.12 = (f32[1280,128]{1,0:T(8,128)S(1)}, f32[1280,128]{1,0:T(8,128)S(1)}, u32[]{:S(2)}, u32[]{:S(2)}) collective-permute-start(f32[1280,128]{1,0:T(8,128)S(1)} %constant_dynamic-update-slice_fusion.a0_ref), channel_id=1, source_target_pairs={{0,1},{1,0},{2,3},{3,2},{4,5},{5,4},{6,7},{7,6},{8,9},{9,8},{10,11... | collective-permute-start | bytes 1966088 | tf_op jit(solution)/shard_map/ppermute | solution.py:76
  72.1 2.1 %copy-start.1 = (f32[1152,128]{1,0:T(8,128)}, f32[1152,128]{1,0:T(8,128)S(1)}, u32[]{:S(2)}) copy-start(f32[1152,128]{1,0:T(8,128)S(1)} %constant_dynamic-update-slice_fusion.5.b0_ref) | copy-start | bytes 1769476
  72.1 2.1 %collective-permute-start.15 = (f32[1152,128]{1,0:T(8,128)S(1)}, f32[1152,128]{1,0:T(8,128)S(1)}, u32[]{:S(2)}, u32[]{:S(2)}) collective-permute-start(f32[1152,128]{1,0:T(8,128)S(1)} %constant_dynamic-update-slice_fusion.5.b0_ref), channel_id=1, source_target_pairs={{0,1},{1,0},{2,3},{3,2},{4,5},{5,4},{6,7},{7,6},{8,9},{9,8},{10,11... | collective-permute-start | bytes 1769480 | tf_op jit(solution)/shard_map/ppermute | solution.py:76
  74.2 0.8 copy-start.4
  75.0 0.9 copy-start.2

commit v3 on v2

--- a/solution.py
+++ b/solution.py
@@ -6,17 +6,17 @@
 from jax.experimental.pallas import tpu as pltpu
 from jax.sharding import PartitionSpec as P
 
-
 ITERS = 4
 TILE = 128
 BAND = 2
 BLOCK = 64
-LOADS = 4
+LOADS = 2
+GRANT = 28 << 20
 F32, BF16 = jnp.float32, jnp.bfloat16
 HIGHEST = lax.Precision.HIGHEST
 VMEM = pl.BlockSpec(memory_space=pltpu.VMEM)
 SMEM = pl.BlockSpec(memory_space=pltpu.SMEM)
-ANY = pl.BlockSpec(memory_space=pl.ANY)
+HBM = pl.BlockSpec(memory_space=pltpu.HBM)
 
 
 def dot(a, b, ca, cb, precision=None):
@@ -28,6 +28,10 @@
 def split(value):
     high = value.astype(BF16)
     return high, (value - high.astype(F32)).astype(BF16)
+
+
+def in_hbm(value):
+    return pltpu.with_memory_space_constraint(value, pltpu.HBM)
 
 
 def iota(shape, dim):
@@ -54,21 +58,37 @@
 
 
 def exchange_plan(mesh_shape, rows):
-    grp = [("grp", 1 << b) for b in range(mesh_shape["grp"].bit_length() - 1)]
-    blk = [("blk", 1 << b) for b in range(mesh_shape["blk"].bit_length() - 1)]
-    rest = blk[1:] + grp[2:]
+    grp = [("grp", (1 << b,)) for b in range(mesh_shape["grp"].bit_length() - 1)]
+    blk = [("blk", (1 << b,)) for b in range(mesh_shape["blk"].bit_length() - 1)]
+    pair = [("blk", blk[1][1] + blk[2][1])] if len(blk) > 2 else blk[1:2]
+    rest = pair + blk[3:] + grp[2:]
     orders = (grp[:1] + blk[:1] + grp[1:2] + rest, grp[:1] + grp[1:2] + blk[:1] + rest)
-    halvings = 0
-    while halvings < len(orders[0]) and all(r % (8 << (halvings + 1)) == 0 for r in rows):
+    halvings, ways = 0, 1
+    for _, masks in orders[0]:
+        ways *= 1 << len(masks)
+        if any(r % (8 * ways) for r in rows):
+            break
         halvings += 1
     return orders, halvings
 
 
+def chunks_of(order, halvings):
+    return 1 << sum(len(masks) for _, masks in order[:halvings])
+
+
 def key_of(order, halvings):
     key = jnp.int32(0)
-    for axis, mask in order[:halvings]:
-        key = key * 2 + jnp.where((lax.axis_index(axis) & mask) != 0, 1, 0)
+    for axis, masks in order[:halvings]:
+        for mask in masks:
+            key = key * 2 + jnp.where((lax.axis_index(axis) & mask) != 0, 1, 0)
     return key
+
+
+def partners(masks):
+    result = [0]
+    for mask in masks:
+        result = [m ^ extra for m in result for extra in (0, mask)]
+    return result
 
 
 def send(value, axis, mask):
@@ -76,103 +96,118 @@
     return lax.ppermute(value, axis, [(i, i ^ mask) for i in range(size)])
 
 
-def exchange(values, steps):
-    if all(step == steps[0] for step in steps):
-        got = send(jnp.concatenate(values, axis=0), *steps[0])
+def exchange(values, stages, mask_at):
+    if all(stage == stages[0] for stage in stages):
+        axis, masks = stages[0]
+        got = send(jnp.concatenate(values, axis=0), axis, partners(masks)[mask_at])
         first = values[0].shape[0]
         return [got[:first], got[first:]]
-    result = []
-    for value, step in zip(values, steps):
-        result.append(send(value, *step))
-    return result
-
-
-def halve(values, got):
-    halves = [v.shape[0] // 2 for v in values]
-    sent = [v[h:] + g[h:] for v, g, h in zip(values, got, halves)]
-    kept = [v[:h] + g[:h] for v, g, h in zip(values, got, halves)]
-    return sent, kept
-
-
-def reduce_parts(kept, sent, got, orders, halvings):
-    steps = list(zip(*orders))
-    for number in range(1, len(steps)):
+    return [
+        send(value, axis, partners(masks)[mask_at])
+        for value, (axis, masks) in zip(values, stages)
+    ]
+
+
+def add_up(terms):
+    while len(terms) > 1:
+        terms = [a + b for a, b in zip(terms[::2], terms[1::2])]
+    return terms[0]
+
+
+def reduce_parts(kept, sent, orders, halvings):
+    stages = list(zip(*orders))
+    terms = [[v, send(s, order[0][0], order[0][1][0])] for v, s, order in zip(kept, sent, orders)]
+    for number in range(1, len(stages)):
+        stage = stages[number]
+        count = 1 << len(stage[0][1])
         if number < halvings:
-            sent, kept = halve(kept, got)
-            got = exchange(sent, steps[number])
+            sizes = [t[0].shape[0] // count for t in terms]
+            cut = [
+                [add_up([v[q * size:(q + 1) * size] for v in t]) for q in range(count)]
+                for t, size in zip(terms, sizes)
+            ]
+            got = [exchange([c[q] for c in cut], stage, q) for q in range(1, count)]
+            terms = [[c[0]] + [g[part] for g in got] for part, c in enumerate(cut)]
         else:
-            kept = [v + g for v, g in zip(kept, got)]
-            got = exchange(kept, steps[number])
-    kept = [v + g for v, g in zip(kept, got)]
+            whole = [add_up(t) for t in terms]
+            got = [exchange(whole, stage, q) for q in range(1, count)]
+            terms = [[v] + [g[part] for g in got] for part, v in enumerate(whole)]
+    kept = [add_up(t) for t in terms]
     for number in range(halvings - 1, 0, -1):
-        got = exchange(kept, steps[number])
-        kept = [jnp.concatenate([v, g], axis=0) for v, g in zip(kept, got)]
-    return kept, [send(v, *order[0]) for v, order in zip(kept, orders)]
-
-
-def gram_kernel(part, chunks, dev_ref, row_ref, keys_ref, s_hbm, low_ref, high_ref, s_ref, work, sems):
+        stage = stages[number]
+        got = [exchange(kept, stage, q) for q in range(1, 1 << len(stage[0][1]))]
+        kept = [
+            jnp.concatenate([v] + [g[part] for g in got], axis=0)
+            for part, v in enumerate(kept)
+        ]
+    return kept, [send(v, order[0][0], order[0][1][0]) for v, order in zip(kept, orders)]
+
+
+def gram_kernel(chunks, dev_ref, row_ref, keys_ref, s_hbm, *refs):
+    outs, work, s_ref, sems = refs[:4], refs[4:6], refs[6], refs[7]
     tiles = s_ref.shape[1] // TILE
     spots = places(tiles)
-    here = s_ref.shape[0]
-    piece = here // LOADS
+    piece = s_ref.shape[0] // LOADS
     copies = []
     for q in range(LOADS):
         at = pl.ds(q * piece, piece)
         copies.append(pltpu.make_async_copy(s_hbm.at[at, :], s_ref.at[at, :], sems.at[q]))
         copies[-1].start()
-    where = {(i, j): row for i, j, row in spots[part][0]}
     for q in range(LOADS):
         copies[q].wait()
         rows = slice(q * piece, (q + 1) * piece)
-        for band in bands_of(tiles)[part]:
-            first = band * BAND * TILE
-            strip = dot(s_ref[rows, first:first + BAND * TILE], s_ref[rows, first:], 0, 0)
-            for a in range(BAND):
-                i = band * BAND + a
-                for j in range(i, tiles):
-                    col = (j - band * BAND) * TILE
-                    row = where[(i, j)]
-                    term = strip[a * TILE:(a + 1) * TILE, col:col + TILE]
-                    if q:
-                        term = work[row:row + TILE, :] + term
-                    work[row:row + TILE, :] = term
-    if part == 0:
-        base = spots[0][1]
-        pivots = dev_ref.shape[0]
-        sub = iota((16, s_ref.shape[1]), 0)
-
-        def pick(p, carry):
-            at = row_ref[p]
-            group = pl.multiple_of((at // 16) * 16, 16)
-            rows = s_ref[pl.ds(group, 16), :].astype(F32)
-            wanted = jnp.where(dev_ref[p] == keys_ref[2], at - group, -1)
-            row = jnp.sum(jnp.where(sub == wanted, rows, 0.0), axis=0, keepdims=True)
-            for t in range(tiles):
-                work[pl.ds(base + t * pivots + p, 1), :] = row[:, t * TILE:(t + 1) * TILE]
-            return carry
-
-        lax.fori_loop(0, pivots, pick, 0)
-    size = work.shape[0] // chunks
-    for q in range(chunks):
-        out = low_ref if q < chunks // 2 else high_ref
-        to = (q % (chunks // 2)) * size
-        at = pl.multiple_of((keys_ref[part] ^ q) * size, 8)
-        out[to:to + size, :] = work[pl.ds(at, size), :]
-
-
-def local_gram(part, snapshots, pivot_dev, pivot_row, keys, rows, chunks):
-    here, snap = snapshots.shape
+        for part in range(2):
+            where = {(i, j): row for i, j, row in spots[part][0]}
+            for band in bands_of(tiles)[part]:
+                first = band * BAND * TILE
+                strip = dot(s_ref[rows, first:first + BAND * TILE], s_ref[rows, first:], 0, 0)
+                for a in range(BAND):
+                    i = band * BAND + a
+                    for j in range(i, tiles):
+                        col = (j - band * BAND) * TILE
+                        row = where[(i, j)]
+                        term = strip[a * TILE:(a + 1) * TILE, col:col + TILE]
+                        if q:
+                            term = work[part][row:row + TILE, :] + term
+                        work[part][row:row + TILE, :] = term
+    base = spots[0][1]
+    pivots = dev_ref.shape[0]
+    sub = iota((16, s_ref.shape[1]), 0)
+
+    def pick(p, carry):
+        at = row_ref[p]
+        group = pl.multiple_of((at // 16) * 16, 16)
+        rows = s_ref[pl.ds(group, 16), :].astype(F32)
+        wanted = jnp.where(dev_ref[p] == keys_ref[2], at - group, -1)
+        row = jnp.sum(jnp.where(sub == wanted, rows, 0.0), axis=0, keepdims=True)
+        for t in range(tiles):
+            work[0][pl.ds(base + t * pivots + p, 1), :] = row[:, t * TILE:(t + 1) * TILE]
+        return carry
+
+    lax.fori_loop(0, pivots, pick, 0, unroll=4)
+    for part in range(2):
+        size = work[part].shape[0] // chunks
+        for q in range(chunks):
+            out = outs[2 * part + q // (chunks // 2)]
+            to = (q % (chunks // 2)) * size
+            at = pl.multiple_of((keys_ref[part] ^ q) * size, 8)
+            out[to:to + size, :] = work[part][pl.ds(at, size), :]
+
+
+def local_gram(snapshots, pivot_dev, pivot_row, keys, rows, chunks):
+    shapes = [jax.ShapeDtypeStruct((r // 2, TILE), F32) for r in rows for _ in range(2)]
     return pl.pallas_call(
-        functools.partial(gram_kernel, part, chunks),
-        out_shape=[jax.ShapeDtypeStruct((rows // 2, TILE), F32)] * 2,
-        in_specs=[SMEM, SMEM, SMEM, ANY],
-        out_specs=[VMEM] * 2,
-        scratch_shapes=[
-            pltpu.VMEM((here, snap), BF16),
-            pltpu.VMEM((rows, TILE), F32),
+        functools.partial(gram_kernel, chunks),
+        out_shape=shapes,
+        in_specs=[SMEM, SMEM, SMEM, HBM],
+        out_specs=[VMEM] * 4,
+        scratch_shapes=[pltpu.VMEM((r, TILE), F32) for r in rows] + [
+            pltpu.VMEM(snapshots.shape, BF16),
             pltpu.SemaphoreType.DMA((LOADS,)),
         ],
-    )(pivot_dev, pivot_row, keys, snapshots)
+        compiler_params=pltpu.CompilerParams(vmem_limit_bytes=GRANT),
+        name="local_gram",
+    )(in_hbm(pivot_dev), in_hbm(pivot_row), keys, in_hbm(snapshots))
 
 
 def eliminate(rows, at):
@@ -284,12 +319,10 @@
 
 
 def solve_kernel(
-    chunks, rows_total, keys_ref, start_ref, s_hbm, a0_ref, a1_ref, b0_ref, b1_ref,
+    chunks, rows_total, keys_ref, start_ref, s_ref, a0_ref, a1_ref, b0_ref, b1_ref,
     modes_ref, scores_ref, basis_ref, pa_ref, pb_ref, gh_ref, gl_ref, xh_ref, xl_ref,
-    yh_ref, yl_ref, z_ref, m_ref, s_ref, sem,
+    yh_ref, yl_ref, z_ref, m_ref,
 ):
-    load = pltpu.make_async_copy(s_hbm, s_ref, sem)
-    load.start()
     packed = (pa_ref, pb_ref)
     halves = ((a0_ref, a1_ref), (b0_ref, b1_ref))
     snap, rank = start_ref.shape
@@ -351,8 +384,9 @@
     coef = (dot(xh, fh, 1, 1) + (dot(xh, fl, 1, 1) + dot(xl, fh, 1, 1))).astype(BF16)
     xh_ref[...] = coef
 
+    chunk = 512
     base = spots[0][1]
-    pivots = basis_ref.shape[1]
+    pivots = basis_ref.shape[0]
     picked = jnp.concatenate(
         [pa_ref[base + t * pivots:base + (t + 1) * pivots, :] for t in range(tiles)], axis=1
     )
@@ -369,26 +403,27 @@
     done = eliminate([wide[8 * g:8 * g + 8] for g in range(pivots // 8)], 0)
     factor = lower(jnp.concatenate(done, axis=0)[:, pivots:2 * pivots]) * across
     turned = dot(factor, panel, 1, 0, HIGHEST)
-    basis_ref[...] = dot(panel, factor, 0, 1, HIGHEST)
+    basis_ref[...] = turned
     th, tl = split(turned)
+    thrice_h = jnp.concatenate([th, th, th], axis=0)
+    thrice_l = jnp.concatenate([tl, tl, tl], axis=0)
+    stacked = jnp.concatenate([th, tl, th], axis=0)
+    from_low = iota((chunk, 3 * pivots), 1) >= 2 * pivots
     ones = jnp.ones((8, rank), BF16)
-    chunk = 512
-    load.wait()
-
     def project(r, carry):
         at = pl.ds(pl.multiple_of(r * chunk, chunk), chunk)
         basis = dot(s_ref[at, :], xh_ref[...], 1, 0)
-        bh, bl = split(basis)
-        modes_ref[at, :] = bh
-        coeffs = dot(bh, th, 1, 1) + (dot(bh, tl, 1, 1) + dot(bl, th, 1, 1))
+        high = basis.astype(BF16)
+        modes_ref[at, :] = high
+        coeffs = dot(high, thrice_h, 1, 1) + dot(high, thrice_l, 1, 1)
         ch, cl = split(coeffs)
-        left = basis - (dot(ch, th, 1, 0) + (dot(ch, tl, 1, 0) + dot(cl, th, 1, 0)))
+        left = basis - dot(jnp.where(from_low, cl, ch), stacked, 1, 0)
         qh, ql = split(left * left)
         total = (dot(ones, qh, 1, 1) + dot(ones, ql, 1, 1)) * (1.0 / rank)
         scores_ref[:, at] = total[0:1, :]
         return carry
 
-    lax.fori_loop(0, s_ref.shape[0] // chunk, project, 0)
+    lax.fori_loop(0, s_ref.shape[0] // chunk, project, 0, unroll=2)
 
 
 def solve(snapshots, start, keys, pieces, pivots, rows, chunks, rows_total):
@@ -399,9 +434,9 @@
         out_shape=[
             jax.ShapeDtypeStruct((here, rank), BF16),
             jax.ShapeDtypeStruct((1, here), F32),
-            jax.ShapeDtypeStruct((rank, pivots), F32),
+            jax.ShapeDtypeStruct((pivots, rank), F32),
         ],
-        in_specs=[SMEM, VMEM, ANY] + [VMEM] * 4,
+        in_specs=[SMEM] + [VMEM] * 6,
         out_specs=[VMEM] * 3,
         scratch_shapes=[pltpu.VMEM((r, TILE), F32) for r in rows] + [
             pltpu.VMEM((snap, snap), BF16),
@@ -412,9 +447,8 @@
             pltpu.VMEM((snap, rank), BF16),
             pltpu.VMEM((snap, rank), F32),
             pltpu.VMEM((rank, rank), F32),
-            pltpu.VMEM((here, snap), BF16),
-            pltpu.SemaphoreType.DMA,
         ],
+        compiler_params=pltpu.CompilerParams(vmem_limit_bytes=GRANT),
         name="solve",
     )(keys, start, snapshots, *pieces)
 
@@ -425,31 +459,23 @@
     spots = places(snap // TILE)
     rows = [spots[0][1] + pivots * (snap // TILE), spots[1][1]]
     orders, halvings = exchange_plan(mesh_shape, rows)
-    chunks = 1 << halvings
+    chunks = chunks_of(orders[0], halvings)
     myself = lax.axis_index(("grp", "blk"))
     keys = jnp.stack([key_of(orders[0], halvings), key_of(orders[1], halvings), myself])
-    first = [order[0] for order in orders]
-    a0, a1 = local_gram(0, snapshots, pivot_dev, pivot_row, keys, rows[0], chunks)
-    got_a = send(a1, *first[0])
-    b0, b1 = local_gram(1, snapshots, pivot_dev, pivot_row, keys, rows[1], chunks)
-    got = [got_a, send(b1, *first[1])]
-    own, other = reduce_parts([a0, b0], [a1, b1], got, orders, halvings)
+    a0, a1, b0, b1 = local_gram(snapshots, pivot_dev, pivot_row, keys, rows, chunks)
+    own, other = reduce_parts([a0, b0], [a1, b1], orders, halvings)
     pieces = (own[0], other[0], own[1], other[1])
     rows_total = here * mesh_shape["grp"] * mesh_shape["blk"]
     modes, scores, basis = solve(
         snapshots, start, keys, pieces, pivots, rows, chunks, rows_total
     )
-    return modes, scores.reshape(here), basis
+    return modes, scores.reshape(here), basis.T
 
 
 def solution(mesh):
     placed = (P(("grp", "blk"), None), P(), P(), P())
-
-    def body(*args):
-        return local(dict(mesh.shape), *args)
-
     return jax.shard_map(
-        body,
+        functools.partial(local, dict(mesh.shape)),
         mesh=mesh,
         in_specs=placed,
         out_specs=(P(("grp", "blk"), None), P(("grp", "blk")), P()),

time: 136 us -> 117 us (0.86)
  Pallas kernels: 70.1 us -> 59.8 us
  local copies, waits for them, and re-layouts: 3.37 us -> 0.16 us
  waiting for transfers between devices: 35.6 us -> 33 us
  other arithmetic: 2.03 us -> 0.4 us
    pallas_call x2 -> x1, Pallas kernels: 11.6 us -> 6.14 us  [local_gram(): pl.pallas_call(functools.partial(gram_kernel, chunks), out_shape=shapes,...]
    pallas_call x1, Pallas kernels: 58.5 us -> 53.6 us  [solve(): pl.pallas_call(functools.partial(solve_kernel, chunks, rows_total), out_s...]
    unnamed x14 -> x12, local copies, waits for them, and re-layouts: 3.3 us -> 0.08 us
    ppermute x16 -> x18, waiting for transfers between devices: 35.6 us -> 33 us  [send(): return lax.ppermute(value, axis, [(i, i ^ mask) for i in range(size)])]
    ppermute x16 -> x18, starting transfers between devices: 24 us -> 22.9 us  [send(): return lax.ppermute(value, axis, [(i, i ^ mask) for i in range(size)])]
  transfers between devices with their start and end apart: 16 -> 18, of which waited for: 12 -> 15; matrix products, arithmetic and copies ran while one was open for 1% -> 0% of each run, Pallas kernels for 5% -> 0%
where the time goes in v3:
time: 117 us
  Pallas kernels  59.8 us (51%)
  waiting for transfers between devices  33 us (28%)
  starting transfers between devices  22.9 us (20%)
    pallas_call x1, Pallas kernels, solve(): pl.pallas_call(functools.partial(solve_kernel, chunks, rows_total), out_s...  53.6 us
    ppermute x18, waiting for transfers between devices, send(): return lax.ppermute(value, axis, [(i, i ^ mask) for i in range(size)])  33 us
    ppermute x18, starting transfers between devices, send(): return lax.ppermute(value, axis, [(i, i ^ mask) for i in range(size)])  22.9 us
    pallas_call x1, Pallas kernels, local_gram(): pl.pallas_call(functools.partial(gram_kernel, chunks), out_shape=shapes,...  6.14 us
  transfers between devices with their start and end apart: 18, of which 15 were waited for; matrix products, arithmetic and copies ran while one was open for 0% of the time, Pallas kernels for 0%

profile of v3, /device:TPU:0, one launch (start us, length us, event | category | flops | bytes accessed | tf_op | source)
XLA Modules:
  0.0 117.1 jit_solution(1782380493143127317)
XLA Ops:
  0.7 0.1 pad_add_fusion.keys_ref
  0.7 6.1 %local_gram.1 = (f32[1280,128]{1,0:T(8,128)S(1)}, f32[1280,128]{1,0:T(8,128)S(1)}, f32[1152,128]{1,0:T(8,128)S(1)}, f32[1152,128]{1,0:T(8,128)S(1)}) custom-call(s32[32]{0:T(128)} %dev_ref.1, s32[32]{0:T(128)} %row_ref.1, s32[3]{0:T(128)S(1)} %pad_add_fusion.keys_ref, bf16[2048,1024]{1,0:T(8,128)(2,1)} %s_ref.1), custom_call_target="tpu_custom_call" | custom-call | tf_op jit(solution)/shard_map/local_gram/pallas_call | solution.py:199
  6.9 0.6 collective-permute-start.3
  7.4 0.1 collective-permute-start
  7.5 1.6 %collective-permute-done.3 = f32[1152,128]{1,0:T(8,128)S(1)} collective-permute-done((f32[1152,128]{1,0:T(8,128)S(1)}, f32[1152,128]{1,0:T(8,128)S(1)}, u32[]{:S(2)}, u32[]{:S(2)}) %collective-permute-start.3) | collective-permute-done | bytes 589856 | tf_op jit(solution)/shard_map/ppermute | solution.py:96
  9.1 0.1 slice_add_fusion.3
  9.1 3.0 %collective-permute-start.4 = (f32[576,128]{1,0:T(8,128)S(1)}, f32[576,128]{1,0:T(8,128)S(1)}, u32[]{:S(2)}, u32[]{:S(2)}) collective-permute-start(f32[576,128]{1,0:T(8,128)S(1)} %get-tuple-element.24), channel_id=1, source_target_pairs={{0,2},{1,3},{2,0},{3,1},{4,6},{5,7},{6,4},{7,5},{8,10},{9,11},{10,... | collective-permute-start | bytes 884744 | tf_op jit(solution)/shard_map/ppermute | solution.py:96
  12.1 0.0 collective-permute-done
  12.1 0.1 slice_add_fusion.1
  12.2 0.0 copy-start
  12.2 0.0 copy-start.1
  12.2 1.5 %collective-permute-start.1 = (f32[640,128]{1,0:T(8,128)S(1)}, f32[640,128]{1,0:T(8,128)S(1)}, u32[]{:S(2)}, u32[]{:S(2)}) collective-permute-start(f32[640,128]{1,0:T(8,128)S(1)} %get-tuple-element.22), channel_id=1, source_target_pairs={{0,4},{4,0},{8,12},{12,8},{16,20},{20,16},{24,28},{28,24},{1,5},{5... | collective-permute-start | bytes 983048 | tf_op jit(solution)/shard_map/ppermute | solution.py:96
  13.7 5.7 %collective-permute-done.4 = f32[576,128]{1,0:T(8,128)S(1)} collective-permute-done((f32[576,128]{1,0:T(8,128)S(1)}, f32[576,128]{1,0:T(8,128)S(1)}, u32[]{:S(2)}, u32[]{:S(2)}) %collective-permute-start.4) | collective-permute-done | bytes 294944 | tf_op jit(solution)/shard_map/ppermute | solution.py:96
  19.4 1.8 %collective-permute-start.5 = (f32[288,128]{1,0:T(8,128)S(1)}, f32[288,128]{1,0:T(8,128)S(1)}, u32[]{:S(2)}, u32[]{:S(2)}) collective-permute-start(f32[288,128]{1,0:T(8,128)S(1)} %get-tuple-element.28), channel_id=1, source_target_pairs={{0,4},{4,0},{8,12},{12,8},{16,20},{20,16},{24,28},{28,24},{1,5},{5... | collective-permute-start | bytes 442376 | tf_op jit(solution)/shard_map/ppermute | solution.py:96
  21.2 0.6 collective-permute-done.1
  21.8 1.1 collective-permute-start.2
  22.9 2.0 %collective-permute-done.5 = f32[288,128]{1,0:T(8,128)S(1)} collective-permute-done((f32[288,128]{1,0:T(8,128)S(1)}, f32[288,128]{1,0:T(8,128)S(1)}, u32[]{:S(2)}, u32[]{:S(2)}) %collective-permute-start.5) | collective-permute-done | bytes 147488 | tf_op jit(solution)/shard_map/ppermute | solution.py:96
  24.9 2.3 %collective-permute-done.2 = f32[320,128]{1,0:T(8,128)S(1)} collective-permute-done((f32[320,128]{1,0:T(8,128)S(1)}, f32[320,128]{1,0:T(8,128)S(1)}, u32[]{:S(2)}, u32[]{:S(2)}) %collective-permute-start.2) | collective-permute-done | bytes 163872 | tf_op jit(solution)/shard_map/ppermute | solution.py:96
  27.3 1.7 %collective-permute-start.7 = (f32[152,128]{1,0:T(8,128)S(1)}, f32[152,128]{1,0:T(8,128)S(1)}, u32[]{:S(2)}, u32[]{:S(2)}) collective-permute-start(f32[152,128]{1,0:T(8,128)S(1)} %pad_maximum_fusion.3), channel_id=1, source_target_pairs={{0,8},{4,12},{8,0},{12,4},{16,24},{20,28},{24,16},{28,20},{1,9},{5... | collective-permute-start | bytes 233480 | tf_op jit(solution)/shard_map/ppermute | solution.py:96
  28.9 2.5 %collective-permute-start.8 = (f32[152,128]{1,0:T(8,128)S(1)}, f32[152,128]{1,0:T(8,128)S(1)}, u32[]{:S(2)}, u32[]{:S(2)}) collective-permute-start(f32[152,128]{1,0:T(8,128)S(1)} %pad_maximum_fusion.4), channel_id=1, source_target_pairs={{0,24},{4,28},{8,16},{12,20},{16,8},{20,12},{24,0},{28,4},{1,25},{... | collective-permute-start | bytes 233480 | tf_op jit(solution)/shard_map/ppermute | solution.py:96
  31.5 0.2 collective-permute-start.6
  31.6 1.0 collective-permute-done.7
  32.7 2.6 %collective-permute-done.8 = f32[152,128]{1,0:T(8,128)S(1)} collective-permute-done((f32[152,128]{1,0:T(8,128)S(1)}, f32[152,128]{1,0:T(8,128)S(1)}, u32[]{:S(2)}, u32[]{:S(2)}) %collective-permute-start.8) | collective-permute-done | bytes 77856 | tf_op jit(solution)/shard_map/ppermute | solution.py:96
  35.2 2.9 %collective-permute-done.6 = f32[152,128]{1,0:T(8,128)S(1)} collective-permute-done((f32[152,128]{1,0:T(8,128)S(1)}, f32[152,128]{1,0:T(8,128)S(1)}, u32[]{:S(2)}, u32[]{:S(2)}) %collective-permute-start.6) | collective-permute-done | bytes 77856 | tf_op jit(solution)/shard_map/ppermute | solution.py:96
  38.2 2.0 %collective-permute-start.11 = (f32[152,128]{1,0:T(8,128)S(1)}, f32[152,128]{1,0:T(8,128)S(1)}, u32[]{:S(2)}, u32[]{:S(2)}) collective-permute-start(f32[152,128]{1,0:T(8,128)S(1)} %pad_maximum_fusion.5), channel_id=1, source_target_pairs={{0,24},{4,28},{8,16},{12,20},{16,8},{20,12},{24,0},{28,4},{1,25},{... | collective-permute-start | bytes 233480 | tf_op jit(solution)/shard_map/ppermute | solution.py:96
  40.2 0.0 collective-permute-start.10
  40.2 2.5 %collective-permute-start.9 = (f32[152,128]{1,0:T(8,128)S(1)}, f32[152,128]{1,0:T(8,128)S(1)}, u32[]{:S(2)}, u32[]{:S(2)}) collective-permute-start(f32[152,128]{1,0:T(8,128)S(1)} %pad_maximum_fusion.5), channel_id=1, source_target_pairs={{0,16},{4,20},{8,24},{12,28},{16,0},{20,4},{24,8},{28,12},{1,17},{... | collective-permute-start | bytes 233480 | tf_op jit(solution)/shard_map/ppermute | solution.py:96
  42.7 2.8 %collective-permute-done.9 = f32[152,128]{1,0:T(8,128)S(1)} collective-permute-done((f32[152,128]{1,0:T(8,128)S(1)}, f32[152,128]{1,0:T(8,128)S(1)}, u32[]{:S(2)}, u32[]{:S(2)}) %collective-permute-start.9) | collective-permute-done | bytes 77856 | tf_op jit(solution)/shard_map/ppermute | solution.py:96
  45.5 0.6 collective-permute-done.10
  46.2 0.0 collective-permute-done.11
  46.2 1.5 %collective-permute-start.12 = (f32[320,128]{1,0:T(8,128)S(1)}, f32[320,128]{1,0:T(8,128)S(1)}, u32[]{:S(2)}, u32[]{:S(2)}) collective-permute-start(f32[320,128]{1,0:T(8,128)S(1)} %pad_maximum_fusion), channel_id=1, source_target_pairs={{0,2},{1,3},{2,0},{3,1},{4,6},{5,7},{6,4},{7,5},{8,10},{9,11},{10,... | collective-permute-start | bytes 491528 | tf_op jit(solution)/shard_map/ppermute | solution.py:96
  47.8 1.6 %collective-permute-start.15 = (f32[288,128]{1,0:T(8,128)S(1)}, f32[288,128]{1,0:T(8,128)S(1)}, u32[]{:S(2)}, u32[]{:S(2)}) collective-permute-start(f32[288,128]{1,0:T(8,128)S(1)} %pad_maximum_fusion.1), channel_id=1, source_target_pairs={{0,4},{4,0},{8,12},{12,8},{16,20},{20,16},{24,28},{28,24},{1,5},{5... | collective-permute-start | bytes 442376 | tf_op jit(solution)/shard_map/ppermute | solution.py:96
  49.3 2.8 %collective-permute-done.12 = f32[320,128]{1,0:T(8,128)S(1)} collective-permute-done((f32[320,128]{1,0:T(8,128)S(1)}, f32[320,128]{1,0:T(8,128)S(1)}, u32[]{:S(2)}, u32[]{:S(2)}) %collective-permute-start.12) | collective-permute-done | bytes 163872 | tf_op jit(solution)/shard_map/ppermute | solution.py:96
  52.2 1.5 %collective-permute-start.13 = (f32[640,128]{1,0:T(8,128)S(1)}, f32[640,128]{1,0:T(8,128)S(1)}, u32[]{:S(2)}, u32[]{:S(2)}) collective-permute-start(f32[640,128]{1,0:T(8,128)S(1)} %get-tuple-element.35), channel_id=1, source_target_pairs={{0,4},{4,0},{8,12},{12,8},{16,20},{20,16},{24,28},{28,24},{1,5},{5... | collective-permute-start | bytes 983048 | tf_op jit(solution)/shard_map/ppermute | solution.py:96
  53.7 0.8 collective-permute-done.15
  54.6 1.4 %collective-permute-start.16 = (f32[576,128]{1,0:T(8,128)S(1)}, f32[576,128]{1,0:T(8,128)S(1)}, u32[]{:S(2)}, u32[]{:S(2)}) collective-permute-start(f32[576,128]{1,0:T(8,128)S(1)} %get-tuple-element.37), channel_id=1, source_target_pairs={{0,2},{1,3},{2,0},{3,1},{4,6},{5,7},{6,4},{7,5},{8,10},{9,11},{10,... | collective-permute-start | bytes 884744 | tf_op jit(solution)/shard_map/ppermute | solution.py:96
  56.0 3.3 %collective-permute-done.13 = f32[640,128]{1,0:T(8,128)S(1)} collective-permute-done((f32[640,128]{1,0:T(8,128)S(1)}, f32[640,128]{1,0:T(8,128)S(1)}, u32[]{:S(2)}, u32[]{:S(2)}) %collective-permute-start.13) | collective-permute-done | bytes 327712 | tf_op jit(solution)/shard_map/ppermute | solution.py:96
  59.3 0.1 collective-permute-start.14
  59.4 2.0 %collective-permute-done.16 = f32[576,128]{1,0:T(8,128)S(1)} collective-permute-done((f32[576,128]{1,0:T(8,128)S(1)}, f32[576,128]{1,0:T(8,128)S(1)}, u32[]{:S(2)}, u32[]{:S(2)}) %collective-permute-start.16) | collective-permute-done | bytes 294944 | tf_op jit(solution)/shard_map/ppermute | solution.py:96
  61.4 0.1 collective-permute-start.17
  61.5 2.0 %collective-permute-done.17.b1_ref = f32[1152,128]{1,0:T(8,128)S(1)} collective-permute-done((f32[1152,128]{1,0:T(8,128)S(1)}, f32[1152,128]{1,0:T(8,128)S(1)}, u32[]{:S(2)}, u32[]{:S(2)}) %collective-permute-start.17) | collective-permute-done | bytes 589856 | tf_op jit(solution)/shard_map/ppermute | solution.py:96
  63.5 0.0 collective-permute-done.14.a1_ref
  63.5 0.0 copy-done
  63.5 0.0 copy-done.1
  63.5 53.6 %solve.1 = (bf16[2048,256]{1,0:T(8,128)(2,1)}, f32[1,2048]{1,0:T(1,128)}, f32[32,256]{1,0:T(8,128)}) custom-call(s32[3]{0:T(128)S(1)} %pad_add_fusion.keys_ref, f32[1024,256]{1,0:T(8,128)S(1)} %copy-done.1, bf16[2048,1024]{1,0:T(8,128)(2,1)S(1)} %copy-done, f32[1280,128]{1,0:T(8,128)S(1)} %constant_dynamic-update-slice_fusion.5.a0_ref, ...), custom_call_target="tpu_custom_call" | custom-call | tf_op jit(solution)/shard_map/solve/pallas_call | solution.py:432
  (24 shorter events, 0.3 us)
Async XLA Ops:
  6.9 2.2 %collective-permute-start.3 = (f32[1152,128]{1,0:T(8,128)S(1)}, f32[1152,128]{1,0:T(8,128)S(1)}, u32[]{:S(2)}, u32[]{:S(2)}) collective-permute-start(f32[1152,128]{1,0:T(8,128)S(1)} %get-tuple-element.13), channel_id=1, source_target_pairs={{0,1},{1,0},{2,3},{3,2},{4,5},{5,4},{6,7},{7,6},{8,9},{9,8},{10,11... | collective-permute-start | bytes 1769480 | tf_op jit(solution)/shard_map/ppermute | solution.py:96
  7.4 4.7 %collective-permute-start = (f32[1280,128]{1,0:T(8,128)S(1)}, f32[1280,128]{1,0:T(8,128)S(1)}, u32[]{:S(2)}, u32[]{:S(2)}) collective-permute-start(f32[1280,128]{1,0:T(8,128)S(1)} %get-tuple-element.11), channel_id=1, source_target_pairs={{0,1},{1,0},{2,3},{3,2},{4,5},{5,4},{6,7},{7,6},{8,9},{9,8},{10,11... | collective-permute-start | bytes 1966088 | tf_op jit(solution)/shard_map/ppermute | solution.py:96
  9.1 10.3 %collective-permute-start.4 = (f32[576,128]{1,0:T(8,128)S(1)}, f32[576,128]{1,0:T(8,128)S(1)}, u32[]{:S(2)}, u32[]{:S(2)}) collective-permute-start(f32[576,128]{1,0:T(8,128)S(1)} %get-tuple-element.24), channel_id=1, source_target_pairs={{0,2},{1,3},{2,0},{3,1},{4,6},{5,7},{6,4},{7,5},{8,10},{9,11},{10,... | collective-permute-start | bytes 884744 | tf_op jit(solution)/shard_map/ppermute | solution.py:96
  12.2 51.3 %copy-start = (bf16[2048,1024]{1,0:T(8,128)(2,1)S(1)}, bf16[2048,1024]{1,0:T(8,128)(2,1)}, u32[]{:S(2)}) copy-start(bf16[2048,1024]{1,0:T(8,128)(2,1)} %s_ref.1) | copy-start | bytes 12582916
  12.2 51.3 %copy-start.1 = (f32[1024,256]{1,0:T(8,128)S(1)}, f32[1024,256]{1,0:T(8,128)}, u32[]{:S(2)}) copy-start(f32[1024,256]{1,0:T(8,128)} %start_ref.1) | copy-start | bytes 3145732
  12.2 9.6 %collective-permute-start.1 = (f32[640,128]{1,0:T(8,128)S(1)}, f32[640,128]{1,0:T(8,128)S(1)}, u32[]{:S(2)}, u32[]{:S(2)}) collective-permute-start(f32[640,128]{1,0:T(8,128)S(1)} %get-tuple-element.22), channel_id=1, source_target_pairs={{0,4},{4,0},{8,12},{12,8},{16,20},{20,16},{24,28},{28,24},{1,5},{5... | collective-permute-start | bytes 983048 | tf_op jit(solution)/shard_map/ppermute | solution.py:96
  19.4 5.4 %collective-permute-start.5 = (f32[288,128]{1,0:T(8,128)S(1)}, f32[288,128]{1,0:T(8,128)S(1)}, u32[]{:S(2)}, u32[]{:S(2)}) collective-permute-start(f32[288,128]{1,0:T(8,128)S(1)} %get-tuple-element.28), channel_id=1, source_target_pairs={{0,4},{4,0},{8,12},{12,8},{16,20},{20,16},{24,28},{28,24},{1,5},{5... | collective-permute-start | bytes 442376 | tf_op jit(solution)/shard_map/ppermute | solution.py:96
  21.8 5.4 %collective-permute-start.2 = (f32[320,128]{1,0:T(8,128)S(1)}, f32[320,128]{1,0:T(8,128)S(1)}, u32[]{:S(2)}, u32[]{:S(2)}) collective-permute-start(f32[320,128]{1,0:T(8,128)S(1)} %get-tuple-element.26), channel_id=1, source_target_pairs={{0,2},{1,3},{2,0},{3,1},{4,6},{5,7},{6,4},{7,5},{8,10},{9,11},{10,... | collective-permute-start | bytes 491528 | tf_op jit(solution)/shard_map/ppermute | solution.py:96
  27.3 5.4 %collective-permute-start.7 = (f32[152,128]{1,0:T(8,128)S(1)}, f32[152,128]{1,0:T(8,128)S(1)}, u32[]{:S(2)}, u32[]{:S(2)}) collective-permute-start(f32[152,128]{1,0:T(8,128)S(1)} %pad_maximum_fusion.3), channel_id=1, source_target_pairs={{0,8},{4,12},{8,0},{12,4},{16,24},{20,28},{24,16},{28,20},{1,9},{5... | collective-permute-start | bytes 233480 | tf_op jit(solution)/shard_map/ppermute | solution.py:96
  28.9 6.3 %collective-permute-start.8 = (f32[152,128]{1,0:T(8,128)S(1)}, f32[152,128]{1,0:T(8,128)S(1)}, u32[]{:S(2)}, u32[]{:S(2)}) collective-permute-start(f32[152,128]{1,0:T(8,128)S(1)} %pad_maximum_fusion.4), channel_id=1, source_target_pairs={{0,24},{4,28},{8,16},{12,20},{16,8},{20,12},{24,0},{28,4},{1,25},{... | collective-permute-start | bytes 233480 | tf_op jit(solution)/shard_map/ppermute | solution.py:96
  31.5 6.7 %collective-permute-start.6 = (f32[152,128]{1,0:T(8,128)S(1)}, f32[152,128]{1,0:T(8,128)S(1)}, u32[]{:S(2)}, u32[]{:S(2)}) collective-permute-start(f32[152,128]{1,0:T(8,128)S(1)} %pad_maximum_fusion.2), channel_id=1, source_target_pairs={{0,16},{4,20},{8,24},{12,28},{16,0},{20,4},{24,8},{28,12},{1,17},{... | collective-permute-start | bytes 233480 | tf_op jit(solution)/shard_map/ppermute | solution.py:96
  38.2 7.9 %collective-permute-start.11 = (f32[152,128]{1,0:T(8,128)S(1)}, f32[152,128]{1,0:T(8,128)S(1)}, u32[]{:S(2)}, u32[]{:S(2)}) collective-permute-start(f32[152,128]{1,0:T(8,128)S(1)} %pad_maximum_fusion.5), channel_id=1, source_target_pairs={{0,24},{4,28},{8,16},{12,20},{16,8},{20,12},{24,0},{28,4},{1,25},{... | collective-permute-start | bytes 233480 | tf_op jit(solution)/shard_map/ppermute | solution.py:96
  40.2 5.9 %collective-permute-start.10 = (f32[152,128]{1,0:T(8,128)S(1)}, f32[152,128]{1,0:T(8,128)S(1)}, u32[]{:S(2)}, u32[]{:S(2)}) collective-permute-start(f32[152,128]{1,0:T(8,128)S(1)} %pad_maximum_fusion.5), channel_id=1, source_target_pairs={{0,8},{4,12},{8,0},{12,4},{16,24},{20,28},{24,16},{28,20},{1,9},{5... | collective-permute-start | bytes 233480 | tf_op jit(solution)/shard_map/ppermute | solution.py:96
  40.2 5.3 %collective-permute-start.9 = (f32[152,128]{1,0:T(8,128)S(1)}, f32[152,128]{1,0:T(8,128)S(1)}, u32[]{:S(2)}, u32[]{:S(2)}) collective-permute-start(f32[152,128]{1,0:T(8,128)S(1)} %pad_maximum_fusion.5), channel_id=1, source_target_pairs={{0,16},{4,20},{8,24},{12,28},{16,0},{20,4},{24,8},{28,12},{1,17},{... | collective-permute-start | bytes 233480 | tf_op jit(solution)/shard_map/ppermute | solution.py:96
  46.2 5.9 %collective-permute-start.12 = (f32[320,128]{1,0:T(8,128)S(1)}, f32[320,128]{1,0:T(8,128)S(1)}, u32[]{:S(2)}, u32[]{:S(2)}) collective-permute-start(f32[320,128]{1,0:T(8,128)S(1)} %pad_maximum_fusion), channel_id=1, source_target_pairs={{0,2},{1,3},{2,0},{3,1},{4,6},{5,7},{6,4},{7,5},{8,10},{9,11},{10,... | collective-permute-start | bytes 491528 | tf_op jit(solution)/shard_map/ppermute | solution.py:96
  47.8 6.8 %collective-permute-start.15 = (f32[288,128]{1,0:T(8,128)S(1)}, f32[288,128]{1,0:T(8,128)S(1)}, u32[]{:S(2)}, u32[]{:S(2)}) collective-permute-start(f32[288,128]{1,0:T(8,128)S(1)} %pad_maximum_fusion.1), channel_id=1, source_target_pairs={{0,4},{4,0},{8,12},{12,8},{16,20},{20,16},{24,28},{28,24},{1,5},{5... | collective-permute-start | bytes 442376 | tf_op jit(solution)/shard_map/ppermute | solution.py:96
  52.2 7.1 %collective-permute-start.13 = (f32[640,128]{1,0:T(8,128)S(1)}, f32[640,128]{1,0:T(8,128)S(1)}, u32[]{:S(2)}, u32[]{:S(2)}) collective-permute-start(f32[640,128]{1,0:T(8,128)S(1)} %get-tuple-element.35), channel_id=1, source_target_pairs={{0,4},{4,0},{8,12},{12,8},{16,20},{20,16},{24,28},{28,24},{1,5},{5... | collective-permute-start | bytes 983048 | tf_op jit(solution)/shard_map/ppermute | solution.py:96
  54.6 6.8 %collective-permute-start.16 = (f32[576,128]{1,0:T(8,128)S(1)}, f32[576,128]{1,0:T(8,128)S(1)}, u32[]{:S(2)}, u32[]{:S(2)}) collective-permute-start(f32[576,128]{1,0:T(8,128)S(1)} %get-tuple-element.37), channel_id=1, source_target_pairs={{0,2},{1,3},{2,0},{3,1},{4,6},{5,7},{6,4},{7,5},{8,10},{9,11},{10,... | collective-permute-start | bytes 884744 | tf_op jit(solution)/shard_map/ppermute | solution.py:96
  59.3 4.1 %collective-permute-start.14 = (f32[1280,128]{1,0:T(8,128)S(1)}, f32[1280,128]{1,0:T(8,128)S(1)}, u32[]{:S(2)}, u32[]{:S(2)}) collective-permute-start(f32[1280,128]{1,0:T(8,128)S(1)} %constant_dynamic-update-slice_fusion.5.a0_ref), channel_id=1, source_target_pairs={{0,1},{1,0},{2,3},{3,2},{4,5},{5,4},{6,7},{7,6},{8,9},{9,8},{10,11... | collective-permute-start | bytes 1966088 | tf_op jit(solution)/shard_map/ppermute | solution.py:96
  61.4 2.1 %collective-permute-start.17 = (f32[1152,128]{1,0:T(8,128)S(1)}, f32[1152,128]{1,0:T(8,128)S(1)}, u32[]{:S(2)}, u32[]{:S(2)}) collective-permute-start(f32[1152,128]{1,0:T(8,128)S(1)} %constant_dynamic-update-slice_fusion.16.b0_ref), channel_id=1, source_target_pairs={{0,1},{1,0},{2,3},{3,2},{4,5},{5,4},{6,7},{7,6},{8,9},{9,8},{10,11... | collective-permute-start | bytes 1769480 | tf_op jit(solution)/shard_map/ppermute | solution.py:96

commit v4 on v3

--- a/solution.py
+++ b/solution.py
@@ -225,40 +225,48 @@
     count = len(rows)
     for g in range(count):
         here = rows[g]
+        e = [subl(here, i) for i in range(8)]
         cols = [lane(here, at + 8 * g + j) * one for j in range(8)]
         p = [[subl(cols[j], i) if j >= i else None for j in range(8)] for i in range(8)]
-        e = [subl(here, i) for i in range(8)]
         c = {h: [lane(rows[h], at + 8 * g + j) for j in range(8)] for h in range(g + 1, count)}
-        scale = []
+        scale = [None] * 8
         u = [[None] * 8 for _ in range(8)]
-        for j in range(8):
-            inverse = 1.0 / p[j][j]
-            scale.append(inverse)
-            for i in range(j + 1, 8):
-                u[j][i] = p[j][i] * inverse
-            for i in range(j + 1, 8):
+        for j in range(0, 8, 2):
+            k = j + 1
+            a, b, d = p[j][j], p[j][k], p[k][k]
+            idet = 1.0 / (a * d - b * b)
+            ia = 1.0 / a
+            scale[j], scale[k] = ia, a * idet
+            u[j][k] = b * ia
+            e[k] = e[k] - u[j][k] * e[j]
+            y0, y1, x0 = {}, {}, {}
+            for i in range(j + 2, 8):
+                y0[i] = d * p[j][i] - b * p[k][i]
+                y1[i] = a * p[k][i] - b * p[j][i]
+                u[j][i] = p[j][i] * ia
+                u[k][i] = y1[i] * idet
+                x0[i] = y0[i] * idet
+            for i in range(j + 2, 8):
                 for m in range(i, 8):
-                    if i == j + 1 and m <= j + 2:
-                        p[i][m] = p[i][m] - (p[j][i] * p[j][m]) * inverse
+                    if m <= j + 3:
+                        p[i][m] = p[i][m] - (y0[i] * p[j][m] + y1[i] * p[k][m]) * idet
                     else:
-                        p[i][m] = p[i][m] - u[j][i] * p[j][m]
-                e[i] = e[i] - u[j][i] * e[j]
+                        p[i][m] = p[i][m] - x0[i] * p[j][m] - u[k][i] * p[k][m]
+                e[i] = e[i] - u[j][i] * e[j] - u[k][i] * e[k]
             if g + 1 < count:
                 near = c[g + 1]
-                x = near[j] * inverse
-                rows[g + 1] = rows[g + 1] - x * e[j]
-                for m in range(j + 1, 8):
-                    near[m] = near[m] - x * p[j][m]
+                z0 = (d * near[j] - b * near[k]) * idet
+                z1 = (a * near[k] - b * near[j]) * idet
+                rows[g + 1] = rows[g + 1] - (near[j] * ia) * e[j] - z1 * e[k]
+                for m in range(j + 2, 8):
+                    near[m] = near[m] - z0 * p[j][m] - z1 * p[k][m]
         if g + 2 < count:
             t = [e[i] * scale[i] for i in range(8)]
             for i in range(7, 0, -1):
                 for m in range(i):
                     t[m] = t[m] - u[m][i] * t[i]
             for h in range(g + 2, count):
-                terms = [c[h][j] * t[j] for j in range(8)]
-                while len(terms) > 1:
-                    terms = [terms[q] + terms[q + 1] for q in range(0, len(terms), 2)]
-                rows[h] = rows[h] - terms[0]
+                rows[h] = rows[h] - add_up([c[h][j] * t[j] for j in range(8)])
         out, factor = e[0], scale[0]
         for i in range(1, 8):
             out = jnp.where(sub == i, e[i], out)
@@ -269,6 +277,14 @@
 
 def lower(value):
     return jnp.where(iota(value.shape, 1) <= iota(value.shape, 0), value, 0.0)
+
+
+def product3(a, b, ca, cb):
+    return dot(a[0], b[0], ca, cb) + (dot(a[0], b[1], ca, cb) + dot(a[1], b[0], ca, cb))
+
+
+def twice(value):
+    return tuple(jnp.concatenate([v, v], axis=0) for v in split(value))
 
 
 def invert_factor(m_ref, beside=None):
@@ -278,50 +294,54 @@
     block = m_ref[:b, :TILE]
     for k in range(n // b):
         first = k * b
-        at = first % TILE
+        tile = first // TILE * TILE
+        at = first - tile
         other = b - at
         inside = (near >= at) & (near < at + b)
         eye = jnp.where(near - other == down, 1.0, 0.0)
         block = jnp.where(inside, block, eye)
         if beside is not None:
             beside(k)
-        done = eliminate([block[8 * g:8 * g + 8] for g in range(b // 8)], at)
-        inverse = lower(jnp.concatenate(done, axis=0)[:, other:other + b])
+        done = jnp.concatenate(
+            eliminate([block[8 * g:8 * g + 8] for g in range(b // 8)], at), axis=0
+        )
+        inverse = split(jnp.where((near >= other) & (near - other <= down), done, 0.0))
         mine = (lanes >= first) & (lanes < first + b)
-        unit = jnp.where(lanes - first == subs, 1.0, 0.0)
-        wh, wl = split(inverse)
-        rh, rl = split(jnp.where(mine, unit, m_ref[first:first + b, :]))
-        row = dot(wh, rh, 1, 0) + (dot(wh, rl, 1, 0) + dot(wl, rh, 1, 0))
-        m_ref[first:first + b, :] = row
+        right = m_ref[first:first + b, :]
         q = first + b
         if q < n:
-            uh, ul = split(row)
-            left = jnp.concatenate([uh, uh, ul], axis=0)
-            right = jnp.concatenate([uh, ul, uh], axis=0)
-            tile = q // TILE * TILE
-            block = m_ref[q:q + b, tile:tile + TILE] - dot(
-                left[:, q:q + b], right[:, tile:tile + TILE], 0, 0)
-            update = dot(left, right, 0, 0)
-            for q in range(first + b, n, b):
-                m_ref[q:q + b, :] = (
-                    jnp.where(mine, 0.0, m_ref[q:q + b, :]) - update[q:q + b, :]
+            to = q // TILE * TILE
+            across = product3(inverse, twice(right[:, to:to + TILE]), 1, 0)
+            below = split(pltpu.roll(m_ref[q:q + b, tile:tile + TILE], b, 1))
+            below = product3(below, inverse, 1, 1)
+            block = m_ref[q:q + b, to:to + TILE] - product3(split(below), split(across), 1, 0)
+        unit = jnp.where(lanes - first == subs, 1.0, 0.0)
+        row = product3(inverse, twice(jnp.where(mine, unit, right)), 1, 0)
+        m_ref[first:first + b, :] = row
+        if q < n:
+            high, low = split(row)
+            update = dot(
+                jnp.concatenate([high, high, low], axis=0),
+                jnp.concatenate([high, low, high], axis=0), 0, 0)
+            for r in range(q, n, b):
+                m_ref[r:r + b, :] = (
+                    jnp.where(mine, 0.0, m_ref[r:r + b, :]) - update[r:r + b, :]
                 )
 
 
-def inverse_factor(matrix, m_ref, beside=None):
+def scale_to_unit(matrix, m_ref, across_ref):
     n = matrix.shape[0]
     diagonal = jnp.where(iota((n, n), 0) == iota((n, n), 1), matrix, 0.0)
     down = lax.rsqrt(jnp.sum(diagonal, axis=1, keepdims=True))
     across = lax.rsqrt(jnp.sum(diagonal, axis=0, keepdims=True))
     m_ref[...] = matrix * down * across
-    invert_factor(m_ref, beside)
-    return lower(m_ref[...]) * across
+    across_ref[...] = across
 
 
 def solve_kernel(
     chunks, rows_total, keys_ref, start_ref, s_ref, a0_ref, a1_ref, b0_ref, b1_ref,
-    modes_ref, scores_ref, basis_ref, pa_ref, pb_ref, gh_ref, gl_ref, xh_ref, xl_ref,
-    yh_ref, yl_ref, z_ref, m_ref,
+    modes_hbm, scores_ref, basis_ref, pa_ref, pb_ref, gh_ref, gl_ref, xh_ref, xl_ref,
+    yh_ref, yl_ref, z_ref, m_ref, across_ref, factor_ref, rows_ref, high_ref, sem,
 ):
     packed = (pa_ref, pb_ref)
     halves = ((a0_ref, a1_ref), (b0_ref, b1_ref))
@@ -356,35 +376,53 @@
     for r in range(strips):
         at = pl.ds(r * step, step)
         z_ref[at, :] = product(at, yh_ref[...], yl_ref[...])
-    yh_ref[...], yl_ref[...] = split(z_ref[...])
+    square = 0.0
+    for r in range(strips):
+        at = pl.ds(r * step, step)
+        yh, yl = split(z_ref[at, :])
+        yh_ref[at, :], yl_ref[at, :] = yh, yl
+        square = square + dot(yh, yh, 0, 0)
+    scale_to_unit(square, m_ref, across_ref)
 
     def iteration(number, carry):
         def beside(k):
             at = pl.ds(k * step, step)
             z_ref[at, :] = product(at, yh_ref[...], yl_ref[...])
 
-        yh = yh_ref[...]
-        factor = inverse_factor(dot(yh, yh, 0, 0), m_ref, beside).astype(BF16)
+        invert_factor(m_ref, beside)
+        factor_ref[...] = (lower(m_ref[...]) * across_ref[...]).astype(BF16)
 
         @pl.when(number == ITERS - 1)
         def _():
+            factor = factor_ref[...]
             iterate = dot(yh_ref[...], factor, 1, 1) + dot(yl_ref[...], factor, 1, 1)
             xh_ref[...], xl_ref[...] = split(iterate)
 
-        zh, zl = split(z_ref[...])
-        yh_ref[...], yl_ref[...] = split(dot(zh, factor, 1, 1) + dot(zl, factor, 1, 1))
+        factor = factor_ref[...]
+        square = 0.0
+        for r in range(strips):
+            at = pl.ds(r * step, step)
+            zh, zl = split(z_ref[at, :])
+            yh, yl = split(dot(zh, factor, 1, 1) + dot(zl, factor, 1, 1))
+            yh_ref[at, :], yl_ref[at, :] = yh, yl
+            square = square + dot(yh, yh, 0, 0)
+        scale_to_unit(square, m_ref, across_ref)
         return carry
 
     lax.fori_loop(0, ITERS, iteration, 0)
     yh, yl = yh_ref[...], yl_ref[...]
     xh, xl = xh_ref[...], xl_ref[...]
     small = dot(xh, yh, 0, 0) + (dot(xh, yl, 0, 0) + dot(xl, yh, 0, 0))
-    small = (small + jnp.transpose(small)) * (0.5 / rows_total)
-    fh, fl = split(inverse_factor(small, m_ref))
+    scale_to_unit((small + jnp.transpose(small)) * (0.5 / rows_total), m_ref, across_ref)
+    invert_factor(m_ref)
+    fh, fl = split(lower(m_ref[...]) * across_ref[...])
     coef = (dot(xh, fh, 1, 1) + (dot(xh, fl, 1, 1) + dot(xl, fh, 1, 1))).astype(BF16)
-    xh_ref[...] = coef
-
     chunk = 512
+    spans = [pl.ds(r * chunk, chunk) for r in range(s_ref.shape[0] // chunk)]
+    for at in spans:
+        basis = dot(s_ref[at, :], coef, 1, 0)
+        rows_ref[at, :] = basis
+        high_ref[at, :] = basis.astype(BF16)
     base = spots[0][1]
     pivots = basis_ref.shape[0]
     picked = jnp.concatenate(
@@ -410,11 +448,12 @@
     stacked = jnp.concatenate([th, tl, th], axis=0)
     from_low = iota((chunk, 3 * pivots), 1) >= 2 * pivots
     ones = jnp.ones((8, rank), BF16)
+    store = pltpu.make_async_copy(high_ref, modes_hbm, sem)
+    store.start()
+
     def project(r, carry):
         at = pl.ds(pl.multiple_of(r * chunk, chunk), chunk)
-        basis = dot(s_ref[at, :], xh_ref[...], 1, 0)
-        high = basis.astype(BF16)
-        modes_ref[at, :] = high
+        basis, high = rows_ref[at, :], high_ref[at, :]
         coeffs = dot(high, thrice_h, 1, 1) + dot(high, thrice_l, 1, 1)
         ch, cl = split(coeffs)
         left = basis - dot(jnp.where(from_low, cl, ch), stacked, 1, 0)
@@ -423,7 +462,8 @@
         scores_ref[:, at] = total[0:1, :]
         return carry
 
-    lax.fori_loop(0, s_ref.shape[0] // chunk, project, 0, unroll=2)
+    lax.fori_loop(0, len(spans), project, 0, unroll=2)
+    store.wait()
 
 
 def solve(snapshots, start, keys, pieces, pivots, rows, chunks, rows_total):
@@ -437,7 +477,7 @@
             jax.ShapeDtypeStruct((pivots, rank), F32),
         ],
         in_specs=[SMEM] + [VMEM] * 6,
-        out_specs=[VMEM] * 3,
+        out_specs=[HBM, VMEM, VMEM],
         scratch_shapes=[pltpu.VMEM((r, TILE), F32) for r in rows] + [
             pltpu.VMEM((snap, snap), BF16),
             pltpu.VMEM((snap, snap), BF16),
@@ -447,6 +487,11 @@
             pltpu.VMEM((snap, rank), BF16),
             pltpu.VMEM((snap, rank), F32),
             pltpu.VMEM((rank, rank), F32),
+            pltpu.VMEM((1, rank), F32),
+            pltpu.VMEM((rank, rank), BF16),
+            pltpu.VMEM((here, rank), F32),
+            pltpu.VMEM((here, rank), BF16),
+            pltpu.SemaphoreType.DMA,
         ],
         compiler_params=pltpu.CompilerParams(vmem_limit_bytes=GRANT),
         name="solve",

time: 117 us -> 109 us (0.932)
  Pallas kernels: 59.8 us -> 51.4 us
    pallas_call x1, Pallas kernels: 53.6 us -> 45.3 us  [solve(): pl.pallas_call(functools.partial(solve_kernel, chunks, rows_total), out_s...]
where the time goes in v4:
time: 109 us
  Pallas kernels  51.4 us (47%)
  waiting for transfers between devices  33 us (30%)
  starting transfers between devices  22.9 us (21%)
    pallas_call x1, Pallas kernels, solve(): pl.pallas_call(functools.partial(solve_kernel, chunks, rows_total), out_s...  45.3 us
    ppermute x18, waiting for transfers between devices, send(): return lax.ppermute(value, axis, [(i, i ^ mask) for i in range(size)])  33 us
    ppermute x18, starting transfers between devices, send(): return lax.ppermute(value, axis, [(i, i ^ mask) for i in range(size)])  22.9 us
    pallas_call x1, Pallas kernels, local_gram(): pl.pallas_call(functools.partial(gram_kernel, chunks), out_shape=shapes,...  6.14 us
  transfers between devices with their start and end apart: 18, of which 15 were waited for; matrix products, arithmetic and copies ran while one was open for 0% of the time, Pallas kernels for 0%

profile of v4, /device:TPU:0, one launch (start us, length us, event | category | flops | bytes accessed | tf_op | source)
XLA Modules:
  0.0 108.9 jit_solution(12965935469375159491)
XLA Ops:
  0.7 0.1 pad_add_fusion.keys_ref
  0.7 6.1 %local_gram.1 = (f32[1280,128]{1,0:T(8,128)S(1)}, f32[1280,128]{1,0:T(8,128)S(1)}, f32[1152,128]{1,0:T(8,128)S(1)}, f32[1152,128]{1,0:T(8,128)S(1)}) custom-call(s32[32]{0:T(128)} %dev_ref.1, s32[32]{0:T(128)} %row_ref.1, s32[3]{0:T(128)S(1)} %pad_add_fusion.keys_ref, bf16[2048,1024]{1,0:T(8,128)(2,1)} %s_ref.1), custom_call_target="tpu_custom_call" | custom-call | tf_op jit(solution)/shard_map/local_gram/pallas_call | solution.py:199
  6.9 0.6 collective-permute-start.3
  7.4 0.1 collective-permute-start
  7.5 1.6 %collective-permute-done.3 = f32[1152,128]{1,0:T(8,128)S(1)} collective-permute-done((f32[1152,128]{1,0:T(8,128)S(1)}, f32[1152,128]{1,0:T(8,128)S(1)}, u32[]{:S(2)}, u32[]{:S(2)}) %collective-permute-start.3) | collective-permute-done | bytes 589856 | tf_op jit(solution)/shard_map/ppermute | solution.py:96
  9.1 0.1 slice_add_fusion.3
  9.1 3.0 %collective-permute-start.4 = (f32[576,128]{1,0:T(8,128)S(1)}, f32[576,128]{1,0:T(8,128)S(1)}, u32[]{:S(2)}, u32[]{:S(2)}) collective-permute-start(f32[576,128]{1,0:T(8,128)S(1)} %get-tuple-element.24), channel_id=1, source_target_pairs={{0,2},{1,3},{2,0},{3,1},{4,6},{5,7},{6,4},{7,5},{8,10},{9,11},{10,... | collective-permute-start | bytes 884744 | tf_op jit(solution)/shard_map/ppermute | solution.py:96
  12.1 0.0 collective-permute-done
  12.1 0.1 slice_add_fusion.1
  12.2 0.0 copy-start
  12.2 0.0 copy-start.1
  12.2 1.5 %collective-permute-start.1 = (f32[640,128]{1,0:T(8,128)S(1)}, f32[640,128]{1,0:T(8,128)S(1)}, u32[]{:S(2)}, u32[]{:S(2)}) collective-permute-start(f32[640,128]{1,0:T(8,128)S(1)} %get-tuple-element.22), channel_id=1, source_target_pairs={{0,4},{4,0},{8,12},{12,8},{16,20},{20,16},{24,28},{28,24},{1,5},{5... | collective-permute-start | bytes 983048 | tf_op jit(solution)/shard_map/ppermute | solution.py:96
  13.7 5.7 %collective-permute-done.4 = f32[576,128]{1,0:T(8,128)S(1)} collective-permute-done((f32[576,128]{1,0:T(8,128)S(1)}, f32[576,128]{1,0:T(8,128)S(1)}, u32[]{:S(2)}, u32[]{:S(2)}) %collective-permute-start.4) | collective-permute-done | bytes 294944 | tf_op jit(solution)/shard_map/ppermute | solution.py:96
  19.4 1.8 %collective-permute-start.5 = (f32[288,128]{1,0:T(8,128)S(1)}, f32[288,128]{1,0:T(8,128)S(1)}, u32[]{:S(2)}, u32[]{:S(2)}) collective-permute-start(f32[288,128]{1,0:T(8,128)S(1)} %get-tuple-element.28), channel_id=1, source_target_pairs={{0,4},{4,0},{8,12},{12,8},{16,20},{20,16},{24,28},{28,24},{1,5},{5... | collective-permute-start | bytes 442376 | tf_op jit(solution)/shard_map/ppermute | solution.py:96
  21.2 0.6 collective-permute-done.1
  21.8 1.1 collective-permute-start.2
  22.9 2.0 %collective-permute-done.5 = f32[288,128]{1,0:T(8,128)S(1)} collective-permute-done((f32[288,128]{1,0:T(8,128)S(1)}, f32[288,128]{1,0:T(8,128)S(1)}, u32[]{:S(2)}, u32[]{:S(2)}) %collective-permute-start.5) | collective-permute-done | bytes 147488 | tf_op jit(solution)/shard_map/ppermute | solution.py:96
  24.9 2.3 %collective-permute-done.2 = f32[320,128]{1,0:T(8,128)S(1)} collective-permute-done((f32[320,128]{1,0:T(8,128)S(1)}, f32[320,128]{1,0:T(8,128)S(1)}, u32[]{:S(2)}, u32[]{:S(2)}) %collective-permute-start.2) | collective-permute-done | bytes 163872 | tf_op jit(solution)/shard_map/ppermute | solution.py:96
  27.3 1.7 %collective-permute-start.7 = (f32[152,128]{1,0:T(8,128)S(1)}, f32[152,128]{1,0:T(8,128)S(1)}, u32[]{:S(2)}, u32[]{:S(2)}) collective-permute-start(f32[152,128]{1,0:T(8,128)S(1)} %pad_maximum_fusion.3), channel_id=1, source_target_pairs={{0,8},{4,12},{8,0},{12,4},{16,24},{20,28},{24,16},{28,20},{1,9},{5... | collective-permute-start | bytes 233480 | tf_op jit(solution)/shard_map/ppermute | solution.py:96
  28.9 2.5 %collective-permute-start.8 = (f32[152,128]{1,0:T(8,128)S(1)}, f32[152,128]{1,0:T(8,128)S(1)}, u32[]{:S(2)}, u32[]{:S(2)}) collective-permute-start(f32[152,128]{1,0:T(8,128)S(1)} %pad_maximum_fusion.4), channel_id=1, source_target_pairs={{0,24},{4,28},{8,16},{12,20},{16,8},{20,12},{24,0},{28,4},{1,25},{... | collective-permute-start | bytes 233480 | tf_op jit(solution)/shard_map/ppermute | solution.py:96
  31.5 0.2 collective-permute-start.6
  31.6 1.0 collective-permute-done.7
  32.7 2.6 %collective-permute-done.8 = f32[152,128]{1,0:T(8,128)S(1)} collective-permute-done((f32[152,128]{1,0:T(8,128)S(1)}, f32[152,128]{1,0:T(8,128)S(1)}, u32[]{:S(2)}, u32[]{:S(2)}) %collective-permute-start.8) | collective-permute-done | bytes 77856 | tf_op jit(solution)/shard_map/ppermute | solution.py:96
  35.2 2.9 %collective-permute-done.6 = f32[152,128]{1,0:T(8,128)S(1)} collective-permute-done((f32[152,128]{1,0:T(8,128)S(1)}, f32[152,128]{1,0:T(8,128)S(1)}, u32[]{:S(2)}, u32[]{:S(2)}) %collective-permute-start.6) | collective-permute-done | bytes 77856 | tf_op jit(solution)/shard_map/ppermute | solution.py:96
  38.2 2.0 %collective-permute-start.11 = (f32[152,128]{1,0:T(8,128)S(1)}, f32[152,128]{1,0:T(8,128)S(1)}, u32[]{:S(2)}, u32[]{:S(2)}) collective-permute-start(f32[152,128]{1,0:T(8,128)S(1)} %pad_maximum_fusion.5), channel_id=1, source_target_pairs={{0,24},{4,28},{8,16},{12,20},{16,8},{20,12},{24,0},{28,4},{1,25},{... | collective-permute-start | bytes 233480 | tf_op jit(solution)/shard_map/ppermute | solution.py:96
  40.2 0.0 collective-permute-start.10
  40.2 2.5 %collective-permute-start.9 = (f32[152,128]{1,0:T(8,128)S(1)}, f32[152,128]{1,0:T(8,128)S(1)}, u32[]{:S(2)}, u32[]{:S(2)}) collective-permute-start(f32[152,128]{1,0:T(8,128)S(1)} %pad_maximum_fusion.5), channel_id=1, source_target_pairs={{0,16},{4,20},{8,24},{12,28},{16,0},{20,4},{24,8},{28,12},{1,17},{... | collective-permute-start | bytes 233480 | tf_op jit(solution)/shard_map/ppermute | solution.py:96
  42.7 2.8 %collective-permute-done.9 = f32[152,128]{1,0:T(8,128)S(1)} collective-permute-done((f32[152,128]{1,0:T(8,128)S(1)}, f32[152,128]{1,0:T(8,128)S(1)}, u32[]{:S(2)}, u32[]{:S(2)}) %collective-permute-start.9) | collective-permute-done | bytes 77856 | tf_op jit(solution)/shard_map/ppermute | solution.py:96
  45.5 0.6 collective-permute-done.10
  46.2 0.0 collective-permute-done.11
  46.2 1.5 %collective-permute-start.12 = (f32[320,128]{1,0:T(8,128)S(1)}, f32[320,128]{1,0:T(8,128)S(1)}, u32[]{:S(2)}, u32[]{:S(2)}) collective-permute-start(f32[320,128]{1,0:T(8,128)S(1)} %pad_maximum_fusion), channel_id=1, source_target_pairs={{0,2},{1,3},{2,0},{3,1},{4,6},{5,7},{6,4},{7,5},{8,10},{9,11},{10,... | collective-permute-start | bytes 491528 | tf_op jit(solution)/shard_map/ppermute | solution.py:96
  47.8 1.6 %collective-permute-start.15 = (f32[288,128]{1,0:T(8,128)S(1)}, f32[288,128]{1,0:T(8,128)S(1)}, u32[]{:S(2)}, u32[]{:S(2)}) collective-permute-start(f32[288,128]{1,0:T(8,128)S(1)} %pad_maximum_fusion.1), channel_id=1, source_target_pairs={{0,4},{4,0},{8,12},{12,8},{16,20},{20,16},{24,28},{28,24},{1,5},{5... | collective-permute-start | bytes 442376 | tf_op jit(solution)/shard_map/ppermute | solution.py:96
  49.3 2.8 %collective-permute-done.12 = f32[320,128]{1,0:T(8,128)S(1)} collective-permute-done((f32[320,128]{1,0:T(8,128)S(1)}, f32[320,128]{1,0:T(8,128)S(1)}, u32[]{:S(2)}, u32[]{:S(2)}) %collective-permute-start.12) | collective-permute-done | bytes 163872 | tf_op jit(solution)/shard_map/ppermute | solution.py:96
  52.2 1.5 %collective-permute-start.13 = (f32[640,128]{1,0:T(8,128)S(1)}, f32[640,128]{1,0:T(8,128)S(1)}, u32[]{:S(2)}, u32[]{:S(2)}) collective-permute-start(f32[640,128]{1,0:T(8,128)S(1)} %get-tuple-element.35), channel_id=1, source_target_pairs={{0,4},{4,0},{8,12},{12,8},{16,20},{20,16},{24,28},{28,24},{1,5},{5... | collective-permute-start | bytes 983048 | tf_op jit(solution)/shard_map/ppermute | solution.py:96
  53.7 0.8 collective-permute-done.15
  54.6 1.4 %collective-permute-start.16 = (f32[576,128]{1,0:T(8,128)S(1)}, f32[576,128]{1,0:T(8,128)S(1)}, u32[]{:S(2)}, u32[]{:S(2)}) collective-permute-start(f32[576,128]{1,0:T(8,128)S(1)} %get-tuple-element.37), channel_id=1, source_target_pairs={{0,2},{1,3},{2,0},{3,1},{4,6},{5,7},{6,4},{7,5},{8,10},{9,11},{10,... | collective-permute-start | bytes 884744 | tf_op jit(solution)/shard_map/ppermute | solution.py:96
  56.0 3.3 %collective-permute-done.13 = f32[640,128]{1,0:T(8,128)S(1)} collective-permute-done((f32[640,128]{1,0:T(8,128)S(1)}, f32[640,128]{1,0:T(8,128)S(1)}, u32[]{:S(2)}, u32[]{:S(2)}) %collective-permute-start.13) | collective-permute-done | bytes 327712 | tf_op jit(solution)/shard_map/ppermute | solution.py:96
  59.3 0.1 collective-permute-start.14
  59.4 2.0 %collective-permute-done.16 = f32[576,128]{1,0:T(8,128)S(1)} collective-permute-done((f32[576,128]{1,0:T(8,128)S(1)}, f32[576,128]{1,0:T(8,128)S(1)}, u32[]{:S(2)}, u32[]{:S(2)}) %collective-permute-start.16) | collective-permute-done | bytes 294944 | tf_op jit(solution)/shard_map/ppermute | solution.py:96
  61.4 0.1 collective-permute-start.17
  61.5 2.0 %collective-permute-done.17.b1_ref = f32[1152,128]{1,0:T(8,128)S(1)} collective-permute-done((f32[1152,128]{1,0:T(8,128)S(1)}, f32[1152,128]{1,0:T(8,128)S(1)}, u32[]{:S(2)}, u32[]{:S(2)}) %collective-permute-start.17) | collective-permute-done | bytes 589856 | tf_op jit(solution)/shard_map/ppermute | solution.py:96
  63.5 0.0 collective-permute-done.14.a1_ref
  63.5 0.0 copy-done
  63.5 0.0 copy-done.1
  63.5 45.3 %solve.1 = (bf16[2048,256]{1,0:T(8,128)(2,1)}, f32[1,2048]{1,0:T(1,128)}, f32[32,256]{1,0:T(8,128)}) custom-call(s32[3]{0:T(128)S(1)} %pad_add_fusion.keys_ref, f32[1024,256]{1,0:T(8,128)S(1)} %copy-done.1, bf16[2048,1024]{1,0:T(8,128)(2,1)S(1)} %copy-done, f32[1280,128]{1,0:T(8,128)S(1)} %constant_dynamic-update-slice_fusion.5.a0_ref, ...), custom_call_target="tpu_custom_call" | custom-call | tf_op jit(solution)/shard_map/solve/pallas_call | solution.py:472
  (24 shorter events, 0.3 us)
Async XLA Ops:
  6.9 2.2 %collective-permute-start.3 = (f32[1152,128]{1,0:T(8,128)S(1)}, f32[1152,128]{1,0:T(8,128)S(1)}, u32[]{:S(2)}, u32[]{:S(2)}) collective-permute-start(f32[1152,128]{1,0:T(8,128)S(1)} %get-tuple-element.13), channel_id=1, source_target_pairs={{0,1},{1,0},{2,3},{3,2},{4,5},{5,4},{6,7},{7,6},{8,9},{9,8},{10,11... | collective-permute-start | bytes 1769480 | tf_op jit(solution)/shard_map/ppermute | solution.py:96
  7.4 4.7 %collective-permute-start = (f32[1280,128]{1,0:T(8,128)S(1)}, f32[1280,128]{1,0:T(8,128)S(1)}, u32[]{:S(2)}, u32[]{:S(2)}) collective-permute-start(f32[1280,128]{1,0:T(8,128)S(1)} %get-tuple-element.11), channel_id=1, source_target_pairs={{0,1},{1,0},{2,3},{3,2},{4,5},{5,4},{6,7},{7,6},{8,9},{9,8},{10,11... | collective-permute-start | bytes 1966088 | tf_op jit(solution)/shard_map/ppermute | solution.py:96
  9.1 10.3 %collective-permute-start.4 = (f32[576,128]{1,0:T(8,128)S(1)}, f32[576,128]{1,0:T(8,128)S(1)}, u32[]{:S(2)}, u32[]{:S(2)}) collective-permute-start(f32[576,128]{1,0:T(8,128)S(1)} %get-tuple-element.24), channel_id=1, source_target_pairs={{0,2},{1,3},{2,0},{3,1},{4,6},{5,7},{6,4},{7,5},{8,10},{9,11},{10,... | collective-permute-start | bytes 884744 | tf_op jit(solution)/shard_map/ppermute | solution.py:96
  12.2 51.3 %copy-start = (bf16[2048,1024]{1,0:T(8,128)(2,1)S(1)}, bf16[2048,1024]{1,0:T(8,128)(2,1)}, u32[]{:S(2)}) copy-start(bf16[2048,1024]{1,0:T(8,128)(2,1)} %s_ref.1) | copy-start | bytes 12582916
  12.2 51.3 %copy-start.1 = (f32[1024,256]{1,0:T(8,128)S(1)}, f32[1024,256]{1,0:T(8,128)}, u32[]{:S(2)}) copy-start(f32[1024,256]{1,0:T(8,128)} %start_ref.1) | copy-start | bytes 3145732
  12.2 9.6 %collective-permute-start.1 = (f32[640,128]{1,0:T(8,128)S(1)}, f32[640,128]{1,0:T(8,128)S(1)}, u32[]{:S(2)}, u32[]{:S(2)}) collective-permute-start(f32[640,128]{1,0:T(8,128)S(1)} %get-tuple-element.22), channel_id=1, source_target_pairs={{0,4},{4,0},{8,12},{12,8},{16,20},{20,16},{24,28},{28,24},{1,5},{5... | collective-permute-start | bytes 983048 | tf_op jit(solution)/shard_map/ppermute | solution.py:96
  19.4 5.4 %collective-permute-start.5 = (f32[288,128]{1,0:T(8,128)S(1)}, f32[288,128]{1,0:T(8,128)S(1)}, u32[]{:S(2)}, u32[]{:S(2)}) collective-permute-start(f32[288,128]{1,0:T(8,128)S(1)} %get-tuple-element.28), channel_id=1, source_target_pairs={{0,4},{4,0},{8,12},{12,8},{16,20},{20,16},{24,28},{28,24},{1,5},{5... | collective-permute-start | bytes 442376 | tf_op jit(solution)/shard_map/ppermute | solution.py:96
  21.8 5.4 %collective-permute-start.2 = (f32[320,128]{1,0:T(8,128)S(1)}, f32[320,128]{1,0:T(8,128)S(1)}, u32[]{:S(2)}, u32[]{:S(2)}) collective-permute-start(f32[320,128]{1,0:T(8,128)S(1)} %get-tuple-element.26), channel_id=1, source_target_pairs={{0,2},{1,3},{2,0},{3,1},{4,6},{5,7},{6,4},{7,5},{8,10},{9,11},{10,... | collective-permute-start | bytes 491528 | tf_op jit(solution)/shard_map/ppermute | solution.py:96
  27.3 5.4 %collective-permute-start.7 = (f32[152,128]{1,0:T(8,128)S(1)}, f32[152,128]{1,0:T(8,128)S(1)}, u32[]{:S(2)}, u32[]{:S(2)}) collective-permute-start(f32[152,128]{1,0:T(8,128)S(1)} %pad_maximum_fusion.3), channel_id=1, source_target_pairs={{0,8},{4,12},{8,0},{12,4},{16,24},{20,28},{24,16},{28,20},{1,9},{5... | collective-permute-start | bytes 233480 | tf_op jit(solution)/shard_map/ppermute | solution.py:96
  28.9 6.3 %collective-permute-start.8 = (f32[152,128]{1,0:T(8,128)S(1)}, f32[152,128]{1,0:T(8,128)S(1)}, u32[]{:S(2)}, u32[]{:S(2)}) collective-permute-start(f32[152,128]{1,0:T(8,128)S(1)} %pad_maximum_fusion.4), channel_id=1, source_target_pairs={{0,24},{4,28},{8,16},{12,20},{16,8},{20,12},{24,0},{28,4},{1,25},{... | collective-permute-start | bytes 233480 | tf_op jit(solution)/shard_map/ppermute | solution.py:96
  31.5 6.7 %collective-permute-start.6 = (f32[152,128]{1,0:T(8,128)S(1)}, f32[152,128]{1,0:T(8,128)S(1)}, u32[]{:S(2)}, u32[]{:S(2)}) collective-permute-start(f32[152,128]{1,0:T(8,128)S(1)} %pad_maximum_fusion.2), channel_id=1, source_target_pairs={{0,16},{4,20},{8,24},{12,28},{16,0},{20,4},{24,8},{28,12},{1,17},{... | collective-permute-start | bytes 233480 | tf_op jit(solution)/shard_map/ppermute | solution.py:96
  38.2 7.9 %collective-permute-start.11 = (f32[152,128]{1,0:T(8,128)S(1)}, f32[152,128]{1,0:T(8,128)S(1)}, u32[]{:S(2)}, u32[]{:S(2)}) collective-permute-start(f32[152,128]{1,0:T(8,128)S(1)} %pad_maximum_fusion.5), channel_id=1, source_target_pairs={{0,24},{4,28},{8,16},{12,20},{16,8},{20,12},{24,0},{28,4},{1,25},{... | collective-permute-start | bytes 233480 | tf_op jit(solution)/shard_map/ppermute | solution.py:96
  40.2 5.9 %collective-permute-start.10 = (f32[152,128]{1,0:T(8,128)S(1)}, f32[152,128]{1,0:T(8,128)S(1)}, u32[]{:S(2)}, u32[]{:S(2)}) collective-permute-start(f32[152,128]{1,0:T(8,128)S(1)} %pad_maximum_fusion.5), channel_id=1, source_target_pairs={{0,8},{4,12},{8,0},{12,4},{16,24},{20,28},{24,16},{28,20},{1,9},{5... | collective-permute-start | bytes 233480 | tf_op jit(solution)/shard_map/ppermute | solution.py:96
  40.2 5.3 %collective-permute-start.9 = (f32[152,128]{1,0:T(8,128)S(1)}, f32[152,128]{1,0:T(8,128)S(1)}, u32[]{:S(2)}, u32[]{:S(2)}) collective-permute-start(f32[152,128]{1,0:T(8,128)S(1)} %pad_maximum_fusion.5), channel_id=1, source_target_pairs={{0,16},{4,20},{8,24},{12,28},{16,0},{20,4},{24,8},{28,12},{1,17},{... | collective-permute-start | bytes 233480 | tf_op jit(solution)/shard_map/ppermute | solution.py:96
  46.2 5.9 %collective-permute-start.12 = (f32[320,128]{1,0:T(8,128)S(1)}, f32[320,128]{1,0:T(8,128)S(1)}, u32[]{:S(2)}, u32[]{:S(2)}) collective-permute-start(f32[320,128]{1,0:T(8,128)S(1)} %pad_maximum_fusion), channel_id=1, source_target_pairs={{0,2},{1,3},{2,0},{3,1},{4,6},{5,7},{6,4},{7,5},{8,10},{9,11},{10,... | collective-permute-start | bytes 491528 | tf_op jit(solution)/shard_map/ppermute | solution.py:96
  47.8 6.8 %collective-permute-start.15 = (f32[288,128]{1,0:T(8,128)S(1)}, f32[288,128]{1,0:T(8,128)S(1)}, u32[]{:S(2)}, u32[]{:S(2)}) collective-permute-start(f32[288,128]{1,0:T(8,128)S(1)} %pad_maximum_fusion.1), channel_id=1, source_target_pairs={{0,4},{4,0},{8,12},{12,8},{16,20},{20,16},{24,28},{28,24},{1,5},{5... | collective-permute-start | bytes 442376 | tf_op jit(solution)/shard_map/ppermute | solution.py:96
  52.2 7.1 %collective-permute-start.13 = (f32[640,128]{1,0:T(8,128)S(1)}, f32[640,128]{1,0:T(8,128)S(1)}, u32[]{:S(2)}, u32[]{:S(2)}) collective-permute-start(f32[640,128]{1,0:T(8,128)S(1)} %get-tuple-element.35), channel_id=1, source_target_pairs={{0,4},{4,0},{8,12},{12,8},{16,20},{20,16},{24,28},{28,24},{1,5},{5... | collective-permute-start | bytes 983048 | tf_op jit(solution)/shard_map/ppermute | solution.py:96
  54.6 6.8 %collective-permute-start.16 = (f32[576,128]{1,0:T(8,128)S(1)}, f32[576,128]{1,0:T(8,128)S(1)}, u32[]{:S(2)}, u32[]{:S(2)}) collective-permute-start(f32[576,128]{1,0:T(8,128)S(1)} %get-tuple-element.37), channel_id=1, source_target_pairs={{0,2},{1,3},{2,0},{3,1},{4,6},{5,7},{6,4},{7,5},{8,10},{9,11},{10,... | collective-permute-start | bytes 884744 | tf_op jit(solution)/shard_map/ppermute | solution.py:96
  59.3 4.1 %collective-permute-start.14 = (f32[1280,128]{1,0:T(8,128)S(1)}, f32[1280,128]{1,0:T(8,128)S(1)}, u32[]{:S(2)}, u32[]{:S(2)}) collective-permute-start(f32[1280,128]{1,0:T(8,128)S(1)} %constant_dynamic-update-slice_fusion.5.a0_ref), channel_id=1, source_target_pairs={{0,1},{1,0},{2,3},{3,2},{4,5},{5,4},{6,7},{7,6},{8,9},{9,8},{10,11... | collective-permute-start | bytes 1966088 | tf_op jit(solution)/shard_map/ppermute | solution.py:96
  61.4 2.1 %collective-permute-start.17 = (f32[1152,128]{1,0:T(8,128)S(1)}, f32[1152,128]{1,0:T(8,128)S(1)}, u32[]{:S(2)}, u32[]{:S(2)}) collective-permute-start(f32[1152,128]{1,0:T(8,128)S(1)} %constant_dynamic-update-slice_fusion.16.b0_ref), channel_id=1, source_target_pairs={{0,1},{1,0},{2,3},{3,2},{4,5},{5,4},{6,7},{7,6},{8,9},{9,8},{10,11... | collective-permute-start | bytes 1769480 | tf_op jit(solution)/shard_map/ppermute | solution.py:96

commit v5 on v4

--- a/solution.py
+++ b/solution.py
@@ -6,11 +6,13 @@
 from jax.experimental.pallas import tpu as pltpu
 from jax.sharding import PartitionSpec as P
 
+
 ITERS = 4
 TILE = 128
 BAND = 2
 BLOCK = 64
 LOADS = 2
+UNIT = 256
 GRANT = 28 << 20
 F32, BF16 = jnp.float32, jnp.bfloat16
 HIGHEST = lax.Precision.HIGHEST
@@ -47,14 +49,22 @@
 def places(tiles):
     result = []
     for bands in bands_of(tiles):
-        row, entries = 0, []
+        row, above, pairs = 0, [], []
         for band in bands:
             for i in range(band * BAND, band * BAND + BAND):
-                for j in range(i, tiles):
-                    entries.append((i, j, row))
+                for j in range(i + 1, tiles):
+                    above.append((i, j, row))
                     row += TILE
-        result.append((entries, row))
+            pairs.append((band, row))
+            row += TILE
+        result.append((above, pairs, row))
     return result
+
+
+def part_rows(tiles, pivots):
+    first, second = places(tiles)
+    ends = (first[2] + pivots * tiles, second[2] + tiles // BAND)
+    return [-(-end // UNIT) * UNIT for end in ends]
 
 
 def exchange_plan(mesh_shape, rows):
@@ -102,10 +112,10 @@
         got = send(jnp.concatenate(values, axis=0), axis, partners(masks)[mask_at])
         first = values[0].shape[0]
         return [got[:first], got[first:]]
-    return [
-        send(value, axis, partners(masks)[mask_at])
-        for value, (axis, masks) in zip(values, stages)
-    ]
+    result = []
+    for value, (axis, masks) in zip(values, stages):
+        result.append(send(value, axis, partners(masks)[mask_at]))
+    return result
 
 
 def add_up(terms):
@@ -116,7 +126,9 @@
 
 def reduce_parts(kept, sent, orders, halvings):
     stages = list(zip(*orders))
-    terms = [[v, send(s, order[0][0], order[0][1][0])] for v, s, order in zip(kept, sent, orders)]
+    terms = []
+    for v, s, order in zip(kept, sent, orders):
+        terms.append([v, send(s, order[0][0], order[0][1][0])])
     for number in range(1, len(stages)):
         stage = stages[number]
         count = 1 << len(stage[0][1])
@@ -126,7 +138,9 @@
                 [add_up([v[q * size:(q + 1) * size] for v in t]) for q in range(count)]
                 for t, size in zip(terms, sizes)
             ]
-            got = [exchange([c[q] for c in cut], stage, q) for q in range(1, count)]
+            got = []
+            for q in range(1, count):
+                got.append(exchange([c[q] for c in cut], stage, q))
             terms = [[c[0]] + [g[part] for g in got] for part, c in enumerate(cut)]
         else:
             whole = [add_up(t) for t in terms]
@@ -148,6 +162,10 @@
     tiles = s_ref.shape[1] // TILE
     spots = places(tiles)
     piece = s_ref.shape[0] // LOADS
+    upper = iota((TILE, TILE), 0) <= iota((TILE, TILE), 1)
+    same = iota((TILE, TILE), 0) == iota((TILE, TILE), 1)
+    last = spots[1][2]
+    work[1][last:, :] = jnp.zeros_like(work[1][last:, :])
     copies = []
     for q in range(LOADS):
         at = pl.ds(q * piece, piece)
@@ -157,20 +175,28 @@
         copies[q].wait()
         rows = slice(q * piece, (q + 1) * piece)
         for part in range(2):
-            where = {(i, j): row for i, j, row in spots[part][0]}
-            for band in bands_of(tiles)[part]:
+            above, pairs, _ = spots[part]
+            where = {(i, j): row for i, j, row in above}
+            for band, pair_row in pairs:
                 first = band * BAND * TILE
                 strip = dot(s_ref[rows, first:first + BAND * TILE], s_ref[rows, first:], 0, 0)
-                for a in range(BAND):
-                    i = band * BAND + a
-                    for j in range(i, tiles):
-                        col = (j - band * BAND) * TILE
-                        row = where[(i, j)]
-                        term = strip[a * TILE:(a + 1) * TILE, col:col + TILE]
-                        if q:
-                            term = work[part][row:row + TILE, :] + term
-                        work[part][row:row + TILE, :] = term
-    base = spots[0][1]
+
+                def tile(a, b):
+                    return strip[a * TILE:(a + 1) * TILE, b * TILE:(b + 1) * TILE]
+
+                terms = [
+                    (part, where[(i, j)], tile(i - band * BAND, j - band * BAND))
+                    for i in range(band * BAND, band * BAND + BAND) for j in range(i + 1, tiles)
+                ]
+                terms.append((part, pair_row, jnp.where(upper, tile(0, 0), tile(1, 1))))
+                diagonal = jnp.sum(jnp.where(same, tile(1, 1), 0.0), axis=0, keepdims=True)
+                terms.append((1, spots[1][2] + band, diagonal))
+                for to, row, term in terms:
+                    size = term.shape[0]
+                    if q:
+                        term = work[to][row:row + size, :] + term
+                    work[to][row:row + size, :] = term
+    base = spots[0][2]
     pivots = dev_ref.shape[0]
     sub = iota((16, s_ref.shape[1]), 0)
 
@@ -355,16 +381,26 @@
             to = pl.multiple_of((keys_ref[part] ^ q) * size, 8)
             packed[part][pl.ds(to, size), :] = half[at:at + size, :]
     spots = places(tiles)
+
+    def put(i, j, value):
+        high, low = split(value)
+        gh_ref[i * TILE:(i + 1) * TILE, j * TILE:(j + 1) * TILE] = high
+        gl_ref[i * TILE:(i + 1) * TILE, j * TILE:(j + 1) * TILE] = low
+
+    across, along = iota((TILE, TILE), 0), iota((TILE, TILE), 1)
     for part in range(2):
         for i, j, row in spots[part][0]:
             value = packed[part][row:row + TILE, :]
-            high, low = split(value)
-            gh_ref[i * TILE:(i + 1) * TILE, j * TILE:(j + 1) * TILE] = high
-            gl_ref[i * TILE:(i + 1) * TILE, j * TILE:(j + 1) * TILE] = low
-            if i != j:
-                high, low = split(jnp.transpose(value))
-                gh_ref[j * TILE:(j + 1) * TILE, i * TILE:(i + 1) * TILE] = high
-                gl_ref[j * TILE:(j + 1) * TILE, i * TILE:(i + 1) * TILE] = low
+            put(i, j, value)
+            put(j, i, jnp.transpose(value))
+        for band, row in spots[part][1]:
+            value = packed[part][row:row + TILE, :]
+            turned = jnp.transpose(value)
+            end = spots[1][2] + band
+            diagonal = jnp.where(across == along, pb_ref[end:end + 1, :], turned)
+            i = band * BAND
+            put(i, i, jnp.where(across <= along, value, turned))
+            put(i + 1, i + 1, jnp.where(across > along, value, diagonal))
     strips = rank // BLOCK
     step = snap // strips
 
@@ -423,7 +459,7 @@
         basis = dot(s_ref[at, :], coef, 1, 0)
         rows_ref[at, :] = basis
         high_ref[at, :] = basis.astype(BF16)
-    base = spots[0][1]
+    base = spots[0][2]
     pivots = basis_ref.shape[0]
     picked = jnp.concatenate(
         [pa_ref[base + t * pivots:base + (t + 1) * pivots, :] for t in range(tiles)], axis=1
@@ -501,8 +537,7 @@
 def local(mesh_shape, snapshots, start, pivot_dev, pivot_row):
     here, snap = snapshots.shape
     pivots = pivot_dev.shape[0]
-    spots = places(snap // TILE)
-    rows = [spots[0][1] + pivots * (snap // TILE), spots[1][1]]
+    rows = part_rows(snap // TILE, pivots)
     orders, halvings = exchange_plan(mesh_shape, rows)
     chunks = chunks_of(orders[0], halvings)
     myself = lax.axis_index(("grp", "blk"))
@@ -519,8 +554,12 @@
 
 def solution(mesh):
     placed = (P(("grp", "blk"), None), P(), P(), P())
+
+    def body(*args):
+        return local(dict(mesh.shape), *args)
+
     return jax.shard_map(
-        functools.partial(local, dict(mesh.shape)),
+        body,
         mesh=mesh,
         in_specs=placed,
         out_specs=(P(("grp", "blk"), None), P(("grp", "blk")), P()),

time: 109 us -> 108 us (level)
  transfers between devices with their start and end apart: 18 -> 18, of which waited for: 15 -> 14; matrix products, arithmetic and copies ran while one was open for 0% -> 0% of each run, Pallas kernels for 0% -> 0%
where the time goes in v5:
time: 108 us
  Pallas kernels  51.6 us (48%)
  waiting for transfers between devices  32 us (30%)
  starting transfers between devices  22.7 us (21%)
    pallas_call x1, Pallas kernels, solve(): pl.pallas_call(functools.partial(solve_kernel, chunks, rows_total), out_s...  45.3 us
    ppermute x18, waiting for transfers between devices, send(): return lax.ppermute(value, axis, [(i, i ^ mask) for i in range(size)])  32 us
    ppermute x18, starting transfers between devices, send(): return lax.ppermute(value, axis, [(i, i ^ mask) for i in range(size)])  22.7 us
    pallas_call x1, Pallas kernels, local_gram(): pl.pallas_call(functools.partial(gram_kernel, chunks), out_shape=shapes,...  6.28 us
  transfers between devices with their start and end apart: 18, of which 14 were waited for; matrix products, arithmetic and copies ran while one was open for 0% of the time, Pallas kernels for 0%

profile of v5, /device:TPU:0, one launch (start us, length us, event | category | flops | bytes accessed | tf_op | source)
XLA Modules:
  0.0 107.9 jit_solution(9782579218853127502)
XLA Ops:
  0.7 0.1 pad_add_fusion.keys_ref
  0.7 6.3 %local_gram.1 = (f32[1152,128]{1,0:T(8,128)S(1)}, f32[1152,128]{1,0:T(8,128)S(1)}, f32[1152,128]{1,0:T(8,128)S(1)}, f32[1152,128]{1,0:T(8,128)S(1)}) custom-call(s32[32]{0:T(128)} %dev_ref.1, s32[32]{0:T(128)} %row_ref.1, s32[3]{0:T(128)S(1)} %pad_add_fusion.keys_ref, bf16[2048,1024]{1,0:T(8,128)(2,1)} %s_ref.1), custom_call_target="tpu_custom_call" | custom-call | tf_op jit(solution)/shard_map/local_gram/pallas_call | solution.py:225
  7.0 0.6 collective-permute-start
  7.6 0.1 collective-permute-start.3
  7.7 1.6 %collective-permute-done = f32[1152,128]{1,0:T(8,128)S(1)} collective-permute-done((f32[1152,128]{1,0:T(8,128)S(1)}, f32[1152,128]{1,0:T(8,128)S(1)}, u32[]{:S(2)}, u32[]{:S(2)}) %collective-permute-start) | collective-permute-done | bytes 589856 | tf_op jit(solution)/shard_map/ppermute | solution.py:106
  9.2 0.1 slice_add_fusion.3
  9.3 2.9 %collective-permute-start.1 = (f32[576,128]{1,0:T(8,128)S(1)}, f32[576,128]{1,0:T(8,128)S(1)}, u32[]{:S(2)}, u32[]{:S(2)}) collective-permute-start(f32[576,128]{1,0:T(8,128)S(1)} %get-tuple-element.22), channel_id=1, source_target_pairs={{0,4},{4,0},{8,12},{12,8},{16,20},{20,16},{24,28},{28,24},{1,5},{5... | collective-permute-start | bytes 884744 | tf_op jit(solution)/shard_map/ppermute | solution.py:106
  12.2 0.0 collective-permute-done.3
  12.2 0.0 copy-start
  12.2 0.0 copy-start.1
  12.2 0.1 slice_add_fusion.1
  12.3 1.6 %collective-permute-start.4 = (f32[576,128]{1,0:T(8,128)S(1)}, f32[576,128]{1,0:T(8,128)S(1)}, u32[]{:S(2)}, u32[]{:S(2)}) collective-permute-start(f32[576,128]{1,0:T(8,128)S(1)} %get-tuple-element.24), channel_id=1, source_target_pairs={{0,2},{1,3},{2,0},{3,1},{4,6},{5,7},{6,4},{7,5},{8,10},{9,11},{10,... | collective-permute-start | bytes 884744 | tf_op jit(solution)/shard_map/ppermute | solution.py:106
  13.9 5.6 %collective-permute-done.1 = f32[576,128]{1,0:T(8,128)S(1)} collective-permute-done((f32[576,128]{1,0:T(8,128)S(1)}, f32[576,128]{1,0:T(8,128)S(1)}, u32[]{:S(2)}, u32[]{:S(2)}) %collective-permute-start.1) | collective-permute-done | bytes 294944 | tf_op jit(solution)/shard_map/ppermute | solution.py:106
  19.5 1.8 %collective-permute-start.2 = (f32[288,128]{1,0:T(8,128)S(1)}, f32[288,128]{1,0:T(8,128)S(1)}, u32[]{:S(2)}, u32[]{:S(2)}) collective-permute-start(f32[288,128]{1,0:T(8,128)S(1)} %get-tuple-element.26), channel_id=1, source_target_pairs={{0,2},{1,3},{2,0},{3,1},{4,6},{5,7},{6,4},{7,5},{8,10},{9,11},{10,... | collective-permute-start | bytes 442376 | tf_op jit(solution)/shard_map/ppermute | solution.py:106
  21.4 0.0 collective-permute-done.4
  21.4 1.5 %collective-permute-start.5 = (f32[288,128]{1,0:T(8,128)S(1)}, f32[288,128]{1,0:T(8,128)S(1)}, u32[]{:S(2)}, u32[]{:S(2)}) collective-permute-start(f32[288,128]{1,0:T(8,128)S(1)} %get-tuple-element.28), channel_id=1, source_target_pairs={{0,4},{4,0},{8,12},{12,8},{16,20},{20,16},{24,28},{28,24},{1,5},{5... | collective-permute-start | bytes 442376 | tf_op jit(solution)/shard_map/ppermute | solution.py:106
  23.0 1.9 %collective-permute-done.2 = f32[288,128]{1,0:T(8,128)S(1)} collective-permute-done((f32[288,128]{1,0:T(8,128)S(1)}, f32[288,128]{1,0:T(8,128)S(1)}, u32[]{:S(2)}, u32[]{:S(2)}) %collective-permute-start.2) | collective-permute-done | bytes 147488 | tf_op jit(solution)/shard_map/ppermute | solution.py:106
  24.9 1.7 %collective-permute-done.5 = f32[288,128]{1,0:T(8,128)S(1)} collective-permute-done((f32[288,128]{1,0:T(8,128)S(1)}, f32[288,128]{1,0:T(8,128)S(1)}, u32[]{:S(2)}, u32[]{:S(2)}) %collective-permute-start.5) | collective-permute-done | bytes 147488 | tf_op jit(solution)/shard_map/ppermute | solution.py:106
  26.7 1.6 %collective-permute-start.7 = (f32[144,128]{1,0:T(8,128)S(1)}, f32[144,128]{1,0:T(8,128)S(1)}, u32[]{:S(2)}, u32[]{:S(2)}) collective-permute-start(f32[144,128]{1,0:T(8,128)S(1)} %pad_maximum_fusion.3), channel_id=1, source_target_pairs={{0,8},{4,12},{8,0},{12,4},{16,24},{20,28},{24,16},{28,20},{1,9},{5... | collective-permute-start | bytes 221192 | tf_op jit(solution)/shard_map/ppermute | solution.py:106
  28.3 2.5 %collective-permute-start.8 = (f32[144,128]{1,0:T(8,128)S(1)}, f32[144,128]{1,0:T(8,128)S(1)}, u32[]{:S(2)}, u32[]{:S(2)}) collective-permute-start(f32[144,128]{1,0:T(8,128)S(1)} %pad_maximum_fusion.4), channel_id=1, source_target_pairs={{0,24},{4,28},{8,16},{12,20},{16,8},{20,12},{24,0},{28,4},{1,25},{... | collective-permute-start | bytes 221192 | tf_op jit(solution)/shard_map/ppermute | solution.py:106
  30.8 0.2 collective-permute-start.6
  31.0 0.9 collective-permute-done.7
  31.9 2.6 %collective-permute-done.8 = f32[144,128]{1,0:T(8,128)S(1)} collective-permute-done((f32[144,128]{1,0:T(8,128)S(1)}, f32[144,128]{1,0:T(8,128)S(1)}, u32[]{:S(2)}, u32[]{:S(2)}) %collective-permute-start.8) | collective-permute-done | bytes 73760 | tf_op jit(solution)/shard_map/ppermute | solution.py:106
  34.5 2.9 %collective-permute-done.6 = f32[144,128]{1,0:T(8,128)S(1)} collective-permute-done((f32[144,128]{1,0:T(8,128)S(1)}, f32[144,128]{1,0:T(8,128)S(1)}, u32[]{:S(2)}, u32[]{:S(2)}) %collective-permute-start.6) | collective-permute-done | bytes 73760 | tf_op jit(solution)/shard_map/ppermute | solution.py:106
  37.5 1.9 %collective-permute-start.11 = (f32[144,128]{1,0:T(8,128)S(1)}, f32[144,128]{1,0:T(8,128)S(1)}, u32[]{:S(2)}, u32[]{:S(2)}) collective-permute-start(f32[144,128]{1,0:T(8,128)S(1)} %pad_maximum_fusion.5), channel_id=1, source_target_pairs={{0,24},{4,28},{8,16},{12,20},{16,8},{20,12},{24,0},{28,4},{1,25},{... | collective-permute-start | bytes 221192 | tf_op jit(solution)/shard_map/ppermute | solution.py:106
  39.3 0.0 collective-permute-start.10
  39.3 2.6 %collective-permute-start.9 = (f32[144,128]{1,0:T(8,128)S(1)}, f32[144,128]{1,0:T(8,128)S(1)}, u32[]{:S(2)}, u32[]{:S(2)}) collective-permute-start(f32[144,128]{1,0:T(8,128)S(1)} %pad_maximum_fusion.5), channel_id=1, source_target_pairs={{0,16},{4,20},{8,24},{12,28},{16,0},{20,4},{24,8},{28,12},{1,17},{... | collective-permute-start | bytes 221192 | tf_op jit(solution)/shard_map/ppermute | solution.py:106
  41.9 2.7 %collective-permute-done.9 = f32[144,128]{1,0:T(8,128)S(1)} collective-permute-done((f32[144,128]{1,0:T(8,128)S(1)}, f32[144,128]{1,0:T(8,128)S(1)}, u32[]{:S(2)}, u32[]{:S(2)}) %collective-permute-start.9) | collective-permute-done | bytes 73760 | tf_op jit(solution)/shard_map/ppermute | solution.py:106
  44.6 0.6 collective-permute-done.10
  45.3 0.0 collective-permute-done.11
  45.3 1.3 %collective-permute-start.12 = (f32[288,128]{1,0:T(8,128)S(1)}, f32[288,128]{1,0:T(8,128)S(1)}, u32[]{:S(2)}, u32[]{:S(2)}) collective-permute-start(f32[288,128]{1,0:T(8,128)S(1)} %pad_maximum_fusion), channel_id=1, source_target_pairs={{0,2},{1,3},{2,0},{3,1},{4,6},{5,7},{6,4},{7,5},{8,10},{9,11},{10,... | collective-permute-start | bytes 442376 | tf_op jit(solution)/shard_map/ppermute | solution.py:106
  46.7 1.1 %collective-permute-start.15 = (f32[288,128]{1,0:T(8,128)S(1)}, f32[288,128]{1,0:T(8,128)S(1)}, u32[]{:S(2)}, u32[]{:S(2)}) collective-permute-start(f32[288,128]{1,0:T(8,128)S(1)} %pad_maximum_fusion.1), channel_id=1, source_target_pairs={{0,4},{4,0},{8,12},{12,8},{16,20},{20,16},{24,28},{28,24},{1,5},{5... | collective-permute-start | bytes 442376 | tf_op jit(solution)/shard_map/ppermute | solution.py:106
  47.8 3.1 %collective-permute-done.12 = f32[288,128]{1,0:T(8,128)S(1)} collective-permute-done((f32[288,128]{1,0:T(8,128)S(1)}, f32[288,128]{1,0:T(8,128)S(1)}, u32[]{:S(2)}, u32[]{:S(2)}) %collective-permute-start.12) | collective-permute-done | bytes 147488 | tf_op jit(solution)/shard_map/ppermute | solution.py:106
  50.9 2.0 %collective-permute-start.13 = (f32[576,128]{1,0:T(8,128)S(1)}, f32[576,128]{1,0:T(8,128)S(1)}, u32[]{:S(2)}, u32[]{:S(2)}) collective-permute-start(f32[576,128]{1,0:T(8,128)S(1)} %get-tuple-element.39), channel_id=1, source_target_pairs={{0,4},{4,0},{8,12},{12,8},{16,20},{20,16},{24,28},{28,24},{1,5},{5... | collective-permute-start | bytes 884744 | tf_op jit(solution)/shard_map/ppermute | solution.py:106
  52.9 0.6 collective-permute-done.15
  53.5 0.8 collective-permute-start.16
  54.3 3.3 %collective-permute-done.13 = f32[576,128]{1,0:T(8,128)S(1)} collective-permute-done((f32[576,128]{1,0:T(8,128)S(1)}, f32[576,128]{1,0:T(8,128)S(1)}, u32[]{:S(2)}, u32[]{:S(2)}) %collective-permute-start.13) | collective-permute-done | bytes 294944 | tf_op jit(solution)/shard_map/ppermute | solution.py:106
  57.7 0.1 collective-permute-start.14
  57.7 2.5 %collective-permute-done.16 = f32[576,128]{1,0:T(8,128)S(1)} collective-permute-done((f32[576,128]{1,0:T(8,128)S(1)}, f32[576,128]{1,0:T(8,128)S(1)}, u32[]{:S(2)}, u32[]{:S(2)}) %collective-permute-start.16) | collective-permute-done | bytes 294944 | tf_op jit(solution)/shard_map/ppermute | solution.py:106
  60.3 0.1 collective-permute-start.17
  60.4 0.0 collective-permute-done.14.a1_ref
  60.4 2.0 %collective-permute-done.17.b1_ref = f32[1152,128]{1,0:T(8,128)S(1)} collective-permute-done((f32[1152,128]{1,0:T(8,128)S(1)}, f32[1152,128]{1,0:T(8,128)S(1)}, u32[]{:S(2)}, u32[]{:S(2)}) %collective-permute-start.17) | collective-permute-done | bytes 589856 | tf_op jit(solution)/shard_map/ppermute | solution.py:106
  62.4 0.0 copy-done
  62.4 0.0 copy-done.1
  62.4 45.3 %solve.1 = (bf16[2048,256]{1,0:T(8,128)(2,1)}, f32[1,2048]{1,0:T(1,128)}, f32[32,256]{1,0:T(8,128)}) custom-call(s32[3]{0:T(128)S(1)} %pad_add_fusion.keys_ref, f32[1024,256]{1,0:T(8,128)S(1)} %copy-done.1, bf16[2048,1024]{1,0:T(8,128)(2,1)S(1)} %copy-done, f32[1152,128]{1,0:T(8,128)S(1)} %constant_dynamic-update-slice_fusion.5.a0_ref, ...), custom_call_target="tpu_custom_call" | custom-call | tf_op jit(solution)/shard_map/solve/pallas_call | solution.py:508
  (19 shorter events, 0.3 us)
Async XLA Ops:
  7.0 2.2 %collective-permute-start = (f32[1152,128]{1,0:T(8,128)S(1)}, f32[1152,128]{1,0:T(8,128)S(1)}, u32[]{:S(2)}, u32[]{:S(2)}) collective-permute-start(f32[1152,128]{1,0:T(8,128)S(1)} %get-tuple-element.11), channel_id=1, source_target_pairs={{0,1},{1,0},{2,3},{3,2},{4,5},{5,4},{6,7},{7,6},{8,9},{9,8},{10,11... | collective-permute-start | bytes 1769480 | tf_op jit(solution)/shard_map/ppermute | solution.py:106
  7.6 4.6 %collective-permute-start.3 = (f32[1152,128]{1,0:T(8,128)S(1)}, f32[1152,128]{1,0:T(8,128)S(1)}, u32[]{:S(2)}, u32[]{:S(2)}) collective-permute-start(f32[1152,128]{1,0:T(8,128)S(1)} %get-tuple-element.13), channel_id=1, source_target_pairs={{0,1},{1,0},{2,3},{3,2},{4,5},{5,4},{6,7},{7,6},{8,9},{9,8},{10,11... | collective-permute-start | bytes 1769480 | tf_op jit(solution)/shard_map/ppermute | solution.py:106
  9.3 10.2 %collective-permute-start.1 = (f32[576,128]{1,0:T(8,128)S(1)}, f32[576,128]{1,0:T(8,128)S(1)}, u32[]{:S(2)}, u32[]{:S(2)}) collective-permute-start(f32[576,128]{1,0:T(8,128)S(1)} %get-tuple-element.22), channel_id=1, source_target_pairs={{0,4},{4,0},{8,12},{12,8},{16,20},{20,16},{24,28},{28,24},{1,5},{5... | collective-permute-start | bytes 884744 | tf_op jit(solution)/shard_map/ppermute | solution.py:106
  12.2 50.2 %copy-start = (bf16[2048,1024]{1,0:T(8,128)(2,1)S(1)}, bf16[2048,1024]{1,0:T(8,128)(2,1)}, u32[]{:S(2)}) copy-start(bf16[2048,1024]{1,0:T(8,128)(2,1)} %s_ref.1) | copy-start | bytes 12582916
  12.2 50.2 %copy-start.1 = (f32[1024,256]{1,0:T(8,128)S(1)}, f32[1024,256]{1,0:T(8,128)}, u32[]{:S(2)}) copy-start(f32[1024,256]{1,0:T(8,128)} %start_ref.1) | copy-start | bytes 3145732
  12.3 9.1 %collective-permute-start.4 = (f32[576,128]{1,0:T(8,128)S(1)}, f32[576,128]{1,0:T(8,128)S(1)}, u32[]{:S(2)}, u32[]{:S(2)}) collective-permute-start(f32[576,128]{1,0:T(8,128)S(1)} %get-tuple-element.24), channel_id=1, source_target_pairs={{0,2},{1,3},{2,0},{3,1},{4,6},{5,7},{6,4},{7,5},{8,10},{9,11},{10,... | collective-permute-start | bytes 884744 | tf_op jit(solution)/shard_map/ppermute | solution.py:106
  19.5 5.4 %collective-permute-start.2 = (f32[288,128]{1,0:T(8,128)S(1)}, f32[288,128]{1,0:T(8,128)S(1)}, u32[]{:S(2)}, u32[]{:S(2)}) collective-permute-start(f32[288,128]{1,0:T(8,128)S(1)} %get-tuple-element.26), channel_id=1, source_target_pairs={{0,2},{1,3},{2,0},{3,1},{4,6},{5,7},{6,4},{7,5},{8,10},{9,11},{10,... | collective-permute-start | bytes 442376 | tf_op jit(solution)/shard_map/ppermute | solution.py:106
  21.4 5.2 %collective-permute-start.5 = (f32[288,128]{1,0:T(8,128)S(1)}, f32[288,128]{1,0:T(8,128)S(1)}, u32[]{:S(2)}, u32[]{:S(2)}) collective-permute-start(f32[288,128]{1,0:T(8,128)S(1)} %get-tuple-element.28), channel_id=1, source_target_pairs={{0,4},{4,0},{8,12},{12,8},{16,20},{20,16},{24,28},{28,24},{1,5},{5... | collective-permute-start | bytes 442376 | tf_op jit(solution)/shard_map/ppermute | solution.py:106
  26.7 5.2 %collective-permute-start.7 = (f32[144,128]{1,0:T(8,128)S(1)}, f32[144,128]{1,0:T(8,128)S(1)}, u32[]{:S(2)}, u32[]{:S(2)}) collective-permute-start(f32[144,128]{1,0:T(8,128)S(1)} %pad_maximum_fusion.3), channel_id=1, source_target_pairs={{0,8},{4,12},{8,0},{12,4},{16,24},{20,28},{24,16},{28,20},{1,9},{5... | collective-permute-start | bytes 221192 | tf_op jit(solution)/shard_map/ppermute | solution.py:106
  28.3 6.2 %collective-permute-start.8 = (f32[144,128]{1,0:T(8,128)S(1)}, f32[144,128]{1,0:T(8,128)S(1)}, u32[]{:S(2)}, u32[]{:S(2)}) collective-permute-start(f32[144,128]{1,0:T(8,128)S(1)} %pad_maximum_fusion.4), channel_id=1, source_target_pairs={{0,24},{4,28},{8,16},{12,20},{16,8},{20,12},{24,0},{28,4},{1,25},{... | collective-permute-start | bytes 221192 | tf_op jit(solution)/shard_map/ppermute | solution.py:106
  30.8 6.6 %collective-permute-start.6 = (f32[144,128]{1,0:T(8,128)S(1)}, f32[144,128]{1,0:T(8,128)S(1)}, u32[]{:S(2)}, u32[]{:S(2)}) collective-permute-start(f32[144,128]{1,0:T(8,128)S(1)} %pad_maximum_fusion.2), channel_id=1, source_target_pairs={{0,16},{4,20},{8,24},{12,28},{16,0},{20,4},{24,8},{28,12},{1,17},{... | collective-permute-start | bytes 221192 | tf_op jit(solution)/shard_map/ppermute | solution.py:106
  37.5 7.8 %collective-permute-start.11 = (f32[144,128]{1,0:T(8,128)S(1)}, f32[144,128]{1,0:T(8,128)S(1)}, u32[]{:S(2)}, u32[]{:S(2)}) collective-permute-start(f32[144,128]{1,0:T(8,128)S(1)} %pad_maximum_fusion.5), channel_id=1, source_target_pairs={{0,24},{4,28},{8,16},{12,20},{16,8},{20,12},{24,0},{28,4},{1,25},{... | collective-permute-start | bytes 221192 | tf_op jit(solution)/shard_map/ppermute | solution.py:106
  39.3 5.9 %collective-permute-start.10 = (f32[144,128]{1,0:T(8,128)S(1)}, f32[144,128]{1,0:T(8,128)S(1)}, u32[]{:S(2)}, u32[]{:S(2)}) collective-permute-start(f32[144,128]{1,0:T(8,128)S(1)} %pad_maximum_fusion.5), channel_id=1, source_target_pairs={{0,8},{4,12},{8,0},{12,4},{16,24},{20,28},{24,16},{28,20},{1,9},{5... | collective-permute-start | bytes 221192 | tf_op jit(solution)/shard_map/ppermute | solution.py:106
  39.3 5.3 %collective-permute-start.9 = (f32[144,128]{1,0:T(8,128)S(1)}, f32[144,128]{1,0:T(8,128)S(1)}, u32[]{:S(2)}, u32[]{:S(2)}) collective-permute-start(f32[144,128]{1,0:T(8,128)S(1)} %pad_maximum_fusion.5), channel_id=1, source_target_pairs={{0,16},{4,20},{8,24},{12,28},{16,0},{20,4},{24,8},{28,12},{1,17},{... | collective-permute-start | bytes 221192 | tf_op jit(solution)/shard_map/ppermute | solution.py:106
  45.3 5.5 %collective-permute-start.12 = (f32[288,128]{1,0:T(8,128)S(1)}, f32[288,128]{1,0:T(8,128)S(1)}, u32[]{:S(2)}, u32[]{:S(2)}) collective-permute-start(f32[288,128]{1,0:T(8,128)S(1)} %pad_maximum_fusion), channel_id=1, source_target_pairs={{0,2},{1,3},{2,0},{3,1},{4,6},{5,7},{6,4},{7,5},{8,10},{9,11},{10,... | collective-permute-start | bytes 442376 | tf_op jit(solution)/shard_map/ppermute | solution.py:106
  46.7 6.8 %collective-permute-start.15 = (f32[288,128]{1,0:T(8,128)S(1)}, f32[288,128]{1,0:T(8,128)S(1)}, u32[]{:S(2)}, u32[]{:S(2)}) collective-permute-start(f32[288,128]{1,0:T(8,128)S(1)} %pad_maximum_fusion.1), channel_id=1, source_target_pairs={{0,4},{4,0},{8,12},{12,8},{16,20},{20,16},{24,28},{28,24},{1,5},{5... | collective-permute-start | bytes 442376 | tf_op jit(solution)/shard_map/ppermute | solution.py:106
  50.9 6.8 %collective-permute-start.13 = (f32[576,128]{1,0:T(8,128)S(1)}, f32[576,128]{1,0:T(8,128)S(1)}, u32[]{:S(2)}, u32[]{:S(2)}) collective-permute-start(f32[576,128]{1,0:T(8,128)S(1)} %get-tuple-element.39), channel_id=1, source_target_pairs={{0,4},{4,0},{8,12},{12,8},{16,20},{20,16},{24,28},{28,24},{1,5},{5... | collective-permute-start | bytes 884744 | tf_op jit(solution)/shard_map/ppermute | solution.py:106
  53.5 6.8 %collective-permute-start.16 = (f32[576,128]{1,0:T(8,128)S(1)}, f32[576,128]{1,0:T(8,128)S(1)}, u32[]{:S(2)}, u32[]{:S(2)}) collective-permute-start(f32[576,128]{1,0:T(8,128)S(1)} %get-tuple-element.37), channel_id=1, source_target_pairs={{0,2},{1,3},{2,0},{3,1},{4,6},{5,7},{6,4},{7,5},{8,10},{9,11},{10,... | collective-permute-start | bytes 884744 | tf_op jit(solution)/shard_map/ppermute | solution.py:106
  57.7 2.7 %collective-permute-start.14 = (f32[1152,128]{1,0:T(8,128)S(1)}, f32[1152,128]{1,0:T(8,128)S(1)}, u32[]{:S(2)}, u32[]{:S(2)}) collective-permute-start(f32[1152,128]{1,0:T(8,128)S(1)} %constant_dynamic-update-slice_fusion.5.a0_ref), channel_id=1, source_target_pairs={{0,1},{1,0},{2,3},{3,2},{4,5},{5,4},{6,7},{7,6},{8,9},{9,8},{10,11... | collective-permute-start | bytes 1769480 | tf_op jit(solution)/shard_map/ppermute | solution.py:106
  60.3 2.1 %collective-permute-start.17 = (f32[1152,128]{1,0:T(8,128)S(1)}, f32[1152,128]{1,0:T(8,128)S(1)}, u32[]{:S(2)}, u32[]{:S(2)}) collective-permute-start(f32[1152,128]{1,0:T(8,128)S(1)} %constant_dynamic-update-slice_fusion.16.b0_ref), channel_id=1, source_target_pairs={{0,1},{1,0},{2,3},{3,2},{4,5},{5,4},{6,7},{7,6},{8,9},{9,8},{10,11... | collective-permute-start | bytes 1769480 | tf_op jit(solution)/shard_map/ppermute | solution.py:106

commit v6 on v5

--- a/solution.py
+++ b/solution.py
@@ -200,17 +200,15 @@
     pivots = dev_ref.shape[0]
     sub = iota((16, s_ref.shape[1]), 0)
 
-    def pick(p, carry):
+    for p in range(pivots):
         at = row_ref[p]
         group = pl.multiple_of((at // 16) * 16, 16)
         rows = s_ref[pl.ds(group, 16), :].astype(F32)
         wanted = jnp.where(dev_ref[p] == keys_ref[2], at - group, -1)
         row = jnp.sum(jnp.where(sub == wanted, rows, 0.0), axis=0, keepdims=True)
         for t in range(tiles):
-            work[0][pl.ds(base + t * pivots + p, 1), :] = row[:, t * TILE:(t + 1) * TILE]
-        return carry
-
-    lax.fori_loop(0, pivots, pick, 0, unroll=4)
+            to = base + t * pivots + p
+            work[0][to:to + 1, :] = row[:, t * TILE:(t + 1) * TILE]
     for part in range(2):
         size = work[part].shape[0] // chunks
         for q in range(chunks):

time: 108 us -> 108 us (level)
  no operation moved by 1% of the time
where the time goes in v6:
time: 108 us
  Pallas kernels  51.4 us (48%)
  waiting for transfers between devices  32.1 us (30%)
  starting transfers between devices  22.7 us (21%)
    pallas_call x1, Pallas kernels, solve(): pl.pallas_call(functools.partial(solve_kernel, chunks, rows_total), out_s...  45.5 us
    ppermute x18, waiting for transfers between devices, send(): return lax.ppermute(value, axis, [(i, i ^ mask) for i in range(size)])  32.1 us
    ppermute x18, starting transfers between devices, send(): return lax.ppermute(value, axis, [(i, i ^ mask) for i in range(size)])  22.7 us
    pallas_call x1, Pallas kernels, local_gram(): pl.pallas_call(functools.partial(gram_kernel, chunks), out_shape=shapes,...  5.87 us
  transfers between devices with their start and end apart: 18, of which 14 were waited for; matrix products, arithmetic and copies ran while one was open for 0% of the time, Pallas kernels for 0%

profile of v6, /device:TPU:0, one launch (start us, length us, event | category | flops | bytes accessed | tf_op | source)
XLA Modules:
  0.0 107.6 jit_solution(10131014193397193567)
XLA Ops:
  0.7 0.1 pad_add_fusion.keys_ref
  0.7 5.9 %local_gram.1 = (f32[1152,128]{1,0:T(8,128)S(1)}, f32[1152,128]{1,0:T(8,128)S(1)}, f32[1152,128]{1,0:T(8,128)S(1)}, f32[1152,128]{1,0:T(8,128)S(1)}) custom-call(s32[32]{0:T(128)} %dev_ref.1, s32[32]{0:T(128)} %row_ref.1, s32[3]{0:T(128)S(1)} %pad_add_fusion.keys_ref, bf16[2048,1024]{1,0:T(8,128)(2,1)} %s_ref.1), custom_call_target="tpu_custom_call" | custom-call | tf_op jit(solution)/shard_map/local_gram/pallas_call | solution.py:223
  6.6 0.6 collective-permute-start
  7.2 0.1 collective-permute-start.3
  7.3 1.6 %collective-permute-done = f32[1152,128]{1,0:T(8,128)S(1)} collective-permute-done((f32[1152,128]{1,0:T(8,128)S(1)}, f32[1152,128]{1,0:T(8,128)S(1)}, u32[]{:S(2)}, u32[]{:S(2)}) %collective-permute-start) | collective-permute-done | bytes 589856 | tf_op jit(solution)/shard_map/ppermute | solution.py:106
  8.8 0.1 slice_add_fusion.3
  8.9 2.9 %collective-permute-start.1 = (f32[576,128]{1,0:T(8,128)S(1)}, f32[576,128]{1,0:T(8,128)S(1)}, u32[]{:S(2)}, u32[]{:S(2)}) collective-permute-start(f32[576,128]{1,0:T(8,128)S(1)} %get-tuple-element.22), channel_id=1, source_target_pairs={{0,4},{4,0},{8,12},{12,8},{16,20},{20,16},{24,28},{28,24},{1,5},{5... | collective-permute-start | bytes 884744 | tf_op jit(solution)/shard_map/ppermute | solution.py:106
  11.8 0.0 collective-permute-done.3
  11.8 0.0 copy-start
  11.8 0.0 copy-start.1
  11.8 0.1 slice_add_fusion.1
  11.9 1.6 %collective-permute-start.4 = (f32[576,128]{1,0:T(8,128)S(1)}, f32[576,128]{1,0:T(8,128)S(1)}, u32[]{:S(2)}, u32[]{:S(2)}) collective-permute-start(f32[576,128]{1,0:T(8,128)S(1)} %get-tuple-element.24), channel_id=1, source_target_pairs={{0,2},{1,3},{2,0},{3,1},{4,6},{5,7},{6,4},{7,5},{8,10},{9,11},{10,... | collective-permute-start | bytes 884744 | tf_op jit(solution)/shard_map/ppermute | solution.py:106
  13.4 5.6 %collective-permute-done.1 = f32[576,128]{1,0:T(8,128)S(1)} collective-permute-done((f32[576,128]{1,0:T(8,128)S(1)}, f32[576,128]{1,0:T(8,128)S(1)}, u32[]{:S(2)}, u32[]{:S(2)}) %collective-permute-start.1) | collective-permute-done | bytes 294944 | tf_op jit(solution)/shard_map/ppermute | solution.py:106
  19.1 1.8 %collective-permute-start.2 = (f32[288,128]{1,0:T(8,128)S(1)}, f32[288,128]{1,0:T(8,128)S(1)}, u32[]{:S(2)}, u32[]{:S(2)}) collective-permute-start(f32[288,128]{1,0:T(8,128)S(1)} %get-tuple-element.26), channel_id=1, source_target_pairs={{0,2},{1,3},{2,0},{3,1},{4,6},{5,7},{6,4},{7,5},{8,10},{9,11},{10,... | collective-permute-start | bytes 442376 | tf_op jit(solution)/shard_map/ppermute | solution.py:106
  21.0 0.0 collective-permute-done.4
  21.0 1.6 %collective-permute-start.5 = (f32[288,128]{1,0:T(8,128)S(1)}, f32[288,128]{1,0:T(8,128)S(1)}, u32[]{:S(2)}, u32[]{:S(2)}) collective-permute-start(f32[288,128]{1,0:T(8,128)S(1)} %get-tuple-element.28), channel_id=1, source_target_pairs={{0,4},{4,0},{8,12},{12,8},{16,20},{20,16},{24,28},{28,24},{1,5},{5... | collective-permute-start | bytes 442376 | tf_op jit(solution)/shard_map/ppermute | solution.py:106
  22.6 2.0 %collective-permute-done.2 = f32[288,128]{1,0:T(8,128)S(1)} collective-permute-done((f32[288,128]{1,0:T(8,128)S(1)}, f32[288,128]{1,0:T(8,128)S(1)}, u32[]{:S(2)}, u32[]{:S(2)}) %collective-permute-start.2) | collective-permute-done | bytes 147488 | tf_op jit(solution)/shard_map/ppermute | solution.py:106
  24.5 1.7 %collective-permute-done.5 = f32[288,128]{1,0:T(8,128)S(1)} collective-permute-done((f32[288,128]{1,0:T(8,128)S(1)}, f32[288,128]{1,0:T(8,128)S(1)}, u32[]{:S(2)}, u32[]{:S(2)}) %collective-permute-start.5) | collective-permute-done | bytes 147488 | tf_op jit(solution)/shard_map/ppermute | solution.py:106
  26.2 1.6 %collective-permute-start.7 = (f32[144,128]{1,0:T(8,128)S(1)}, f32[144,128]{1,0:T(8,128)S(1)}, u32[]{:S(2)}, u32[]{:S(2)}) collective-permute-start(f32[144,128]{1,0:T(8,128)S(1)} %pad_maximum_fusion.3), channel_id=1, source_target_pairs={{0,8},{4,12},{8,0},{12,4},{16,24},{20,28},{24,16},{28,20},{1,9},{5... | collective-permute-start | bytes 221192 | tf_op jit(solution)/shard_map/ppermute | solution.py:106
  27.9 2.5 %collective-permute-start.8 = (f32[144,128]{1,0:T(8,128)S(1)}, f32[144,128]{1,0:T(8,128)S(1)}, u32[]{:S(2)}, u32[]{:S(2)}) collective-permute-start(f32[144,128]{1,0:T(8,128)S(1)} %pad_maximum_fusion.4), channel_id=1, source_target_pairs={{0,24},{4,28},{8,16},{12,20},{16,8},{20,12},{24,0},{28,4},{1,25},{... | collective-permute-start | bytes 221192 | tf_op jit(solution)/shard_map/ppermute | solution.py:106
  30.4 0.2 collective-permute-start.6
  30.6 0.9 collective-permute-done.7
  31.5 2.6 %collective-permute-done.8 = f32[144,128]{1,0:T(8,128)S(1)} collective-permute-done((f32[144,128]{1,0:T(8,128)S(1)}, f32[144,128]{1,0:T(8,128)S(1)}, u32[]{:S(2)}, u32[]{:S(2)}) %collective-permute-start.8) | collective-permute-done | bytes 73760 | tf_op jit(solution)/shard_map/ppermute | solution.py:106
  34.1 2.9 %collective-permute-done.6 = f32[144,128]{1,0:T(8,128)S(1)} collective-permute-done((f32[144,128]{1,0:T(8,128)S(1)}, f32[144,128]{1,0:T(8,128)S(1)}, u32[]{:S(2)}, u32[]{:S(2)}) %collective-permute-start.6) | collective-permute-done | bytes 73760 | tf_op jit(solution)/shard_map/ppermute | solution.py:106
  37.0 1.9 %collective-permute-start.11 = (f32[144,128]{1,0:T(8,128)S(1)}, f32[144,128]{1,0:T(8,128)S(1)}, u32[]{:S(2)}, u32[]{:S(2)}) collective-permute-start(f32[144,128]{1,0:T(8,128)S(1)} %pad_maximum_fusion.5), channel_id=1, source_target_pairs={{0,24},{4,28},{8,16},{12,20},{16,8},{20,12},{24,0},{28,4},{1,25},{... | collective-permute-start | bytes 221192 | tf_op jit(solution)/shard_map/ppermute | solution.py:106
  38.9 0.0 collective-permute-start.10
  38.9 2.6 %collective-permute-start.9 = (f32[144,128]{1,0:T(8,128)S(1)}, f32[144,128]{1,0:T(8,128)S(1)}, u32[]{:S(2)}, u32[]{:S(2)}) collective-permute-start(f32[144,128]{1,0:T(8,128)S(1)} %pad_maximum_fusion.5), channel_id=1, source_target_pairs={{0,16},{4,20},{8,24},{12,28},{16,0},{20,4},{24,8},{28,12},{1,17},{... | collective-permute-start | bytes 221192 | tf_op jit(solution)/shard_map/ppermute | solution.py:106
  41.5 2.7 %collective-permute-done.9 = f32[144,128]{1,0:T(8,128)S(1)} collective-permute-done((f32[144,128]{1,0:T(8,128)S(1)}, f32[144,128]{1,0:T(8,128)S(1)}, u32[]{:S(2)}, u32[]{:S(2)}) %collective-permute-start.9) | collective-permute-done | bytes 73760 | tf_op jit(solution)/shard_map/ppermute | solution.py:106
  44.2 0.6 collective-permute-done.10
  44.9 0.0 collective-permute-done.11
  44.9 1.3 %collective-permute-start.12 = (f32[288,128]{1,0:T(8,128)S(1)}, f32[288,128]{1,0:T(8,128)S(1)}, u32[]{:S(2)}, u32[]{:S(2)}) collective-permute-start(f32[288,128]{1,0:T(8,128)S(1)} %pad_maximum_fusion), channel_id=1, source_target_pairs={{0,2},{1,3},{2,0},{3,1},{4,6},{5,7},{6,4},{7,5},{8,10},{9,11},{10,... | collective-permute-start | bytes 442376 | tf_op jit(solution)/shard_map/ppermute | solution.py:106
  46.2 1.1 %collective-permute-start.15 = (f32[288,128]{1,0:T(8,128)S(1)}, f32[288,128]{1,0:T(8,128)S(1)}, u32[]{:S(2)}, u32[]{:S(2)}) collective-permute-start(f32[288,128]{1,0:T(8,128)S(1)} %pad_maximum_fusion.1), channel_id=1, source_target_pairs={{0,4},{4,0},{8,12},{12,8},{16,20},{20,16},{24,28},{28,24},{1,5},{5... | collective-permute-start | bytes 442376 | tf_op jit(solution)/shard_map/ppermute | solution.py:106
  47.4 3.1 %collective-permute-done.12 = f32[288,128]{1,0:T(8,128)S(1)} collective-permute-done((f32[288,128]{1,0:T(8,128)S(1)}, f32[288,128]{1,0:T(8,128)S(1)}, u32[]{:S(2)}, u32[]{:S(2)}) %collective-permute-start.12) | collective-permute-done | bytes 147488 | tf_op jit(solution)/shard_map/ppermute | solution.py:106
  50.5 2.0 %collective-permute-start.13 = (f32[576,128]{1,0:T(8,128)S(1)}, f32[576,128]{1,0:T(8,128)S(1)}, u32[]{:S(2)}, u32[]{:S(2)}) collective-permute-start(f32[576,128]{1,0:T(8,128)S(1)} %get-tuple-element.39), channel_id=1, source_target_pairs={{0,4},{4,0},{8,12},{12,8},{16,20},{20,16},{24,28},{28,24},{1,5},{5... | collective-permute-start | bytes 884744 | tf_op jit(solution)/shard_map/ppermute | solution.py:106
  52.5 0.6 collective-permute-done.15
  53.1 0.8 collective-permute-start.16
  53.9 3.3 %collective-permute-done.13 = f32[576,128]{1,0:T(8,128)S(1)} collective-permute-done((f32[576,128]{1,0:T(8,128)S(1)}, f32[576,128]{1,0:T(8,128)S(1)}, u32[]{:S(2)}, u32[]{:S(2)}) %collective-permute-start.13) | collective-permute-done | bytes 294944 | tf_op jit(solution)/shard_map/ppermute | solution.py:106
  57.3 0.1 collective-permute-start.14
  57.3 2.5 %collective-permute-done.16 = f32[576,128]{1,0:T(8,128)S(1)} collective-permute-done((f32[576,128]{1,0:T(8,128)S(1)}, f32[576,128]{1,0:T(8,128)S(1)}, u32[]{:S(2)}, u32[]{:S(2)}) %collective-permute-start.16) | collective-permute-done | bytes 294944 | tf_op jit(solution)/shard_map/ppermute | solution.py:106
  59.9 0.1 collective-permute-start.17
  60.0 0.0 collective-permute-done.14.a1_ref
  60.0 2.0 %collective-permute-done.17.b1_ref = f32[1152,128]{1,0:T(8,128)S(1)} collective-permute-done((f32[1152,128]{1,0:T(8,128)S(1)}, f32[1152,128]{1,0:T(8,128)S(1)}, u32[]{:S(2)}, u32[]{:S(2)}) %collective-permute-start.17) | collective-permute-done | bytes 589856 | tf_op jit(solution)/shard_map/ppermute | solution.py:106
  61.9 0.0 copy-done
  61.9 0.0 copy-done.1
  62.0 45.5 %solve.1 = (bf16[2048,256]{1,0:T(8,128)(2,1)}, f32[1,2048]{1,0:T(1,128)}, f32[32,256]{1,0:T(8,128)}) custom-call(s32[3]{0:T(128)S(1)} %pad_add_fusion.keys_ref, f32[1024,256]{1,0:T(8,128)S(1)} %copy-done.1, bf16[2048,1024]{1,0:T(8,128)(2,1)S(1)} %copy-done, f32[1152,128]{1,0:T(8,128)S(1)} %constant_dynamic-update-slice_fusion.5.a0_ref, ...), custom_call_target="tpu_custom_call" | custom-call | tf_op jit(solution)/shard_map/solve/pallas_call | solution.py:506
  (19 shorter events, 0.3 us)
Async XLA Ops:
  6.6 2.2 %collective-permute-start = (f32[1152,128]{1,0:T(8,128)S(1)}, f32[1152,128]{1,0:T(8,128)S(1)}, u32[]{:S(2)}, u32[]{:S(2)}) collective-permute-start(f32[1152,128]{1,0:T(8,128)S(1)} %get-tuple-element.11), channel_id=1, source_target_pairs={{0,1},{1,0},{2,3},{3,2},{4,5},{5,4},{6,7},{7,6},{8,9},{9,8},{10,11... | collective-permute-start | bytes 1769480 | tf_op jit(solution)/shard_map/ppermute | solution.py:106
  7.2 4.6 %collective-permute-start.3 = (f32[1152,128]{1,0:T(8,128)S(1)}, f32[1152,128]{1,0:T(8,128)S(1)}, u32[]{:S(2)}, u32[]{:S(2)}) collective-permute-start(f32[1152,128]{1,0:T(8,128)S(1)} %get-tuple-element.13), channel_id=1, source_target_pairs={{0,1},{1,0},{2,3},{3,2},{4,5},{5,4},{6,7},{7,6},{8,9},{9,8},{10,11... | collective-permute-start | bytes 1769480 | tf_op jit(solution)/shard_map/ppermute | solution.py:106
  8.9 10.2 %collective-permute-start.1 = (f32[576,128]{1,0:T(8,128)S(1)}, f32[576,128]{1,0:T(8,128)S(1)}, u32[]{:S(2)}, u32[]{:S(2)}) collective-permute-start(f32[576,128]{1,0:T(8,128)S(1)} %get-tuple-element.22), channel_id=1, source_target_pairs={{0,4},{4,0},{8,12},{12,8},{16,20},{20,16},{24,28},{28,24},{1,5},{5... | collective-permute-start | bytes 884744 | tf_op jit(solution)/shard_map/ppermute | solution.py:106
  11.8 50.2 %copy-start = (bf16[2048,1024]{1,0:T(8,128)(2,1)S(1)}, bf16[2048,1024]{1,0:T(8,128)(2,1)}, u32[]{:S(2)}) copy-start(bf16[2048,1024]{1,0:T(8,128)(2,1)} %s_ref.1) | copy-start | bytes 12582916
  11.8 50.2 %copy-start.1 = (f32[1024,256]{1,0:T(8,128)S(1)}, f32[1024,256]{1,0:T(8,128)}, u32[]{:S(2)}) copy-start(f32[1024,256]{1,0:T(8,128)} %start_ref.1) | copy-start | bytes 3145732
  11.9 9.1 %collective-permute-start.4 = (f32[576,128]{1,0:T(8,128)S(1)}, f32[576,128]{1,0:T(8,128)S(1)}, u32[]{:S(2)}, u32[]{:S(2)}) collective-permute-start(f32[576,128]{1,0:T(8,128)S(1)} %get-tuple-element.24), channel_id=1, source_target_pairs={{0,2},{1,3},{2,0},{3,1},{4,6},{5,7},{6,4},{7,5},{8,10},{9,11},{10,... | collective-permute-start | bytes 884744 | tf_op jit(solution)/shard_map/ppermute | solution.py:106
  19.1 5.4 %collective-permute-start.2 = (f32[288,128]{1,0:T(8,128)S(1)}, f32[288,128]{1,0:T(8,128)S(1)}, u32[]{:S(2)}, u32[]{:S(2)}) collective-permute-start(f32[288,128]{1,0:T(8,128)S(1)} %get-tuple-element.26), channel_id=1, source_target_pairs={{0,2},{1,3},{2,0},{3,1},{4,6},{5,7},{6,4},{7,5},{8,10},{9,11},{10,... | collective-permute-start | bytes 442376 | tf_op jit(solution)/shard_map/ppermute | solution.py:106
  21.0 5.2 %collective-permute-start.5 = (f32[288,128]{1,0:T(8,128)S(1)}, f32[288,128]{1,0:T(8,128)S(1)}, u32[]{:S(2)}, u32[]{:S(2)}) collective-permute-start(f32[288,128]{1,0:T(8,128)S(1)} %get-tuple-element.28), channel_id=1, source_target_pairs={{0,4},{4,0},{8,12},{12,8},{16,20},{20,16},{24,28},{28,24},{1,5},{5... | collective-permute-start | bytes 442376 | tf_op jit(solution)/shard_map/ppermute | solution.py:106
  26.2 5.2 %collective-permute-start.7 = (f32[144,128]{1,0:T(8,128)S(1)}, f32[144,128]{1,0:T(8,128)S(1)}, u32[]{:S(2)}, u32[]{:S(2)}) collective-permute-start(f32[144,128]{1,0:T(8,128)S(1)} %pad_maximum_fusion.3), channel_id=1, source_target_pairs={{0,8},{4,12},{8,0},{12,4},{16,24},{20,28},{24,16},{28,20},{1,9},{5... | collective-permute-start | bytes 221192 | tf_op jit(solution)/shard_map/ppermute | solution.py:106
  27.9 6.2 %collective-permute-start.8 = (f32[144,128]{1,0:T(8,128)S(1)}, f32[144,128]{1,0:T(8,128)S(1)}, u32[]{:S(2)}, u32[]{:S(2)}) collective-permute-start(f32[144,128]{1,0:T(8,128)S(1)} %pad_maximum_fusion.4), channel_id=1, source_target_pairs={{0,24},{4,28},{8,16},{12,20},{16,8},{20,12},{24,0},{28,4},{1,25},{... | collective-permute-start | bytes 221192 | tf_op jit(solution)/shard_map/ppermute | solution.py:106
  30.4 6.6 %collective-permute-start.6 = (f32[144,128]{1,0:T(8,128)S(1)}, f32[144,128]{1,0:T(8,128)S(1)}, u32[]{:S(2)}, u32[]{:S(2)}) collective-permute-start(f32[144,128]{1,0:T(8,128)S(1)} %pad_maximum_fusion.2), channel_id=1, source_target_pairs={{0,16},{4,20},{8,24},{12,28},{16,0},{20,4},{24,8},{28,12},{1,17},{... | collective-permute-start | bytes 221192 | tf_op jit(solution)/shard_map/ppermute | solution.py:106
  37.0 7.8 %collective-permute-start.11 = (f32[144,128]{1,0:T(8,128)S(1)}, f32[144,128]{1,0:T(8,128)S(1)}, u32[]{:S(2)}, u32[]{:S(2)}) collective-permute-start(f32[144,128]{1,0:T(8,128)S(1)} %pad_maximum_fusion.5), channel_id=1, source_target_pairs={{0,24},{4,28},{8,16},{12,20},{16,8},{20,12},{24,0},{28,4},{1,25},{... | collective-permute-start | bytes 221192 | tf_op jit(solution)/shard_map/ppermute | solution.py:106
  38.9 5.9 %collective-permute-start.10 = (f32[144,128]{1,0:T(8,128)S(1)}, f32[144,128]{1,0:T(8,128)S(1)}, u32[]{:S(2)}, u32[]{:S(2)}) collective-permute-start(f32[144,128]{1,0:T(8,128)S(1)} %pad_maximum_fusion.5), channel_id=1, source_target_pairs={{0,8},{4,12},{8,0},{12,4},{16,24},{20,28},{24,16},{28,20},{1,9},{5... | collective-permute-start | bytes 221192 | tf_op jit(solution)/shard_map/ppermute | solution.py:106
  38.9 5.3 %collective-permute-start.9 = (f32[144,128]{1,0:T(8,128)S(1)}, f32[144,128]{1,0:T(8,128)S(1)}, u32[]{:S(2)}, u32[]{:S(2)}) collective-permute-start(f32[144,128]{1,0:T(8,128)S(1)} %pad_maximum_fusion.5), channel_id=1, source_target_pairs={{0,16},{4,20},{8,24},{12,28},{16,0},{20,4},{24,8},{28,12},{1,17},{... | collective-permute-start | bytes 221192 | tf_op jit(solution)/shard_map/ppermute | solution.py:106
  44.9 5.5 %collective-permute-start.12 = (f32[288,128]{1,0:T(8,128)S(1)}, f32[288,128]{1,0:T(8,128)S(1)}, u32[]{:S(2)}, u32[]{:S(2)}) collective-permute-start(f32[288,128]{1,0:T(8,128)S(1)} %pad_maximum_fusion), channel_id=1, source_target_pairs={{0,2},{1,3},{2,0},{3,1},{4,6},{5,7},{6,4},{7,5},{8,10},{9,11},{10,... | collective-permute-start | bytes 442376 | tf_op jit(solution)/shard_map/ppermute | solution.py:106
  46.2 6.8 %collective-permute-start.15 = (f32[288,128]{1,0:T(8,128)S(1)}, f32[288,128]{1,0:T(8,128)S(1)}, u32[]{:S(2)}, u32[]{:S(2)}) collective-permute-start(f32[288,128]{1,0:T(8,128)S(1)} %pad_maximum_fusion.1), channel_id=1, source_target_pairs={{0,4},{4,0},{8,12},{12,8},{16,20},{20,16},{24,28},{28,24},{1,5},{5... | collective-permute-start | bytes 442376 | tf_op jit(solution)/shard_map/ppermute | solution.py:106
  50.5 6.8 %collective-permute-start.13 = (f32[576,128]{1,0:T(8,128)S(1)}, f32[576,128]{1,0:T(8,128)S(1)}, u32[]{:S(2)}, u32[]{:S(2)}) collective-permute-start(f32[576,128]{1,0:T(8,128)S(1)} %get-tuple-element.39), channel_id=1, source_target_pairs={{0,4},{4,0},{8,12},{12,8},{16,20},{20,16},{24,28},{28,24},{1,5},{5... | collective-permute-start | bytes 884744 | tf_op jit(solution)/shard_map/ppermute | solution.py:106
  53.1 6.8 %collective-permute-start.16 = (f32[576,128]{1,0:T(8,128)S(1)}, f32[576,128]{1,0:T(8,128)S(1)}, u32[]{:S(2)}, u32[]{:S(2)}) collective-permute-start(f32[576,128]{1,0:T(8,128)S(1)} %get-tuple-element.37), channel_id=1, source_target_pairs={{0,2},{1,3},{2,0},{3,1},{4,6},{5,7},{6,4},{7,5},{8,10},{9,11},{10,... | collective-permute-start | bytes 884744 | tf_op jit(solution)/shard_map/ppermute | solution.py:106
  57.3 2.7 %collective-permute-start.14 = (f32[1152,128]{1,0:T(8,128)S(1)}, f32[1152,128]{1,0:T(8,128)S(1)}, u32[]{:S(2)}, u32[]{:S(2)}) collective-permute-start(f32[1152,128]{1,0:T(8,128)S(1)} %constant_dynamic-update-slice_fusion.5.a0_ref), channel_id=1, source_target_pairs={{0,1},{1,0},{2,3},{3,2},{4,5},{5,4},{6,7},{7,6},{8,9},{9,8},{10,11... | collective-permute-start | bytes 1769480 | tf_op jit(solution)/shard_map/ppermute | solution.py:106
  59.9 2.1 %collective-permute-start.17 = (f32[1152,128]{1,0:T(8,128)S(1)}, f32[1152,128]{1,0:T(8,128)S(1)}, u32[]{:S(2)}, u32[]{:S(2)}) collective-permute-start(f32[1152,128]{1,0:T(8,128)S(1)} %constant_dynamic-update-slice_fusion.16.b0_ref), channel_id=1, source_target_pairs={{0,1},{1,0},{2,3},{3,2},{4,5},{5,4},{6,7},{7,6},{8,9},{9,8},{10,11... | collective-permute-start | bytes 1769480 | tf_op jit(solution)/shard_map/ppermute | solution.py:106
